TPU v7x, 512 devices: a whole 4x8x8 slice. The times are simulated.
512 devices in a mesh: cells: 128 (over z, x_lo, y), harm: 4 (over x_hi, core).
Axes of the slice: x: 4 (x_hi: 2, x_lo: 2; x = x_hi * 2 + x_lo), y: 8, z: 8, core: 2. Of those that a mesh axis runs over, the one named last changes fastest.
Arguments:
- mean_adjoint: float32 [5, 262144], P(None, 'cells'), may hold values from -6 to 6
- harm_adjoint: float32 [4, 2, 5, 262144], P('harm', None, None, 'cells'), may hold values from -6 to 6
- harm_flow: float32 [4, 2, 5, 262144], P('harm', None, None, 'cells'), may hold values from -4 to 4
- flux_jacobian: float32 [5, 5, 262144], P(None, None, 'cells'), may hold values from -2.5 to 2.5
- face_weight: float32 [6, 262144], P(None, 'cells'), may hold values from 0.1 to 1
- face_links: int32 [6, 262144], P(None, 'cells'), may hold values from 0 to 4095, as said below
- face_tiles: int32 [2, 131072], P(None, 'cells'), may hold values from 0 to 2047, as said below
- pseudo_step: float32 [262144], P('cells'), may hold values from 0.1 to 0.4
- mean_source: float32 [5, 262144], P(None, 'cells'), may hold values from -6 to 6
- harm_order: int32 [4], P('harm'), may hold values from 0 to 3, each once
Outputs:
- mean_new: float32 [5, 262144], P(None, 'cells')
- harm_new: float32 [4, 2, 5, 262144], P('harm', None, None, 'cells')
Inputs may be any that keep to these rules, and one draw needn't show every extreme that they name: `face_links`: an entry below 2048 names a cell of the same block; 2048 + r names entry r of the lower neighbour block's upper tile; 3072 + r names entry r of the upper neighbour block's lower tile. `face_tiles`: indices within the own block; columns b * 1024 to (b + 1) * 1024 - 1 belong to block b. `harm_order`: each index of harm holds a different harmonic.
All inputs are finite; a program needn't handle non-finite values.
Results may differ from a plain program's by a relative error of at most 0.0001.
Values sent between devices are 32-bit elements; how exact they have to be, the bound alone decides.
No kernel may reach another device: no remote copies, remote signals or barrier semaphores. Data moves between devices by JAX's collectives and lax.ppermute only.
A program may use at most 64 MiB of HBM per device.

v0:
```python
import jax
import jax.numpy as jnp
from jax import lax
from jax.sharding import Mesh
from jax.sharding import PartitionSpec as P

VARS = 5
FACES = 6
SECTIONS = 2
HARM = ("harm_0", "harm_1")


BASE_FREQ = 0.8


def extended_2(block, sides, width):
    for axis, dim in sides:
        count = lax.axis_size(axis)
        forward = [(i, i + 1) for i in range(count - 1)]
        forward.append((count - 1, 0))
        backward = [(target, source) for source, target in forward]
        low = lax.ppermute(
            lax.slice_in_dim(block, block.shape[dim] - width, None, axis=dim), axis, forward
        )
        high = lax.ppermute(lax.slice_in_dim(block, 0, width, axis=dim), axis, backward)
        block = jnp.concatenate([low, block, high], axis=dim)
    return block


def cut_along(array, dim, count):
    lengths = array.shape
    blocks = array.reshape(*lengths[:dim], count, lengths[dim] // count, *lengths[dim + 1 :])
    return jnp.moveaxis(blocks, dim, 0)


def scatter_pairs(array, chips, core, dim):
    sizes = (lax.axis_size(chips), lax.axis_size(core))
    blocks = cut_along(array, dim, sizes[0] * sizes[1])
    inside = blocks.shape[1:]
    blocks = blocks.reshape(*sizes, *inside).swapaxes(0, 1).reshape(-1, *inside)
    blocks = lax.psum_scatter(blocks, core, scatter_dimension=0, tiled=True)
    return lax.psum_scatter(blocks, chips, scatter_dimension=0, tiled=True)[0]


def gather_faces(extended, face_links, face_weight, first_cell, cell_count):
    summed = jnp.zeros((extended.shape[0], cell_count), jnp.float32)
    for face_num in range(FACES):
        neighbours = lax.dynamic_slice_in_dim(face_links[face_num], first_cell, cell_count)
        weights = lax.dynamic_slice_in_dim(face_weight[face_num], first_cell, cell_count)
        summed = summed + weights[None] * jnp.take(extended, neighbours, axis=1)
    return summed


def apply_transpose(flux_jacobian, vectors):
    return jnp.einsum("jic,bjc->bic", flux_jacobian, vectors, precision=lax.Precision.HIGHEST)


def tile_pair(field, lower_cells, upper_cells):
    return jnp.concatenate(
        [jnp.take(field, lower_cells, axis=1), jnp.take(field, upper_cells, axis=1)], axis=1
    )


def shards(
    mean_adjoint,
    harm_adjoint,
    harm_flow,
    flux_jacobian,
    face_weight,
    face_links,
    face_tiles,
    pseudo_step,
    mean_source,
    harm_order,
):
    cell_count = mean_adjoint.shape[1]
    rim_width = face_tiles.shape[1]
    harm_devices = lax.axis_size(HARM)
    weight_sum = jnp.sum(face_weight, axis=0)
    frequency = BASE_FREQ * (harm_order[0].astype(jnp.float32) + 1.0)
    mean_state = mean_adjoint
    harm_state = harm_adjoint[0]
    flow_real = harm_flow[0, 0]
    flow_imag = harm_flow[0, 1]
    for section_num in range(SECTIONS):
        section_coeff = 1.0 / (SECTIONS - section_num)
        harm_rows = harm_state.reshape(2 * VARS, cell_count)
        harm_wide = extended_2(
            tile_pair(harm_rows, face_tiles[0], face_tiles[1]), (("cells", 1),), rim_width
        )
        piece_len = rim_width // harm_devices
        offset = lax.axis_index(HARM) * piece_len
        lower_part = lax.dynamic_slice_in_dim(face_tiles[0], offset, piece_len)
        upper_part = lax.dynamic_slice_in_dim(face_tiles[1], offset, piece_len)
        mean_wide = extended_2(
            tile_pair(mean_state, lower_part, upper_part), (("cells", 1),), piece_len
        )
        lower_rim, upper_rim = (
            lax.all_gather(mean_wide[:, :piece_len], HARM, axis=1, tiled=True),
            lax.all_gather(mean_wide[:, 3 * piece_len :], HARM, axis=1, tiled=True),
        )
        mean_ext = jnp.concatenate([mean_state, lower_rim, upper_rim], axis=1)
        harm_ext = jnp.concatenate(
            [harm_rows, harm_wide[:, :rim_width], harm_wide[:, 3 * rim_width :]], axis=1
        )
        extended = jnp.concatenate([mean_ext, harm_ext], axis=0)
        local_stress = harm_state[0] * flow_real + harm_state[1] * flow_imag
        harm_gathered = gather_faces(extended[VARS:], face_links, face_weight, 0, cell_count)
        harm_flux = (weight_sum[None] * harm_rows - harm_gathered).reshape(2, VARS, cell_count)
        harm_terms = apply_transpose(flux_jacobian, harm_flux)
        real_res = harm_terms[0] + frequency * harm_state[1] - mean_state * flow_real
        imag_res = harm_terms[1] - frequency * harm_state[0] - mean_state * flow_imag
        harm_res = jnp.stack([real_res, imag_res], axis=0)
        stress_part = scatter_pairs(local_stress, "harm_0", "harm_1", 1)
        quarter = cell_count // harm_devices
        offset_cells = lax.axis_index(HARM) * quarter
        mean_gathered = gather_faces(
            extended[:VARS], face_links, face_weight, offset_cells, quarter
        )
        mean_slice = lax.dynamic_slice_in_dim(mean_state, offset_cells, quarter, 1)
        weight_slice = lax.dynamic_slice_in_dim(weight_sum, offset_cells, quarter)
        jacobian_slice = lax.dynamic_slice_in_dim(flux_jacobian, offset_cells, quarter, 2)
        source_slice = lax.dynamic_slice_in_dim(mean_source, offset_cells, quarter, 1)
        start_slice = lax.dynamic_slice_in_dim(mean_adjoint, offset_cells, quarter, 1)
        step_slice = lax.dynamic_slice_in_dim(pseudo_step, offset_cells, quarter)
        mean_flux = weight_slice[None] * mean_slice - mean_gathered - stress_part
        mean_res = apply_transpose(jacobian_slice, mean_flux[None])[0] - source_slice
        new_slice = start_slice - section_coeff * step_slice[None] * mean_res
        next_mean = lax.all_gather(new_slice, HARM, axis=1, tiled=True)
        harm_state = harm_adjoint[0] - section_coeff * pseudo_step * harm_res
        mean_state = next_mean
    return (mean_state, harm_state[None])


def solution(mesh):
    finer = Mesh(mesh.devices.reshape(mesh.shape["cells"], 2, 2), ("cells", "harm_0", "harm_1"))
    return jax.shard_map(
        shards,
        mesh=finer,
        in_specs=(
            P(None, "cells"),
            P(HARM, None, None, "cells"),
            P(HARM, None, None, "cells"),
            P(None, None, "cells"),
            P(None, "cells"),
            P(None, "cells"),
            P(None, "cells"),
            P("cells"),
            P(None, "cells"),
            P(HARM),
        ),
        out_specs=(P(None, "cells"), P(HARM, None, None, "cells")),
        check_vma=False,
    )
```

profile of v0, /device:TPU:1, one launch (start us, length us, event | category | flops | bytes accessed | tf_op | source)
XLA Modules:
  0.0 329.4 jit_solution(17895792721489467537)
XLA Ops:
  20.5 13.2 %collective-permute-start.5 = (f32[10,1024]{0,1:T(8,128)}, f32[10,1024]{0,1:T(8,128)}, u32[]{:S(2)}, u32[]{:S(2)}) collective-permute-start(f32[10,1024]{0,1:T(8,128)} %select_bitcast_fusion), channel_id=1, source_target_pairs={{4,0},{8,4},{12,8},{16,12},{20,16},{24,20},{28,24},{32,28},{36,32}... | collective-permute-start | bytes 122888 | tf_op jit(solution)/shard_map/ppermute | solution.py:25
  39.1 7.6 %collective-permute-start.1 = (f32[5,256]{0,1:T(8,128)}, f32[5,256]{0,1:T(8,128)}, u32[]{:S(2)}, u32[]{:S(2)}) collective-permute-start(f32[5,256]{0,1:T(8,128)} %select_bitcast_fusion.2), channel_id=1, source_target_pairs={{4,0},{8,4},{12,8},{16,12},{20,16},{24,20},{28,24},{32,28},{36,32}... | collective-permute-start | bytes 15368 | tf_op jit(solution)/shard_map/ppermute | solution.py:25
  74.3 10.8 %all_gather.18 = f32[5,1024]{0,1:T(8,128)} all-gather(f32[5,256]{0,1:T(8,128)} %collective-permute-done), channel_id=1, replica_groups=mesh['cells'=128,'harm_0'=2,'harm_1'=2] {'harm_0','harm_1'}, dimensions={1}, use_global_device_ids=true | all-gather | bytes 25600 | tf_op jit(solution)/shard_map/all_gather | solution.py:99
  85.1 9.9 %all_gather.19 = f32[5,1024]{0,1:T(8,128)} all-gather(f32[5,256]{0,1:T(8,128)} %collective-permute-done.1), channel_id=1, replica_groups=mesh['cells'=128,'harm_0'=2,'harm_1'=2] {'harm_0','harm_1'}, dimensions={1}, use_global_device_ids=true | all-gather | bytes 25600 | tf_op jit(solution)/shard_map/all_gather | solution.py:100
  96.3 5.5 %gather_fusion.18 = f32[2048,10]{1,0:T(8,128)S(1)} fusion(f32[10,4096]{0,1:T(8,128)S(1)} %pad_maximum_fusion.1, s32[2048]{0:T(1024)S(1)} %copy-done.31), kind=kCustom, calls=%fused_computation.3.clone | custom fusion | bytes 172032 | tf_op jit(solution)/shard_map/jit(_take)/gather | solution.py:50
  102.1 6.4 %gather_fusion.19 = f32[2048,10]{1,0:T(8,128)S(1)} fusion(f32[10,4096]{0,1:T(8,128)S(1)} %pad_maximum_fusion.1, s32[2048]{0:T(1024)} %get-tuple-element.55), kind=kCustom, calls=%fused_computation.21.clone | custom fusion | bytes 172032 | tf_op jit(solution)/shard_map/jit(_take)/gather | solution.py:50
  109.6 6.4 %gather_fusion.20 = f32[2048,10]{1,0:T(8,128)S(1)} fusion(f32[10,4096]{0,1:T(8,128)S(1)} %pad_maximum_fusion.1, s32[2048]{0:T(1024)} %get-tuple-element.56), kind=kCustom, calls=%fused_computation.22.clone | custom fusion | bytes 172032 | tf_op jit(solution)/shard_map/jit(_take)/gather | solution.py:50
  117.0 6.4 %gather_fusion.21 = f32[2048,10]{1,0:T(8,128)S(1)} fusion(f32[10,4096]{0,1:T(8,128)S(1)} %pad_maximum_fusion.1, s32[2048]{0:T(1024)} %get-tuple-element.57), kind=kCustom, calls=%fused_computation.23.clone | custom fusion | bytes 172032 | tf_op jit(solution)/shard_map/jit(_take)/gather | solution.py:50
  124.4 6.4 %gather_fusion.22 = f32[2048,10]{1,0:T(8,128)S(1)} fusion(f32[10,4096]{0,1:T(8,128)S(1)} %pad_maximum_fusion.1, s32[2048]{0:T(1024)} %get-tuple-element.58), kind=kCustom, calls=%fused_computation.24.clone | custom fusion | bytes 172032 | tf_op jit(solution)/shard_map/jit(_take)/gather | solution.py:50
  131.9 6.4 %gather_fusion.23 = f32[2048,10]{1,0:T(8,128)S(1)} fusion(f32[10,4096]{0,1:T(8,128)S(1)} %pad_maximum_fusion.1, s32[2048]{0:T(1024)} %get-tuple-element.59), kind=kCustom, calls=%fused_computation.25.clone | custom fusion | bytes 172032 | tf_op jit(solution)/shard_map/jit(_take)/gather | solution.py:50
  141.1 16.4 %fusion.58 = f32[2048,2,5]{2,1,0:T(2,128)} fusion(f32[2,5,2048]{1,0,2:T(2,128)S(1)} %copy.274, f32[5,5,2048]{1,0,2:T(8,128)} %copy.275), kind=kOutput, calls=%fused_computation.202 | convolution fusion | flops 1228800 | bytes 368640 | tf_op jit(solution)/shard_map/jic,bjc->bic/dot_general | solution.py:55
  171.2 7.6 %collective-permute-start.7 = (f32[10,1024]{1,0:T(8,128)}, f32[10,1024]{1,0:T(8,128)}, u32[]{:S(2)}, u32[]{:S(2)}) collective-permute-start(f32[10,1024]{1,0:T(8,128)} %select_bitcast_fusion.4), channel_id=1, source_target_pairs={{4,0},{8,4},{12,8},{16,12},{20,16},{24,20},{28,24},{32,28},{36,32}... | collective-permute-start | bytes 122888 | tf_op jit(solution)/shard_map/ppermute | solution.py:25
  195.1 5.5 %gather_fusion.26 = f32[2048,10]{1,0:T(8,128)S(1)} fusion(f32[10,4096]{0,1:T(8,128)S(1)} %copy.282, s32[2048]{0:T(1024)S(1)} %copy-done.32), kind=kCustom, calls=%fused_computation.26.clone | custom fusion | bytes 172032 | tf_op jit(solution)/shard_map/jit(_take)/gather | solution.py:50
  200.6 7.6 %gather_fusion.27 = f32[2048,10]{1,0:T(8,128)} fusion(f32[10,4096]{0,1:T(8,128)S(1)} %copy.282, s32[2048]{0:T(1024)S(1)} %copy-done.30), kind=kCustom, calls=%fused_computation.27.clone | custom fusion | bytes 172032 | tf_op jit(solution)/shard_map/jit(_take)/gather | solution.py:50
  208.2 7.6 %gather_fusion.28 = f32[2048,10]{1,0:T(8,128)} fusion(f32[10,4096]{0,1:T(8,128)S(1)} %copy.282, s32[2048]{0:T(1024)S(1)} %copy-done.29), kind=kCustom, calls=%fused_computation.28.clone | custom fusion | bytes 172032 | tf_op jit(solution)/shard_map/jit(_take)/gather | solution.py:50
  215.8 7.6 %gather_fusion.29 = f32[2048,10]{1,0:T(8,128)} fusion(f32[10,4096]{0,1:T(8,128)S(1)} %copy.282, s32[2048]{0:T(1024)S(1)} %copy-done.28), kind=kCustom, calls=%fused_computation.29.clone | custom fusion | bytes 172032 | tf_op jit(solution)/shard_map/jit(_take)/gather | solution.py:50
  223.5 7.6 %gather_fusion.30 = f32[2048,10]{1,0:T(8,128)} fusion(f32[10,4096]{0,1:T(8,128)S(1)} %copy.282, s32[2048]{0:T(1024)S(1)} %copy-done.27), kind=kCustom, calls=%fused_computation.30.clone | custom fusion | bytes 172032 | tf_op jit(solution)/shard_map/jit(_take)/gather | solution.py:50
  231.1 7.6 %gather_fusion.31 = f32[2048,10]{1,0:T(8,128)} fusion(f32[10,4096]{0,1:T(8,128)S(1)} %copy.282, s32[2048]{0:T(1024)S(1)} %copy-done.26), kind=kCustom, calls=%fused_computation.31.clone | custom fusion | bytes 172032 | tf_op jit(solution)/shard_map/jit(_take)/gather | solution.py:50
  245.9 16.4 %fusion.59 = f32[2048,2,5]{2,1,0:T(2,128)} fusion(f32[2,5,2048]{1,0,2:T(2,128)S(1)} %copy.294, f32[5,5,2048]{1,0,2:T(8,128)} %copy.275), kind=kOutput, calls=%fused_computation.203 | convolution fusion | flops 1228800 | bytes 368640 | tf_op jit(solution)/shard_map/jic,bjc->bic/dot_general | solution.py:55
  267.1 7.3 %all_gather.20 = f32[5,2048]{1,0:T(8,128)S(1)} all-gather(f32[5,512]{1,0:T(8,128)S(1)} %fusion.28), channel_id=1, replica_groups=mesh['cells'=128,'harm_0'=2,'harm_1'=2] {'harm_0','harm_1'}, dimensions={1}, use_global_device_ids=true | all-gather | bytes 51200 | tf_op jit(solution)/shard_map/all_gather | solution.py:129
  278.9 7.6 %collective-permute-start.3 = (f32[5,256]{1,0:T(8,128)S(1)}, f32[5,256]{1,0:T(8,128)S(1)}, u32[]{:S(2)}, u32[]{:S(2)}) collective-permute-start(f32[5,256]{1,0:T(8,128)S(1)} %select_bitcast_fusion.6), channel_id=1, source_target_pairs={{4,0},{8,4},{12,8},{16,12},{20,16},{24,20},{28,24},{32,28},{36,32}... | collective-permute-start | bytes 15368 | tf_op jit(solution)/shard_map/ppermute | solution.py:25
  287.2 7.2 %all_gather.21 = f32[5,1024]{1,0:T(8,128)S(1)} all-gather(f32[5,256]{1,0:T(8,128)S(1)} %collective-permute-done.2), channel_id=1, replica_groups=mesh['cells'=128,'harm_0'=2,'harm_1'=2] {'harm_0','harm_1'}, dimensions={1}, use_global_device_ids=true | all-gather | bytes 25600 | tf_op jit(solution)/shard_map/all_gather | solution.py:99
  294.5 6.9 %all_gather.22 = f32[5,1024]{1,0:T(8,128)S(1)} all-gather(f32[5,256]{1,0:T(8,128)S(1)} %collective-permute-done.3), channel_id=1, replica_groups=mesh['cells'=128,'harm_0'=2,'harm_1'=2] {'harm_0','harm_1'}, dimensions={1}, use_global_device_ids=true | all-gather | bytes 25600 | tf_op jit(solution)/shard_map/all_gather | solution.py:100
  315.5 6.7 %all_gather.23 = f32[5,2048]{1,0:T(8,128)S(1)} all-gather(f32[5,512]{1,0:T(8,128)S(1)} %fusion.26), channel_id=1, replica_groups=mesh['cells'=128,'harm_0'=2,'harm_1'=2] {'harm_0','harm_1'}, dimensions={1}, use_global_device_ids=true | all-gather | bytes 51200 | tf_op jit(solution)/shard_map/all_gather | solution.py:129
  (375 shorter events, 114.2 us)
Async XLA Ops:
  7.2 238.6 %reduce-scatter.5.cloned.1.call-start = ((), (), s32[]{:S(2)}) async-start(), calls=%async_computation.4 | async-start | bytes 98304 | tf_op jit(solution)/shard_map/reduce_scatter | solution.py:41
  12.2 34.5 %copy-start.45 = (s32[6,2048]{1,0:T(8,128)S(1)}, s32[6,2048]{1,0:T(8,128)}, u32[]{:S(2)}) copy-start(s32[6,2048]{1,0:T(8,128)} %param.23) | copy-start | bytes 147460
  12.5 39.8 %copy-start.40 = (f32[2048]{0:T(1024)S(1)}, f32[2048]{0:T(1024)}, u32[]{:S(2)}) copy-start(f32[2048]{0:T(1024)} %param.25) | copy-start | bytes 24580
  12.5 41.0 %copy-start.20 = (f32[6,2048]{1,0:T(8,128)S(1)}, f32[6,2048]{1,0:T(8,128)}, u32[]{:S(2)}) copy-start(f32[6,2048]{1,0:T(8,128)} %param.22) | copy-start | bytes 147460
  12.5 82.5 %collective-permute-start.4 = (f32[10,1024]{0,1:T(8,128)S(1)}, f32[10,1024]{0,1:T(8,128)}, u32[]{:S(2)}, u32[]{:S(2)}) collective-permute-start(f32[10,1024]{0,1:T(8,128)S(1)} %select_bitcast_fusion.1), channel_id=1, source_target_pairs={{0,4},{4,8},{8,12},{12,16},{16,20},{20,24},{24,28},{28,32},{32,36}... | collective-permute-start | bytes 122888 | tf_op jit(solution)/shard_map/ppermute | solution.py:22
  19.5 45.5 %copy-start.6 = (f32[5,5,2048]{2,1,0:T(8,128)S(1)}, f32[5,5,2048]{2,1,0:T(8,128)}, u32[]{:S(2)}) copy-start(f32[5,5,2048]{2,1,0:T(8,128)} %param.21) | copy-start | bytes 614404
  20.5 74.5 %collective-permute-start.5 = (f32[10,1024]{0,1:T(8,128)}, f32[10,1024]{0,1:T(8,128)}, u32[]{:S(2)}, u32[]{:S(2)}) collective-permute-start(f32[10,1024]{0,1:T(8,128)} %select_bitcast_fusion), channel_id=1, source_target_pairs={{4,0},{8,4},{12,8},{16,12},{20,16},{24,20},{28,24},{32,28},{36,32}... | collective-permute-start | bytes 122888 | tf_op jit(solution)/shard_map/ppermute | solution.py:25
  34.2 35.5 %copy-start = (f32[5,2048]{0,1:T(8,128)}, f32[5,2048]{0,1:T(8,128)S(1)}, u32[]{:S(2)}) copy-start(f32[5,2048]{0,1:T(8,128)S(1)} %copy.235) | copy-start | bytes 122884
  35.7 38.6 %collective-permute-start = (f32[5,256]{0,1:T(8,128)}, f32[5,256]{0,1:T(8,128)}, u32[]{:S(2)}, u32[]{:S(2)}) collective-permute-start(f32[5,256]{0,1:T(8,128)} %select_bitcast_fusion.3), channel_id=1, source_target_pairs={{0,4},{4,8},{8,12},{12,16},{16,20},{20,24},{24,28},{28,32},{32,36}... | collective-permute-start | bytes 15368 | tf_op jit(solution)/shard_map/ppermute | solution.py:22
  39.1 45.9 %collective-permute-start.1 = (f32[5,256]{0,1:T(8,128)}, f32[5,256]{0,1:T(8,128)}, u32[]{:S(2)}, u32[]{:S(2)}) collective-permute-start(f32[5,256]{0,1:T(8,128)} %select_bitcast_fusion.2), channel_id=1, source_target_pairs={{4,0},{8,4},{12,8},{16,12},{20,16},{24,20},{28,24},{32,28},{36,32}... | collective-permute-start | bytes 15368 | tf_op jit(solution)/shard_map/ppermute | solution.py:25
  168.5 25.0 %collective-permute-start.6 = (f32[10,1024]{1,0:T(8,128)}, f32[10,1024]{1,0:T(8,128)}, u32[]{:S(2)}, u32[]{:S(2)}) collective-permute-start(f32[10,1024]{1,0:T(8,128)} %select_bitcast_fusion.5), channel_id=1, source_target_pairs={{0,4},{4,8},{8,12},{12,16},{16,20},{20,24},{24,28},{28,32},{32,36}... | collective-permute-start | bytes 122888 | tf_op jit(solution)/shard_map/ppermute | solution.py:22
  171.2 22.3 %collective-permute-start.7 = (f32[10,1024]{1,0:T(8,128)}, f32[10,1024]{1,0:T(8,128)}, u32[]{:S(2)}, u32[]{:S(2)}) collective-permute-start(f32[10,1024]{1,0:T(8,128)} %select_bitcast_fusion.4), channel_id=1, source_target_pairs={{4,0},{8,4},{12,8},{16,12},{20,16},{24,20},{28,24},{32,28},{36,32}... | collective-permute-start | bytes 122888 | tf_op jit(solution)/shard_map/ppermute | solution.py:25
  180.5 84.8 %reduce-scatter.9.cloned.1.call-start = ((), (), s32[]{:S(2)}) async-start(), calls=%async_computation.6 | async-start | bytes 98304 | tf_op jit(solution)/shard_map/reduce_scatter | solution.py:41
  193.2 72.2 %reduce-scatter.7.cloned.1.call-start = ((), (), s32[]{:S(2)}) async-start(), calls=%async_computation.5 | async-start | bytes 49152 | tf_op jit(solution)/shard_map/reduce_scatter | solution.py:42
  195.1 28.4 %copy-start.27 = (s32[2048]{0:T(1024)S(1)}, s32[2048]{0:T(1024)}, u32[]{:S(2)}) copy-start(s32[2048]{0:T(1024)} %get-tuple-element.58) | copy-start | bytes 24580
  200.6 30.5 %copy-start.26 = (s32[2048]{0:T(1024)S(1)}, s32[2048]{0:T(1024)}, u32[]{:S(2)}) copy-start(s32[2048]{0:T(1024)} %get-tuple-element.59) | copy-start | bytes 24580
  245.8 68.1 %reduce-scatter.11.cloned.1.call-start = ((), (), s32[]{:S(2)}) async-start(), calls=%async_computation.7 | async-start | bytes 49152 | tf_op jit(solution)/shard_map/reduce_scatter | solution.py:42
  274.8 28.5 %copy-start.69 = (s32[1024]{0:T(1024)S(1)}, s32[1024]{0:T(1024)}, u32[]{:S(2)}) copy-start(s32[1024]{0:T(1024)} %pad_clamp_fusion.4) | copy-start | bytes 12292
  276.6 27.7 %copy-start.71 = (s32[1024]{0:T(1024)S(1)}, s32[1024]{0:T(1024)}, u32[]{:S(2)}) copy-start(s32[1024]{0:T(1024)} %pad_clamp_fusion.3) | copy-start | bytes 12292
  276.6 28.7 %copy-start.73 = (s32[1024]{0:T(1024)S(1)}, s32[1024]{0:T(1024)}, u32[]{:S(2)}) copy-start(s32[1024]{0:T(1024)} %pad_clamp_fusion.2) | copy-start | bytes 12292
  276.6 30.4 %copy-start.75 = (s32[1024]{0:T(1024)S(1)}, s32[1024]{0:T(1024)}, u32[]{:S(2)}) copy-start(s32[1024]{0:T(1024)} %pad_clamp_fusion.1) | copy-start | bytes 12292
  276.7 32.0 %copy-start.77 = (s32[1024]{0:T(1024)S(1)}, s32[1024]{0:T(1024)}, u32[]{:S(2)}) copy-start(s32[1024]{0:T(1024)} %pad_clamp_fusion) | copy-start | bytes 12292
  276.9 10.4 %collective-permute-start.2 = (f32[5,256]{1,0:T(8,128)S(1)}, f32[5,256]{1,0:T(8,128)S(1)}, u32[]{:S(2)}, u32[]{:S(2)}) collective-permute-start(f32[5,256]{1,0:T(8,128)S(1)} %select_bitcast_fusion.7), channel_id=1, source_target_pairs={{0,4},{4,8},{8,12},{12,16},{16,20},{20,24},{24,28},{28,32},{32,36}... | collective-permute-start | bytes 15368 | tf_op jit(solution)/shard_map/ppermute | solution.py:22
  278.9 15.6 %collective-permute-start.3 = (f32[5,256]{1,0:T(8,128)S(1)}, f32[5,256]{1,0:T(8,128)S(1)}, u32[]{:S(2)}, u32[]{:S(2)}) collective-permute-start(f32[5,256]{1,0:T(8,128)S(1)} %select_bitcast_fusion.6), channel_id=1, source_target_pairs={{4,0},{8,4},{12,8},{16,12},{20,16},{24,20},{28,24},{32,28},{36,32}... | collective-permute-start | bytes 15368 | tf_op jit(solution)/shard_map/ppermute | solution.py:25
  (89 other events, 658.6 us)
Sparse Core Ops, SparseCore 0:
  180.6 8.8 reduce-scatter.4
  193.3 16.3 reduce-scatter.8
  245.9 10.5 reduce-scatter.6
  265.5 12.3 reduce-scatter.10
where the time goes:
time: 331 us; the launch traced here: 329 us
  local copies, waits for them, and re-layouts  160 us (48%)
  blocking collectives  48.9 us (15%)
  starting transfers between devices  46.2 us (14%)
  matrix products  32.9 us (10%)
  other arithmetic  25.3 us (8%)
  between operations  16.3 us (5%)
    gather x48, local copies, waits for them, and re-layouts, gather_faces(): summed = summed + weights[None] * jnp.take(extended, neighbours, axis=1)  113 us
    ppermute x4, starting transfers between devices, extended_2(): lax.ppermute(lax.slice_in_dim(block, 0, width, axis=dim), axis, backward)  35.9 us
    dot_general x2, matrix products, apply_transpose(): jnp.einsum('jic,bjc->bic', flux_jacobian, vectors, precision=lax.Precisio...  32.9 us
    all_gather x2, blocking collectives, shards(): lax.all_gather(mean_wide[:, :piece_len], HARM, axis=1, tiled=True)  18 us
    all_gather x2, blocking collectives, shards(): lax.all_gather(mean_wide[:, 3 * piece_len:], HARM, axis=1, tiled=True)  16.8 us
    all_gather x2, blocking collectives, shards(): next_mean = lax.all_gather(new_slice, HARM, axis=1, tiled=True)  14 us
    ppermute x4, starting transfers between devices, extended_2(): lax.ppermute(lax.slice_in_dim(block, block.shape[dim] - width, None, axis...  9.89 us
    gather x6, local copies, waits for them, and re-layouts, tile_pair(): jnp.take(field, lower_cells, axis=1)  7.97 us
  transfers between devices with their start and end apart: 12, of which 0 were waited for; matrix products, arithmetic and copies ran while one was open for 41% of the time, Pallas kernels for 0%

commit v1 on v0

v1 whole, which is shorter than its diff:
```python
import jax
import jax.numpy as jnp
from jax import lax
from jax.experimental import pallas as pl
from jax.experimental.pallas import tpu as pltpu
from jax.sharding import Mesh
from jax.sharding import PartitionSpec as P

VARS = 5
FACES = 6
SECTIONS = 2
ROWS = 3 * VARS
HARM = ("harm_0", "harm_1")
LANES = 128
SUBS = 8
BASE_FREQ = 0.8
F32 = jnp.float32


def struct(*shape, dtype=F32):
    return jax.ShapeDtypeStruct(shape, dtype)


def spread(row):
    return jnp.broadcast_to(row, (SUBS, LANES))


def packed(tile, first):
    sub = lax.broadcasted_iota(jnp.int32, (SUBS, LANES), 0)
    out = spread(tile(first))
    for i in range(1, SUBS):
        out = jnp.where(sub == i, spread(tile(first + i)), out)
    return out


def picked(row, count, index):
    low = index & (LANES - 1)
    high = index >> 7
    out = [None] * ROWS
    for h in range(count):
        hit = high == h
        for r in range(ROWS):
            value = jnp.take_along_axis(spread(row(r, h)), low, axis=1)
            out[r] = jnp.where(hit, value, 0.0 if h == 0 else out[r])
    return out


def store_tiles(row, tile_index, pay_a, pay_b, rows):
    for pay, index in zip((pay_a, pay_b), tile_index):
        for r, value in enumerate(picked(row, rows, index)):
            pay[r] = value


def native_row(mean_ref, harm_ref):
    def row(r, h):
        lanes = slice(h * LANES, (h + 1) * LANES)
        if r < VARS:
            return mean_ref[r : r + 1, lanes]
        part, var = divmod(r - VARS, VARS)
        return harm_ref[0, part, var : var + 1, lanes]

    return row


def open_kernel(odd_ref, mean_ref, harm_ref, flow_ref, tiles_ref, pay_a, pay_b, stress_ref, tile_idx):
    groups = mean_ref.shape[1] // LANES
    odd = odd_ref[0] == 1
    lower, upper = (
        packed(lambda t, k=k: tiles_ref[k : k + 1, t * LANES : (t + 1) * LANES], 0) for k in range(2)
    )
    first = jnp.where(odd, lower, upper)
    second = jnp.where(odd, upper, lower)
    tile_idx[0] = first
    tile_idx[1] = second
    row = native_row(mean_ref, harm_ref)
    store_tiles(row, (first, second), pay_a, pay_b, groups)
    flow = native_row(mean_ref, flow_ref)
    for v in range(VARS):
        for g in range(0, groups, SUBS):
            part = packed(
                lambda t: row(VARS + v, t) * flow(VARS + v, t) + row(2 * VARS + v, t) * flow(2 * VARS + v, t), g
            )
            stress_ref[v, g : g + SUBS, :] = part


def gather_into(row, count, first, index_ref, weight_ref, start):
    halves = index_ref.shape[0] // FACES
    out = []
    for g in range(halves):

        def face(f, acc):
            values = picked(row, count, index_ref[f * halves + g] - first)
            weight = weight_ref[f * halves + g]
            return tuple(a + weight * v for a, v in zip(acc, values))

        out.append(lax.fori_loop(0, FACES, face, tuple(start(r, g) for r in range(ROWS))))
    return out


def prepare_kernel(
    odd_ref, mean_ref, harm_ref, flow_ref, jac_ref, weight_in, links_ref, source_ref,
    acc_ref, index_ref, weight_ref, wsum_ref, state_ref, jac_out, flow_out, source_out,
):
    groups = mean_ref.shape[1] // LANES
    halves = groups // SUBS
    even = odd_ref[0] == 0
    rim = groups * LANES
    for g in range(halves):
        total = None
        for f in range(FACES):
            lane = lambda t: slice(t * LANES, (t + 1) * LANES)
            link = packed(lambda t: links_ref[f : f + 1, lane(t)], g * SUBS)
            flipped = jnp.where(link >= rim, link ^ (rim // 2), link)
            index_ref[f * halves + g] = jnp.where(even, flipped, link)
            weight = packed(lambda t: weight_in[f : f + 1, lane(t)], g * SUBS)
            weight_ref[f * halves + g] = weight
            total = weight if total is None else total + weight
        wsum_ref[g * SUBS : (g + 1) * SUBS, :] = total
    row = native_row(mean_ref, harm_ref)
    flow = native_row(mean_ref, flow_ref)
    for g in range(0, groups, SUBS):
        at = slice(g, g + SUBS)
        for r in range(ROWS):
            state_ref[r, at, :] = packed(lambda t: row(r, t), g)
        for r in range(2 * VARS):
            flow_out[r, at, :] = packed(lambda t: flow(VARS + r, t), g)
        for v in range(VARS):
            source_out[v, at, :] = packed(lambda t: source_ref[v : v + 1, t * LANES : (t + 1) * LANES], g)
        for j in range(VARS):
            for i in range(VARS):
                jac_out[j * VARS + i, at, :] = packed(
                    lambda t: jac_ref[j, i : i + 1, t * LANES : (t + 1) * LANES], g
                )
    gather_own(state_ref, index_ref, weight_ref, acc_ref)


def gather_own(state_ref, index_ref, weight_ref, acc_ref):
    zero = jnp.zeros((SUBS, LANES), F32)
    row = lambda r, h: state_ref[r, h : h + 1, :]
    out = gather_into(row, state_ref.shape[1], 0, index_ref, weight_ref, lambda r, g: zero)
    for g, values in enumerate(out):
        for r in range(ROWS):
            acc_ref[r, g * SUBS : (g + 1) * SUBS, :] = values[r]


def new_state(
    coeff, order_ref, acc_ref, rim_a, rim_b, index_ref, weight_ref, wsum_ref, state_ref, start_ref,
    jac_ref, flow_ref, source_ref, step_ref, stress_refs, out_ref,
):
    groups = acc_ref.shape[1]
    rim_rows = rim_a.shape[1]

    def row(r, h):
        ref = rim_a if h < rim_rows else rim_b
        h = h % rim_rows
        return ref[r, h : h + 1, :]

    omega = BASE_FREQ * (order_ref[0].astype(F32) + 1.0)
    gathered = gather_into(
        row, 2 * rim_rows, groups * LANES, index_ref, weight_ref,
        lambda r, g: acc_ref[r, g * SUBS : (g + 1) * SUBS, :],
    )
    for g in range(groups // SUBS):
        at = slice(g * SUBS, (g + 1) * SUBS)
        state = [state_ref[r, at, :] for r in range(ROWS)]
        wsum = wsum_ref[at, :]
        flux = [wsum * s - x for s, x in zip(state, gathered[g])]
        scale = coeff * step_ref[at, :]
        for v in range(VARS):
            total = stress_refs[0][v, at, :]
            for ref in stress_refs[1:]:
                total = total + ref[v, at, :]
            flux[v] = flux[v] - total
        for part in range(3):
            for i in range(VARS):
                r = part * VARS + i
                res = jac_ref[i, at, :] * flux[part * VARS]
                for j in range(1, VARS):
                    res = res + jac_ref[j * VARS + i, at, :] * flux[part * VARS + j]
                if part == 0:
                    res = res - source_ref[i, at, :]
                else:
                    other = state[(3 - part) * VARS + i]
                    turned = omega * other
                    res = res + turned if part == 1 else res - turned
                    res = res - state[i] * flow_ref[(part - 1) * VARS + i, at, :]
                out_ref[r, at, :] = start_ref[r, at, :] - scale * res


def middle_kernel(
    order_ref, acc_ref, rim_a, rim_b, index_ref, weight_ref, wsum_ref, state_ref,
    jac_ref, flow_ref, source_ref, step_ref, tile_idx, s0, s1, s2, s3,
    out_ref, pay_a, pay_b, stress_ref, *, coeff,
):
    new_state(
        coeff, order_ref, acc_ref, rim_a, rim_b, index_ref, weight_ref, wsum_ref, state_ref, state_ref,
        jac_ref, flow_ref, source_ref, step_ref, (s0, s1, s2, s3), out_ref,
    )
    groups = acc_ref.shape[1]
    store_tiles(lambda r, h: out_ref[r, h : h + 1, :], (tile_idx[0], tile_idx[1]), pay_a, pay_b, groups)
    for v in range(VARS):
        stress_ref[v] = out_ref[VARS + v] * flow_ref[v] + out_ref[2 * VARS + v] * flow_ref[VARS + v]


def close_kernel(
    order_ref, acc_ref, rim_a, rim_b, index_ref, weight_ref, wsum_ref, state_ref, start_ref,
    jac_ref, flow_ref, source_ref, step_ref, s0, s1, s2, s3,
    mean_out, harm_out, out_ref, *, coeff,
):
    new_state(
        coeff, order_ref, acc_ref, rim_a, rim_b, index_ref, weight_ref, wsum_ref, state_ref, start_ref,
        jac_ref, flow_ref, source_ref, step_ref, (s0, s1, s2, s3), out_ref,
    )
    for t in range(acc_ref.shape[1]):
        lanes = slice(t * LANES, (t + 1) * LANES)
        for part in range(3):
            tile = packed_vars(lambda i: out_ref[part * VARS + i, t : t + 1, :])
            if part == 0:
                mean_out[:, lanes] = tile
            else:
                harm_out[0, part - 1, :, lanes] = tile


def packed_vars(row):
    sub = lax.broadcasted_iota(jnp.int32, (SUBS, LANES), 0)
    out = spread(row(0))
    for i in range(1, VARS):
        out = jnp.where(sub == i, spread(row(i)), out)
    return out[:VARS]


def launch(body, name, out_shape, scalars, args, scratch=()):
    smem = pl.BlockSpec(memory_space=pltpu.SMEM)
    vmem = pl.BlockSpec(memory_space=pltpu.VMEM)
    return pl.pallas_call(
        body,
        name=name,
        out_shape=out_shape,
        in_specs=[smem] * len(scalars) + [vmem] * len(args),
        out_specs=[vmem] * len(out_shape),
        scratch_shapes=scratch,
    )(*scalars, *args)


def exchange(pay_a, pay_b, stress):
    count = lax.axis_size("cells")
    near = [(b, b ^ 1) for b in range(count)]
    far = [(b, (b - 1 + 2 * (b % 2)) % count) for b in range(count)]
    rim_b = lax.ppermute(pay_b, "cells", far)
    rim_a = lax.ppermute(pay_a, "cells", near)
    others = [lax.ppermute(stress, HARM, [(k, k ^ m) for k in range(4)]) for m in (1, 2, 3)]
    return rim_a, rim_b, (stress, *others)


def shards(
    mean_adjoint,
    harm_adjoint,
    harm_flow,
    flux_jacobian,
    face_weight,
    face_links,
    face_tiles,
    pseudo_step,
    mean_source,
    harm_order,
):
    cells = mean_adjoint.shape[1]
    groups = cells // LANES
    halves = groups // SUBS
    rim_rows = face_tiles.shape[1] // LANES
    odd = (lax.axis_index("cells") % 2).astype(jnp.int32)[None]
    step = pseudo_step.reshape(groups, LANES)
    pays = (struct(ROWS, rim_rows, LANES), struct(ROWS, rim_rows, LANES), struct(VARS, groups, LANES))
    pay_a, pay_b, stress, tile_idx = launch(
        open_kernel, "open", pays + (struct(2, rim_rows, LANES, dtype=jnp.int32),), (odd,),
        (mean_adjoint, harm_adjoint, harm_flow, face_tiles),
    )
    rim_a, rim_b, parts = exchange(pay_a, pay_b, stress)
    fields = struct(ROWS, groups, LANES)
    acc, index, weight, wsum, start, jac, flow, source = launch(
        prepare_kernel, "prepare",
        (
            fields,
            struct(FACES * halves, SUBS, LANES, dtype=jnp.int32),
            struct(FACES * halves, SUBS, LANES),
            struct(groups, LANES),
            fields,
            struct(VARS * VARS, groups, LANES),
            struct(2 * VARS, groups, LANES),
            struct(VARS, groups, LANES),
        ),
        (odd,),
        (mean_adjoint, harm_adjoint, harm_flow, flux_jacobian, face_weight, face_links, mean_source),
    )
    state, pay_a, pay_b, stress = launch(
        lambda *refs: middle_kernel(*refs, coeff=1.0 / SECTIONS), "middle", (fields,) + pays, (harm_order,),
        (acc, rim_a, rim_b, index, weight, wsum, start, jac, flow, source, step, tile_idx, *parts),
    )
    rim_a, rim_b, parts = exchange(pay_a, pay_b, stress)
    (acc,) = launch(gather_own, "own", (fields,), (), (state, index, weight))
    mean_new, harm_new = launch(
        lambda *refs: close_kernel(*refs, coeff=1.0), "close",
        (struct(VARS, cells), struct(1, 2, VARS, cells)), (harm_order,),
        (acc, rim_a, rim_b, index, weight, wsum, state, start, jac, flow, source, step, *parts),
        scratch=[pltpu.VMEM((ROWS, groups, LANES), F32)],
    )
    return mean_new, harm_new


def solution(mesh):
    finer = Mesh(mesh.devices.reshape(mesh.shape["cells"], 2, 2), ("cells", *HARM))
    return jax.shard_map(
        shards,
        mesh=finer,
        in_specs=(
            P(None, "cells"),
            P(HARM, None, None, "cells"),
            P(HARM, None, None, "cells"),
            P(None, None, "cells"),
            P(None, "cells"),
            P(None, "cells"),
            P(None, "cells"),
            P("cells"),
            P(None, "cells"),
            P(HARM),
        ),
        out_specs=(P(None, "cells"), P(HARM, None, None, "cells")),
        check_vma=False,
    )
```

time: 331 us -> 77.8 us (0.24)
  local copies, waits for them, and re-layouts: 160 us -> 5.78 us
  blocking collectives: 48.9 us -> 0 us
  matrix products: 32.9 us -> 0 us
  Pallas kernels: 0 us -> 26.2 us
  other arithmetic: 25.3 us -> 0 us
  between operations: 16.3 us -> 1.51 us
    gather x60 -> x0, local copies, waits for them, and re-layouts: 129 us -> none  [the longest x48 113 us: gather_faces(): summed = summed + weights[None] * jnp.take(extended, neighbours, axis=1)]
    all_gather x6 -> x0, blocking collectives: 48.9 us -> none  [the longest x2 18 us: shards(): lax.all_gather(mean_wide[:, :piece_len], HARM, axis=1, tiled=True)]
    dot_general x2 -> x0, matrix products: 32.9 us -> none  [apply_transpose(): jnp.einsum('jic,bjc->bic', flux_jacobian, vectors, precision=lax.Precisio...]
    pallas_call x0 -> x5, Pallas kernels: none -> 26.2 us  [launch(): pl.pallas_call(body, name=name, out_shape=out_shape, in_specs=[smem] * le...]
    dot_general x2 -> x0, local copies, waits for them, and re-layouts: 5.53 us -> none  [apply_transpose(): jnp.einsum('jic,bjc->bic', flux_jacobian, vectors, precision=lax.Precisio...]
    gather x12 -> x0, other arithmetic: 5.42 us -> none
    dynamic_slice x12 -> x0, local copies, waits for them, and re-layouts: 5.2 us -> none  [the longest x3 3.77 us: gather_faces(): lax.dynamic_slice_in_dim(face_weight[face_num], first_cell, cell_count)]
    select_n x12 -> x0, other arithmetic: 4.64 us -> none  [the longest x5 2.41 us: tile_pair(): jnp.take(field, lower_cells, axis=1)]
  transfers between devices with their start and end apart: 12 -> 10, of which waited for: 0 -> 0; matrix products, arithmetic and copies ran while one was open for 41% -> 0% of each run, Pallas kernels for 0% -> 15%
where the time goes in v1:
time: 77.8 us; the launch traced here: 77.2 us
  starting transfers between devices  43.7 us (56%)
  Pallas kernels  26.2 us (34%)
  local copies, waits for them, and re-layouts  5.78 us (7%)
  between operations  1.51 us (2%)
    pallas_call x5, Pallas kernels, launch(): pl.pallas_call(body, name=name, out_shape=out_shape, in_specs=[smem] * le...  26.2 us
    ppermute x6, starting transfers between devices, exchange(): lax.ppermute(stress, HARM, [(k, k ^ m) for k in range(4)])  19.5 us
    ppermute x2, starting transfers between devices, exchange(): rim_b = lax.ppermute(pay_b, 'cells', far)  18.3 us
    ppermute x2, starting transfers between devices, exchange(): rim_a = lax.ppermute(pay_a, 'cells', near)  5.92 us
    unnamed x24, local copies, waits for them, and re-layouts  4.18 us
    pallas_call x1, local copies, waits for them, and re-layouts, launch(): pl.pallas_call(body, name=name, out_shape=out_shape, in_specs=[smem] * le...  1.6 us
  transfers between devices with their start and end apart: 10, of which 0 were waited for; matrix products, arithmetic and copies ran while one was open for 0% of the time, Pallas kernels for 15%

profile of v1, /device:TPU:1, one launch (start us, length us, event | category | flops | bytes accessed | tf_op | source)
XLA Modules:
  0.0 77.2 jit_solution(11680090636954318498)
XLA Ops:
  0.6 1.6 %copy.12.harm_ref = f32[1,2,5,2048]{3,2,1,0:T(8,128)} copy(f32[1,2,5,2048]{3,1,2,0:T(2,128)} %param.11) | data formatting | bytes 163840 | tf_op args[1]
  2.3 0.7 copy.13.flow_ref
  3.0 2.2 %open.1 = (f32[15,8,128]{2,1,0:T(8,128)}, f32[15,8,128]{2,1,0:T(8,128)}, f32[5,16,128]{2,1,0:T(8,128)}, s32[2,8,128]{2,1,0:T(8,128)}) custom-call(s32[1]{0:T(128)} %bitcast.odd_ref, f32[5,2048]{1,0:T(8,128)} %mean_ref.3, f32[1,2,5,2048]{3,2,1,0:T(8,128)} %copy.12.harm_ref, f32[1,2,5,2048]{3,2,1,0:T(8,128)} %copy.13.flow_ref, s32[2,1024]{1,0:T(2,128)} %tiles_ref.1), custom_call_target="tpu_custom_call" | custom-call | tf_op jit(solution)/shard_map/open/pallas_call | solution.py:235
  5.2 4.0 %collective-permute-start = (f32[15,8,128]{2,1,0:T(8,128)}, f32[15,8,128]{2,1,0:T(8,128)S(1)}, u32[]{:S(2)}, u32[]{:S(2)}) collective-permute-start(f32[15,8,128]{2,1,0:T(8,128)} %get-tuple-element.19), channel_id=1, source_target_pairs={{0,4},{4,0},{8,12},{12,8},{16,20},{20,16},{24,28},{28,24},{32,36},... | collective-permute-start | bytes 184328 | tf_op jit(solution)/shard_map/ppermute | solution.py:250
  9.2 14.3 %collective-permute-start.1 = (f32[15,8,128]{2,1,0:T(8,128)}, f32[15,8,128]{2,1,0:T(8,128)S(1)}, u32[]{:S(2)}, u32[]{:S(2)}) collective-permute-start(f32[15,8,128]{2,1,0:T(8,128)} %get-tuple-element.20), channel_id=1, source_target_pairs={{0,508},{4,8},{8,4},{12,16},{16,12},{20,24},{24,20},{28,32},{32,28... | collective-permute-start | bytes 184328 | tf_op jit(solution)/shard_map/ppermute | solution.py:249
  23.5 5.5 %collective-permute-start.4 = (f32[5,16,128]{2,1,0:T(8,128)}, f32[5,16,128]{2,1,0:T(8,128)S(1)}, u32[]{:S(2)}, u32[]{:S(2)}) collective-permute-start(f32[5,16,128]{2,1,0:T(8,128)} %get-tuple-element.29.refs_13_), channel_id=1, source_target_pairs={{0,3},{1,2},{2,1},{3,0},{4,7},{5,6},{6,5},{7,4},{8,11},{9,10},{10,... | collective-permute-start | bytes 122888 | tf_op jit(solution)/shard_map/ppermute | solution.py:251
  29.0 2.4 %collective-permute-start.3 = (f32[5,16,128]{2,1,0:T(8,128)}, f32[5,16,128]{2,1,0:T(8,128)S(1)}, u32[]{:S(2)}, u32[]{:S(2)}) collective-permute-start(f32[5,16,128]{2,1,0:T(8,128)} %get-tuple-element.29.refs_13_), channel_id=1, source_target_pairs={{0,2},{1,3},{2,0},{3,1},{4,6},{5,7},{6,4},{7,5},{8,10},{9,11},{10,... | collective-permute-start | bytes 122888 | tf_op jit(solution)/shard_map/ppermute | solution.py:251
  31.4 1.9 %collective-permute-start.2 = (f32[5,16,128]{2,1,0:T(8,128)}, f32[5,16,128]{2,1,0:T(8,128)S(1)}, u32[]{:S(2)}, u32[]{:S(2)}) collective-permute-start(f32[5,16,128]{2,1,0:T(8,128)} %get-tuple-element.29.refs_13_), channel_id=1, source_target_pairs={{0,1},{1,0},{2,3},{3,2},{4,5},{5,4},{6,7},{7,6},{8,9},{9,8},{10,11... | collective-permute-start | bytes 122888 | tf_op jit(solution)/shard_map/ppermute | solution.py:251
  34.0 6.0 %prepare.1 = (f32[15,16,128]{2,1,0:T(8,128)}, s32[12,8,128]{2,1,0:T(8,128)}, f32[12,8,128]{2,1,0:T(8,128)}, f32[16,128]{1,0:T(8,128)}, f32[15,16,128]{2,1,0:T(8,...) custom-call(s32[1]{0:T(128)} %bitcast.odd_ref, f32[5,2048]{1,0:T(8,128)} %mean_ref.3, ...), custom_call_target="tpu_custom_call" | custom-call | tf_op jit(solution)/shard_map/prepare/pallas_call | solution.py:235
  40.1 0.5 copy-done.5
  40.6 0.0 copy-done.7
  40.6 0.0 copy-done.1
  40.7 6.5 %middle.1 = (f32[15,16,128]{2,1,0:T(8,128)}, f32[15,8,128]{2,1,0:T(8,128)}, f32[15,8,128]{2,1,0:T(8,128)}, f32[5,16,128]{2,1,0:T(8,128)}) custom-call(s32[1]{0:T(128)S(6)} %copy.17.refs_0_, f32[15,16,128]{2,1,0:T(8,128)} %get-tuple-element.18.refs_1_, f32[15,8,128]{2,1,0:T(8,128)} %copy-done.1, f32[15,8,128]{2,1,0:T(8,128)} %copy-done.2, ...), custom_call_target="tpu_custom_call" | custom-call | tf_op jit(solution)/shard_map/middle/pallas_call | solution.py:235
  47.1 1.9 %collective-permute-start.5 = (f32[15,8,128]{2,1,0:T(8,128)}, f32[15,8,128]{2,1,0:T(8,128)S(1)}, u32[]{:S(2)}, u32[]{:S(2)}) collective-permute-start(f32[15,8,128]{2,1,0:T(8,128)} %get-tuple-element.31), channel_id=1, source_target_pairs={{0,4},{4,0},{8,12},{12,8},{16,20},{20,16},{24,28},{28,24},{32,36},... | collective-permute-start | bytes 184328 | tf_op jit(solution)/shard_map/ppermute | solution.py:250
  49.0 4.0 %collective-permute-start.6 = (f32[15,8,128]{2,1,0:T(8,128)}, f32[15,8,128]{2,1,0:T(8,128)S(1)}, u32[]{:S(2)}, u32[]{:S(2)}) collective-permute-start(f32[15,8,128]{2,1,0:T(8,128)} %get-tuple-element.32), channel_id=1, source_target_pairs={{0,508},{4,8},{8,4},{12,16},{16,12},{20,24},{24,20},{28,32},{32,28... | collective-permute-start | bytes 184328 | tf_op jit(solution)/shard_map/ppermute | solution.py:249
  53.1 5.3 %collective-permute-start.9 = (f32[5,16,128]{2,1,0:T(8,128)}, f32[5,16,128]{2,1,0:T(8,128)S(1)}, u32[]{:S(2)}, u32[]{:S(2)}) collective-permute-start(f32[5,16,128]{2,1,0:T(8,128)} %get-tuple-element.33.refs_13_), channel_id=1, source_target_pairs={{0,3},{1,2},{2,1},{3,0},{4,7},{5,6},{6,5},{7,4},{8,11},{9,10},{10,... | collective-permute-start | bytes 122888 | tf_op jit(solution)/shard_map/ppermute | solution.py:251
  58.4 2.4 %collective-permute-start.8 = (f32[5,16,128]{2,1,0:T(8,128)}, f32[5,16,128]{2,1,0:T(8,128)S(1)}, u32[]{:S(2)}, u32[]{:S(2)}) collective-permute-start(f32[5,16,128]{2,1,0:T(8,128)} %get-tuple-element.33.refs_13_), channel_id=1, source_target_pairs={{0,2},{1,3},{2,0},{3,1},{4,6},{5,7},{6,4},{7,5},{8,10},{9,11},{10,... | collective-permute-start | bytes 122888 | tf_op jit(solution)/shard_map/ppermute | solution.py:251
  60.8 1.9 %collective-permute-start.7 = (f32[5,16,128]{2,1,0:T(8,128)}, f32[5,16,128]{2,1,0:T(8,128)S(1)}, u32[]{:S(2)}, u32[]{:S(2)}) collective-permute-start(f32[5,16,128]{2,1,0:T(8,128)} %get-tuple-element.33.refs_13_), channel_id=1, source_target_pairs={{0,1},{1,0},{2,3},{3,2},{4,5},{5,4},{6,7},{7,6},{8,9},{9,8},{10,11... | collective-permute-start | bytes 122888 | tf_op jit(solution)/shard_map/ppermute | solution.py:251
  62.7 5.5 %own.1.refs_1_ = f32[15,16,128]{2,1,0:T(8,128)} custom-call(f32[15,16,128]{2,1,0:T(8,128)} %get-tuple-element.30.state_ref.refs_7_, s32[12,8,128]{2,1,0:T(8,128)} %get-tuple-element.21.refs_4_.index_ref, f32[12,8,128]{2,1,0:T(8,128)} %get-tuple-element.22.refs_5_.weight_ref), custom_call_target="tpu_custom_call" | custom-call | tf_op jit(solution)/shard_map/own/pallas_call | solution.py:235
  68.3 0.5 copy-done.8
  68.9 0.0 copy-done.3
  69.0 0.6 copy-done.4
  69.6 6.0 %close.1 = (f32[5,2048]{1,0:T(8,128)}, f32[1,2,5,2048]{3,2,1,0:T(8,128)}) custom-call(s32[1]{0:T(128)S(6)} %copy.17.refs_0_, f32[15,16,128]{2,1,0:T(8,128)} %own.1.refs_1_, f32[15,8,128]{2,1,0:T(8,128)} %copy-done.3, f32[15,8,128]{2,1,0:T(8,128)} %copy-done.4, s32[12,8,128]{2,1,0:T(8,128)} %get-tuple-element.21.refs_4_.index_ref, ...), custom_call_target="tpu_custom_call" | custom-call | tf_op jit(solution)/shard_map/close/pallas_call | solution.py:235
  75.6 1.6 %copy.16 = f32[1,2,5,2048]{3,1,2,0:T(2,128)} copy(f32[1,2,5,2048]{3,2,1,0:T(8,128)} %get-tuple-element.35) | data formatting | bytes 163840 | tf_op jit(solution)/shard_map/close/pallas_call | solution.py:235
  (26 shorter events, 0.1 us)
Async XLA Ops:
  0.6 1.6 %copy-start = (f32[1,2,5,2048]{3,1,2,0:T(2,128)S(1)}, f32[1,2,5,2048]{3,1,2,0:T(2,128)}, u32[]{:S(2)}) copy-start(f32[1,2,5,2048]{3,1,2,0:T(2,128)} %param.12) | copy-start | bytes 245764
  5.2 34.8 %collective-permute-start = (f32[15,8,128]{2,1,0:T(8,128)}, f32[15,8,128]{2,1,0:T(8,128)S(1)}, u32[]{:S(2)}, u32[]{:S(2)}) collective-permute-start(f32[15,8,128]{2,1,0:T(8,128)} %get-tuple-element.19), channel_id=1, source_target_pairs={{0,4},{4,0},{8,12},{12,8},{16,20},{20,16},{24,28},{28,24},{32,36},... | collective-permute-start | bytes 184328 | tf_op jit(solution)/shard_map/ppermute | solution.py:250
  9.2 30.8 %collective-permute-start.1 = (f32[15,8,128]{2,1,0:T(8,128)}, f32[15,8,128]{2,1,0:T(8,128)S(1)}, u32[]{:S(2)}, u32[]{:S(2)}) collective-permute-start(f32[15,8,128]{2,1,0:T(8,128)} %get-tuple-element.20), channel_id=1, source_target_pairs={{0,508},{4,8},{8,4},{12,16},{16,12},{20,24},{24,20},{28,32},{32,28... | collective-permute-start | bytes 184328 | tf_op jit(solution)/shard_map/ppermute | solution.py:249
  23.5 16.5 %collective-permute-start.4 = (f32[5,16,128]{2,1,0:T(8,128)}, f32[5,16,128]{2,1,0:T(8,128)S(1)}, u32[]{:S(2)}, u32[]{:S(2)}) collective-permute-start(f32[5,16,128]{2,1,0:T(8,128)} %get-tuple-element.29.refs_13_), channel_id=1, source_target_pairs={{0,3},{1,2},{2,1},{3,0},{4,7},{5,6},{6,5},{7,4},{8,11},{9,10},{10,... | collective-permute-start | bytes 122888 | tf_op jit(solution)/shard_map/ppermute | solution.py:251
  29.0 11.0 %collective-permute-start.3 = (f32[5,16,128]{2,1,0:T(8,128)}, f32[5,16,128]{2,1,0:T(8,128)S(1)}, u32[]{:S(2)}, u32[]{:S(2)}) collective-permute-start(f32[5,16,128]{2,1,0:T(8,128)} %get-tuple-element.29.refs_13_), channel_id=1, source_target_pairs={{0,2},{1,3},{2,0},{3,1},{4,6},{5,7},{6,4},{7,5},{8,10},{9,11},{10,... | collective-permute-start | bytes 122888 | tf_op jit(solution)/shard_map/ppermute | solution.py:251
  31.4 8.6 %collective-permute-start.2 = (f32[5,16,128]{2,1,0:T(8,128)}, f32[5,16,128]{2,1,0:T(8,128)S(1)}, u32[]{:S(2)}, u32[]{:S(2)}) collective-permute-start(f32[5,16,128]{2,1,0:T(8,128)} %get-tuple-element.29.refs_13_), channel_id=1, source_target_pairs={{0,1},{1,0},{2,3},{3,2},{4,5},{5,4},{6,7},{7,6},{8,9},{9,8},{10,11... | collective-permute-start | bytes 122888 | tf_op jit(solution)/shard_map/ppermute | solution.py:251
  40.0 0.6 copy-start.5
  40.0 0.6 copy-start.6
  40.0 0.6 copy-start.7
  40.0 0.6 copy-start.1
  40.0 0.6 copy-start.2
  47.1 21.2 %collective-permute-start.5 = (f32[15,8,128]{2,1,0:T(8,128)}, f32[15,8,128]{2,1,0:T(8,128)S(1)}, u32[]{:S(2)}, u32[]{:S(2)}) collective-permute-start(f32[15,8,128]{2,1,0:T(8,128)} %get-tuple-element.31), channel_id=1, source_target_pairs={{0,4},{4,0},{8,12},{12,8},{16,20},{20,16},{24,28},{28,24},{32,36},... | collective-permute-start | bytes 184328 | tf_op jit(solution)/shard_map/ppermute | solution.py:250
  49.0 19.3 %collective-permute-start.6 = (f32[15,8,128]{2,1,0:T(8,128)}, f32[15,8,128]{2,1,0:T(8,128)S(1)}, u32[]{:S(2)}, u32[]{:S(2)}) collective-permute-start(f32[15,8,128]{2,1,0:T(8,128)} %get-tuple-element.32), channel_id=1, source_target_pairs={{0,508},{4,8},{8,4},{12,16},{16,12},{20,24},{24,20},{28,32},{32,28... | collective-permute-start | bytes 184328 | tf_op jit(solution)/shard_map/ppermute | solution.py:249
  53.1 15.2 %collective-permute-start.9 = (f32[5,16,128]{2,1,0:T(8,128)}, f32[5,16,128]{2,1,0:T(8,128)S(1)}, u32[]{:S(2)}, u32[]{:S(2)}) collective-permute-start(f32[5,16,128]{2,1,0:T(8,128)} %get-tuple-element.33.refs_13_), channel_id=1, source_target_pairs={{0,3},{1,2},{2,1},{3,0},{4,7},{5,6},{6,5},{7,4},{8,11},{9,10},{10,... | collective-permute-start | bytes 122888 | tf_op jit(solution)/shard_map/ppermute | solution.py:251
  58.4 9.9 %collective-permute-start.8 = (f32[5,16,128]{2,1,0:T(8,128)}, f32[5,16,128]{2,1,0:T(8,128)S(1)}, u32[]{:S(2)}, u32[]{:S(2)}) collective-permute-start(f32[5,16,128]{2,1,0:T(8,128)} %get-tuple-element.33.refs_13_), channel_id=1, source_target_pairs={{0,2},{1,3},{2,0},{3,1},{4,6},{5,7},{6,4},{7,5},{8,10},{9,11},{10,... | collective-permute-start | bytes 122888 | tf_op jit(solution)/shard_map/ppermute | solution.py:251
  60.8 7.5 %collective-permute-start.7 = (f32[5,16,128]{2,1,0:T(8,128)}, f32[5,16,128]{2,1,0:T(8,128)S(1)}, u32[]{:S(2)}, u32[]{:S(2)}) collective-permute-start(f32[5,16,128]{2,1,0:T(8,128)} %get-tuple-element.33.refs_13_), channel_id=1, source_target_pairs={{0,1},{1,0},{2,3},{3,2},{4,5},{5,4},{6,7},{7,6},{8,9},{9,8},{10,11... | collective-permute-start | bytes 122888 | tf_op jit(solution)/shard_map/ppermute | solution.py:251
  68.3 0.6 copy-start.8
  68.3 0.6 copy-start.9
  68.3 0.6 copy-start.10
  68.3 0.6 copy-start.3
  69.0 0.6 copy-start.4

commit v2 on v1

--- a/solution.py
+++ b/solution.py
@@ -18,7 +18,7 @@
 
 
 def struct(*shape, dtype=F32):
-    return jax.ShapeDtypeStruct(shape, dtype)
+    return pltpu.VMEM(shape, dtype)
 
 
 def spread(row):
@@ -57,12 +57,27 @@
         if r < VARS:
             return mean_ref[r : r + 1, lanes]
         part, var = divmod(r - VARS, VARS)
-        return harm_ref[0, part, var : var + 1, lanes]
+        return harm_ref[var, part : part + 1, lanes]
 
     return row
 
 
-def open_kernel(odd_ref, mean_ref, harm_ref, flow_ref, tiles_ref, pay_a, pay_b, stress_ref, tile_idx):
+def fetch(sources, targets, sems):
+    copies = [pltpu.make_async_copy(s, t, sems.at[i]) for i, (s, t) in enumerate(zip(sources, targets))]
+    for copy in copies:
+        copy.start()
+    return [copy.wait for copy in copies]
+
+
+def open_kernel(
+    odd_ref, mean_hbm, harm_hbm, flow_hbm, tiles_hbm, pay_a, pay_b, stress_ref, tile_idx,
+    tiles_ref, mean_ref, harm_ref, flow_ref, sems,
+):
+    waits = fetch(
+        (tiles_hbm, mean_hbm, harm_hbm, flow_hbm), (tiles_ref, mean_ref, harm_ref, flow_ref), sems
+    )
+    for wait in waits:
+        wait()
     groups = mean_ref.shape[1] // LANES
     odd = odd_ref[0] == 1
     lower, upper = (
@@ -98,9 +113,17 @@
 
 
 def prepare_kernel(
-    odd_ref, mean_ref, harm_ref, flow_ref, jac_ref, weight_in, links_ref, source_ref,
-    acc_ref, index_ref, weight_ref, wsum_ref, state_ref, jac_out, flow_out, source_out,
-):
+    odd_ref, mean_hbm, harm_hbm, flow_hbm, jac_hbm, weight_hbm, links_hbm, source_hbm, step_hbm,
+    acc_ref, index_ref, weight_ref, wsum_ref, state_ref, jac_out, flow_out, source_out, step_out,
+    links_ref, weight_in, mean_ref, harm_ref, flow_ref, source_ref, jac_ref, sems,
+):
+    waits = fetch(
+        (links_hbm, weight_hbm, mean_hbm, harm_hbm, flow_hbm, source_hbm, jac_hbm, step_hbm),
+        (links_ref, weight_in, mean_ref, harm_ref, flow_ref, source_ref, jac_ref, step_out),
+        sems,
+    )
+    for wait in waits[:2]:
+        wait()
     groups = mean_ref.shape[1] // LANES
     halves = groups // SUBS
     even = odd_ref[0] == 0
@@ -118,10 +141,16 @@
         wsum_ref[g * SUBS : (g + 1) * SUBS, :] = total
     row = native_row(mean_ref, harm_ref)
     flow = native_row(mean_ref, flow_ref)
+    for wait in waits[2:4]:
+        wait()
+    for g in range(0, groups, SUBS):
+        for r in range(ROWS):
+            state_ref[r, g : g + SUBS, :] = packed(lambda t: row(r, t), g)
+    gather_own(state_ref, index_ref, weight_ref, acc_ref)
+    for wait in waits[4:]:
+        wait()
     for g in range(0, groups, SUBS):
         at = slice(g, g + SUBS)
-        for r in range(ROWS):
-            state_ref[r, at, :] = packed(lambda t: row(r, t), g)
         for r in range(2 * VARS):
             flow_out[r, at, :] = packed(lambda t: flow(VARS + r, t), g)
         for v in range(VARS):
@@ -131,7 +160,6 @@
                 jac_out[j * VARS + i, at, :] = packed(
                     lambda t: jac_ref[j, i : i + 1, t * LANES : (t + 1) * LANES], g
                 )
-    gather_own(state_ref, index_ref, weight_ref, acc_ref)
 
 
 def gather_own(state_ref, index_ref, weight_ref, acc_ref):
@@ -189,12 +217,12 @@
 
 def middle_kernel(
     order_ref, acc_ref, rim_a, rim_b, index_ref, weight_ref, wsum_ref, state_ref,
-    jac_ref, flow_ref, source_ref, step_ref, tile_idx, s0, s1, s2, s3,
+    jac_ref, flow_ref, source_ref, step_ref, tile_idx, s0, s1,
     out_ref, pay_a, pay_b, stress_ref, *, coeff,
 ):
     new_state(
         coeff, order_ref, acc_ref, rim_a, rim_b, index_ref, weight_ref, wsum_ref, state_ref, state_ref,
-        jac_ref, flow_ref, source_ref, step_ref, (s0, s1, s2, s3), out_ref,
+        jac_ref, flow_ref, source_ref, step_ref, (s0, s1), out_ref,
     )
     groups = acc_ref.shape[1]
     store_tiles(lambda r, h: out_ref[r, h : h + 1, :], (tile_idx[0], tile_idx[1]), pay_a, pay_b, groups)
@@ -204,42 +232,52 @@
 
 def close_kernel(
     order_ref, acc_ref, rim_a, rim_b, index_ref, weight_ref, wsum_ref, state_ref, start_ref,
-    jac_ref, flow_ref, source_ref, step_ref, s0, s1, s2, s3,
-    mean_out, harm_out, out_ref, *, coeff,
+    jac_ref, flow_ref, source_ref, step_ref, s0, s1,
+    mean_hbm, harm_hbm, out_ref, mean_out, harm_out, sems, *, coeff,
 ):
     new_state(
         coeff, order_ref, acc_ref, rim_a, rim_b, index_ref, weight_ref, wsum_ref, state_ref, start_ref,
-        jac_ref, flow_ref, source_ref, step_ref, (s0, s1, s2, s3), out_ref,
+        jac_ref, flow_ref, source_ref, step_ref, (s0, s1), out_ref,
     )
     for t in range(acc_ref.shape[1]):
         lanes = slice(t * LANES, (t + 1) * LANES)
-        for part in range(3):
-            tile = packed_vars(lambda i: out_ref[part * VARS + i, t : t + 1, :])
-            if part == 0:
-                mean_out[:, lanes] = tile
-            else:
-                harm_out[0, part - 1, :, lanes] = tile
-
-
-def packed_vars(row):
-    sub = lax.broadcasted_iota(jnp.int32, (SUBS, LANES), 0)
-    out = spread(row(0))
-    for i in range(1, VARS):
-        out = jnp.where(sub == i, spread(row(i)), out)
-    return out[:VARS]
-
-
-def launch(body, name, out_shape, scalars, args, scratch=()):
+        mean_out[:, lanes] = stacked(lambda i: out_ref[i, t : t + 1, :], VARS)
+    mean_copy = pltpu.make_async_copy(mean_out, mean_hbm, sems.at[0])
+    mean_copy.start()
+    for t in range(acc_ref.shape[1]):
+        lanes = slice(t * LANES, (t + 1) * LANES)
+        for v in range(VARS):
+            harm_out[v, :, lanes] = stacked(lambda i: out_ref[(i + 1) * VARS + v, t : t + 1, :], 2)
+    harm_copy = pltpu.make_async_copy(harm_out, harm_hbm, sems.at[1])
+    harm_copy.start()
+    mean_copy.wait()
+    harm_copy.wait()
+
+
+def stacked(row, count):
+    sub = lax.broadcasted_iota(jnp.int32, (count, LANES), 0)
+    out = jnp.broadcast_to(row(0), (count, LANES))
+    for i in range(1, count):
+        out = jnp.where(sub == i, jnp.broadcast_to(row(i), (count, LANES)), out)
+    return out
+
+
+def held(*arrays):
+    return [*(pltpu.VMEM(a.shape, a.dtype) for a in arrays), pltpu.SemaphoreType.DMA((SUBS,))]
+
+
+def launch(body, name, out_shape, scalars, args, raw=(), scratch=()):
     smem = pl.BlockSpec(memory_space=pltpu.SMEM)
     vmem = pl.BlockSpec(memory_space=pltpu.VMEM)
+    anywhere = pl.BlockSpec(memory_space=pl.ANY)
     return pl.pallas_call(
         body,
         name=name,
         out_shape=out_shape,
-        in_specs=[smem] * len(scalars) + [vmem] * len(args),
-        out_specs=[vmem] * len(out_shape),
+        in_specs=[smem] * len(scalars) + [anywhere] * len(raw) + [vmem] * len(args),
+        out_specs=[anywhere if isinstance(s, jax.ShapeDtypeStruct) else vmem for s in out_shape],
         scratch_shapes=scratch,
-    )(*scalars, *args)
+    )(*scalars, *raw, *(pltpu.with_memory_space_constraint(a, pltpu.VMEM) for a in args))
 
 
 def exchange(pay_a, pay_b, stress):
@@ -248,8 +286,9 @@
     far = [(b, (b - 1 + 2 * (b % 2)) % count) for b in range(count)]
     rim_b = lax.ppermute(pay_b, "cells", far)
     rim_a = lax.ppermute(pay_a, "cells", near)
-    others = [lax.ppermute(stress, HARM, [(k, k ^ m) for k in range(4)]) for m in (1, 2, 3)]
-    return rim_a, rim_b, (stress, *others)
+    swap = [(0, 1), (1, 0)]
+    chip = stress + lax.ppermute(stress, HARM[1], swap)
+    return rim_a, rim_b, (chip, lax.ppermute(chip, HARM[0], swap))
 
 
 def shards(
@@ -268,16 +307,20 @@
     groups = cells // LANES
     halves = groups // SUBS
     rim_rows = face_tiles.shape[1] // LANES
+    harm_adjoint, harm_flow = (
+        a[0].swapaxes(0, 1) for a in (harm_adjoint, harm_flow)
+    )
     odd = (lax.axis_index("cells") % 2).astype(jnp.int32)[None]
     step = pseudo_step.reshape(groups, LANES)
     pays = (struct(ROWS, rim_rows, LANES), struct(ROWS, rim_rows, LANES), struct(VARS, groups, LANES))
     pay_a, pay_b, stress, tile_idx = launch(
-        open_kernel, "open", pays + (struct(2, rim_rows, LANES, dtype=jnp.int32),), (odd,),
+        open_kernel, "open", pays + (struct(2, rim_rows, LANES, dtype=jnp.int32),), (odd,), (),
         (mean_adjoint, harm_adjoint, harm_flow, face_tiles),
+        held(face_tiles, mean_adjoint, harm_adjoint, harm_flow),
     )
     rim_a, rim_b, parts = exchange(pay_a, pay_b, stress)
     fields = struct(ROWS, groups, LANES)
-    acc, index, weight, wsum, start, jac, flow, source = launch(
+    acc, index, weight, wsum, start, jac, flow, source, step = launch(
         prepare_kernel, "prepare",
         (
             fields,
@@ -288,9 +331,12 @@
             struct(VARS * VARS, groups, LANES),
             struct(2 * VARS, groups, LANES),
             struct(VARS, groups, LANES),
+            struct(groups, LANES),
         ),
         (odd,),
-        (mean_adjoint, harm_adjoint, harm_flow, flux_jacobian, face_weight, face_links, mean_source),
+        (),
+        (mean_adjoint, harm_adjoint, harm_flow, flux_jacobian, face_weight, face_links, mean_source, step),
+        held(face_links, face_weight, mean_adjoint, harm_adjoint, harm_flow, mean_source, flux_jacobian),
     )
     state, pay_a, pay_b, stress = launch(
         lambda *refs: middle_kernel(*refs, coeff=1.0 / SECTIONS), "middle", (fields,) + pays, (harm_order,),
@@ -298,13 +344,14 @@
     )
     rim_a, rim_b, parts = exchange(pay_a, pay_b, stress)
     (acc,) = launch(gather_own, "own", (fields,), (), (state, index, weight))
+    outs = [jax.ShapeDtypeStruct(s, F32) for s in ((VARS, cells), (VARS, 2, cells))]
     mean_new, harm_new = launch(
         lambda *refs: close_kernel(*refs, coeff=1.0), "close",
-        (struct(VARS, cells), struct(1, 2, VARS, cells)), (harm_order,),
+        tuple(outs), (harm_order,),
         (acc, rim_a, rim_b, index, weight, wsum, state, start, jac, flow, source, step, *parts),
-        scratch=[pltpu.VMEM((ROWS, groups, LANES), F32)],
-    )
-    return mean_new, harm_new
+        scratch=[fields, *held(*outs)],
+    )
+    return mean_new, harm_new.swapaxes(0, 1)[None]
 
 
 def solution(mesh):

time: 77.8 us -> 59.3 us (0.76)
  starting transfers between devices: 43.7 us -> 37 us
  Pallas kernels: 26.2 us -> 20.4 us
  local copies, waits for them, and re-layouts: 5.78 us -> 0 us
    pallas_call x5, Pallas kernels: 26.2 us -> 20.4 us  [launch(): pl.pallas_call(body, name=name, out_shape=out_shape, in_specs=[smem] * le...]
    ppermute x2, starting transfers between devices: 18.3 us -> 13.6 us  [exchange(): rim_b = lax.ppermute(pay_b, 'cells', far)]
    unnamed x24 -> x0, local copies, waits for them, and re-layouts: 4.18 us -> none
    ppermute x2, starting transfers between devices: 5.92 us -> 3.84 us  [exchange(): rim_a = lax.ppermute(pay_a, 'cells', near)]
    pallas_call x1 -> x0, local copies, waits for them, and re-layouts: 1.6 us -> none  [launch(): pl.pallas_call(body, name=name, out_shape=out_shape, in_specs=[smem] * le...]
    ppermute x6 -> x4, starting transfers between devices: 19.5 us -> 19.5 us  [the longest x2 11.5 us: exchange(): chip = stress + lax.ppermute(stress, HARM[1], swap)]
  transfers between devices with their start and end apart: 10 -> 8, of which waited for: 0 -> 0; matrix products, arithmetic and copies ran while one was open for 0% -> 0% of each run, Pallas kernels for 15% -> 16%
where the time goes in v2:
time: 59.3 us; the launch traced here: 58.9 us
  starting transfers between devices  37 us (62%)
  Pallas kernels  20.4 us (34%)
  between operations  1.46 us (2%)
    pallas_call x5, Pallas kernels, launch(): pl.pallas_call(body, name=name, out_shape=out_shape, in_specs=[smem] * le...  20.4 us
    ppermute x2, starting transfers between devices, exchange(): rim_b = lax.ppermute(pay_b, 'cells', far)  13.6 us
    ppermute x2, starting transfers between devices, exchange(): chip = stress + lax.ppermute(stress, HARM[1], swap)  11.5 us
    ppermute x2, starting transfers between devices, exchange(): return (rim_a, rim_b, (chip, lax.ppermute(chip, HARM[0], swap)))  8 us
    ppermute x2, starting transfers between devices, exchange(): rim_a = lax.ppermute(pay_a, 'cells', near)  3.84 us
  transfers between devices with their start and end apart: 8, of which 0 were waited for; matrix products, arithmetic and copies ran while one was open for 0% of the time, Pallas kernels for 16%

profile of v2, /device:TPU:1, one launch (start us, length us, event | category | flops | bytes accessed | tf_op | source)
XLA Modules:
  0.0 58.9 jit_solution(16992018980243824534)
XLA Ops:
  0.6 1.7 %open.1 = (f32[15,8,128]{2,1,0:T(8,128)S(1)}, f32[15,8,128]{2,1,0:T(8,128)S(1)}, f32[5,16,128]{2,1,0:T(8,128)S(1)}, s32[2,8,128]{2,1,0:T(8,128)S(1)}) custom-call(s32[1]{0:T(128)} %bitcast.odd_ref, f32[5,2048]{1,0:T(8,128)} %mean_hbm.3, f32[5,2,2048]{2,1,0:T(2,128)} %bitcast.11, f32[5,2,2048]{2,1,0:T(2,128)} %bitcast.13, s32[2,1024]{1,0:T(2,128)} %tiles_hbm.1), custom_call_target="tpu_custom_call" | custom-call | tf_op jit(solution)/shard_map/open/pallas_call | solution.py:273
  2.4 8.7 %collective-permute-start.2 = (f32[5,16,128]{2,1,0:T(8,128)S(1)}, f32[5,16,128]{2,1,0:T(8,128)S(1)}, u32[]{:S(2)}, u32[]{:S(2)}) collective-permute-start(f32[5,16,128]{2,1,0:T(8,128)S(1)} %get-tuple-element.33), channel_id=1, source_target_pairs={{0,1},{1,0},{2,3},{3,2},{4,5},{5,4},{6,7},{7,6},{8,9},{9,8},{10,11... | collective-permute-start | bytes 122888 | tf_op jit(solution)/shard_map/ppermute | solution.py:290
  11.1 1.9 %collective-permute-start = (f32[15,8,128]{2,1,0:T(8,128)S(1)}, f32[15,8,128]{2,1,0:T(8,128)S(1)}, u32[]{:S(2)}, u32[]{:S(2)}) collective-permute-start(f32[15,8,128]{2,1,0:T(8,128)S(1)} %get-tuple-element.22), channel_id=1, source_target_pairs={{0,4},{4,0},{8,12},{12,8},{16,20},{20,16},{24,28},{28,24},{32,36},... | collective-permute-start | bytes 184328 | tf_op jit(solution)/shard_map/ppermute | solution.py:288
  13.0 10.2 %collective-permute-start.1 = (f32[15,8,128]{2,1,0:T(8,128)S(1)}, f32[15,8,128]{2,1,0:T(8,128)S(1)}, u32[]{:S(2)}, u32[]{:S(2)}) collective-permute-start(f32[15,8,128]{2,1,0:T(8,128)S(1)} %get-tuple-element.23), channel_id=1, source_target_pairs={{0,508},{4,8},{8,4},{12,16},{16,12},{20,24},{24,20},{28,32},{32,28... | collective-permute-start | bytes 184328 | tf_op jit(solution)/shard_map/ppermute | solution.py:287
  23.3 0.0 collective-permute-done.2
  23.3 4.4 %collective-permute-start.3 = (f32[5,16,128]{2,1,0:T(8,128)S(1)}, f32[5,16,128]{2,1,0:T(8,128)S(1)}, u32[]{:S(2)}, u32[]{:S(2)}) collective-permute-start(f32[5,16,128]{2,1,0:T(8,128)S(1)} %add.11.refs_13_), channel_id=1, source_target_pairs={{0,2},{2,0},{1,3},{3,1},{4,6},{6,4},{5,7},{7,5},{8,10},{10,8},{9,1... | collective-permute-start | bytes 122888 | tf_op jit(solution)/shard_map/ppermute | solution.py:291
  28.3 5.2 %prepare.1 = (f32[15,16,128]{2,1,0:T(8,128)S(1)}, s32[12,8,128]{2,1,0:T(8,128)S(1)}, f32[12,8,128]{2,1,0:T(8,128)S(1)}, f32[16,128]{1,0:T(8,128)S(1)}, f32[15,16...) custom-call(s32[1]{0:T(128)} %bitcast.odd_ref, ...), custom_call_target="tpu_custom_call" | custom-call | tf_op jit(solution)/shard_map/prepare/pallas_call | solution.py:273
  33.5 0.0 collective-permute-done.refs_2_
  33.5 0.0 collective-permute-done.1.refs_3_
  33.5 0.0 collective-permute-done.3.refs_14_
  33.5 4.7 %middle.1 = (f32[15,16,128]{2,1,0:T(8,128)S(1)}, f32[15,8,128]{2,1,0:T(8,128)S(1)}, f32[15,8,128]{2,1,0:T(8,128)S(1)}, f32[5,16,128]{2,1,0:T(8,128)S(1)}) custom-call(s32[1]{0:T(128)S(6)} %copy.12.refs_0_, f32[15,16,128]{2,1,0:T(8,128)S(1)} %get-tuple-element.21.refs_1_, f32[15,8,128]{2,1,0:T(8,128)S(1)} %collective-permute-done.refs_2_, ...), custom_call_target="tpu_custom_call" | custom-call | tf_op jit(solution)/shard_map/middle/pallas_call | solution.py:273
  38.2 2.8 %collective-permute-start.6 = (f32[5,16,128]{2,1,0:T(8,128)S(1)}, f32[5,16,128]{2,1,0:T(8,128)S(1)}, u32[]{:S(2)}, u32[]{:S(2)}) collective-permute-start(f32[5,16,128]{2,1,0:T(8,128)S(1)} %get-tuple-element.37), channel_id=1, source_target_pairs={{0,1},{1,0},{2,3},{3,2},{4,5},{5,4},{6,7},{7,6},{8,9},{9,8},{10,11... | collective-permute-start | bytes 122888 | tf_op jit(solution)/shard_map/ppermute | solution.py:290
  41.0 1.9 %collective-permute-start.4 = (f32[15,8,128]{2,1,0:T(8,128)S(1)}, f32[15,8,128]{2,1,0:T(8,128)S(1)}, u32[]{:S(2)}, u32[]{:S(2)}) collective-permute-start(f32[15,8,128]{2,1,0:T(8,128)S(1)} %get-tuple-element.35), channel_id=1, source_target_pairs={{0,4},{4,0},{8,12},{12,8},{16,20},{20,16},{24,28},{28,24},{32,36},... | collective-permute-start | bytes 184328 | tf_op jit(solution)/shard_map/ppermute | solution.py:288
  42.9 3.4 %collective-permute-start.5 = (f32[15,8,128]{2,1,0:T(8,128)S(1)}, f32[15,8,128]{2,1,0:T(8,128)S(1)}, u32[]{:S(2)}, u32[]{:S(2)}) collective-permute-start(f32[15,8,128]{2,1,0:T(8,128)S(1)} %get-tuple-element.36), channel_id=1, source_target_pairs={{0,508},{4,8},{8,4},{12,16},{16,12},{20,24},{24,20},{28,32},{32,28... | collective-permute-start | bytes 184328 | tf_op jit(solution)/shard_map/ppermute | solution.py:287
  46.3 0.0 collective-permute-done.6
  46.4 3.6 %collective-permute-start.7 = (f32[5,16,128]{2,1,0:T(8,128)S(1)}, f32[5,16,128]{2,1,0:T(8,128)S(1)}, u32[]{:S(2)}, u32[]{:S(2)}) collective-permute-start(f32[5,16,128]{2,1,0:T(8,128)S(1)} %add.12.refs_13_), channel_id=1, source_target_pairs={{0,2},{2,0},{1,3},{3,1},{4,6},{6,4},{5,7},{7,5},{8,10},{10,8},{9,1... | collective-permute-start | bytes 122888 | tf_op jit(solution)/shard_map/ppermute | solution.py:291
  50.0 4.0 %own.1.refs_1_ = f32[15,16,128]{2,1,0:T(8,128)S(1)} custom-call(f32[15,16,128]{2,1,0:T(8,128)S(1)} %get-tuple-element.34.state_ref.refs_7_, s32[12,8,128]{2,1,0:T(8,128)S(1)} %get-tuple-element.24.refs_4_.index_ref, f32[12,8,128]{2,1,0:T(8,128)S(1)} %get-tuple-element.25.refs_5_.weight_ref), custom_call_target="tpu_custom_call" | custom-call | tf_op jit(solution)/shard_map/own/pallas_call | solution.py:273
  54.0 0.0 collective-permute-done.4.refs_2_
  54.1 0.0 collective-permute-done.5.refs_3_
  54.1 0.0 collective-permute-done.7.refs_14_
  54.1 4.8 %close.1 = (f32[5,2048]{1,0:T(8,128)}, f32[5,2,2048]{2,1,0:T(2,128)}) custom-call(s32[1]{0:T(128)S(6)} %copy.12.refs_0_, f32[15,16,128]{2,1,0:T(8,128)S(1)} %own.1.refs_1_, f32[15,8,128]{2,1,0:T(8,128)S(1)} %collective-permute-done.4.refs_2_, f32[15,8,128]{2,1,0:T(8,128)S(1)} %collective-permute-done.5.refs_3_, ...), custom_call_target="tpu_custom_call" | custom-call | tf_op jit(solution)/shard_map/close/pallas_call | solution.py:273
  (2 shorter events, 0.0 us)
Async XLA Ops:
  2.4 20.9 %collective-permute-start.2 = (f32[5,16,128]{2,1,0:T(8,128)S(1)}, f32[5,16,128]{2,1,0:T(8,128)S(1)}, u32[]{:S(2)}, u32[]{:S(2)}) collective-permute-start(f32[5,16,128]{2,1,0:T(8,128)S(1)} %get-tuple-element.33), channel_id=1, source_target_pairs={{0,1},{1,0},{2,3},{3,2},{4,5},{5,4},{6,7},{7,6},{8,9},{9,8},{10,11... | collective-permute-start | bytes 122888 | tf_op jit(solution)/shard_map/ppermute | solution.py:290
  11.1 22.4 %collective-permute-start = (f32[15,8,128]{2,1,0:T(8,128)S(1)}, f32[15,8,128]{2,1,0:T(8,128)S(1)}, u32[]{:S(2)}, u32[]{:S(2)}) collective-permute-start(f32[15,8,128]{2,1,0:T(8,128)S(1)} %get-tuple-element.22), channel_id=1, source_target_pairs={{0,4},{4,0},{8,12},{12,8},{16,20},{20,16},{24,28},{28,24},{32,36},... | collective-permute-start | bytes 184328 | tf_op jit(solution)/shard_map/ppermute | solution.py:288
  13.0 20.5 %collective-permute-start.1 = (f32[15,8,128]{2,1,0:T(8,128)S(1)}, f32[15,8,128]{2,1,0:T(8,128)S(1)}, u32[]{:S(2)}, u32[]{:S(2)}) collective-permute-start(f32[15,8,128]{2,1,0:T(8,128)S(1)} %get-tuple-element.23), channel_id=1, source_target_pairs={{0,508},{4,8},{8,4},{12,16},{16,12},{20,24},{24,20},{28,32},{32,28... | collective-permute-start | bytes 184328 | tf_op jit(solution)/shard_map/ppermute | solution.py:287
  23.3 10.2 %collective-permute-start.3 = (f32[5,16,128]{2,1,0:T(8,128)S(1)}, f32[5,16,128]{2,1,0:T(8,128)S(1)}, u32[]{:S(2)}, u32[]{:S(2)}) collective-permute-start(f32[5,16,128]{2,1,0:T(8,128)S(1)} %add.11.refs_13_), channel_id=1, source_target_pairs={{0,2},{2,0},{1,3},{3,1},{4,6},{6,4},{5,7},{7,5},{8,10},{10,8},{9,1... | collective-permute-start | bytes 122888 | tf_op jit(solution)/shard_map/ppermute | solution.py:291
  38.2 8.1 %collective-permute-start.6 = (f32[5,16,128]{2,1,0:T(8,128)S(1)}, f32[5,16,128]{2,1,0:T(8,128)S(1)}, u32[]{:S(2)}, u32[]{:S(2)}) collective-permute-start(f32[5,16,128]{2,1,0:T(8,128)S(1)} %get-tuple-element.37), channel_id=1, source_target_pairs={{0,1},{1,0},{2,3},{3,2},{4,5},{5,4},{6,7},{7,6},{8,9},{9,8},{10,11... | collective-permute-start | bytes 122888 | tf_op jit(solution)/shard_map/ppermute | solution.py:290
  41.0 13.1 %collective-permute-start.4 = (f32[15,8,128]{2,1,0:T(8,128)S(1)}, f32[15,8,128]{2,1,0:T(8,128)S(1)}, u32[]{:S(2)}, u32[]{:S(2)}) collective-permute-start(f32[15,8,128]{2,1,0:T(8,128)S(1)} %get-tuple-element.35), channel_id=1, source_target_pairs={{0,4},{4,0},{8,12},{12,8},{16,20},{20,16},{24,28},{28,24},{32,36},... | collective-permute-start | bytes 184328 | tf_op jit(solution)/shard_map/ppermute | solution.py:288
  42.9 11.2 %collective-permute-start.5 = (f32[15,8,128]{2,1,0:T(8,128)S(1)}, f32[15,8,128]{2,1,0:T(8,128)S(1)}, u32[]{:S(2)}, u32[]{:S(2)}) collective-permute-start(f32[15,8,128]{2,1,0:T(8,128)S(1)} %get-tuple-element.36), channel_id=1, source_target_pairs={{0,508},{4,8},{8,4},{12,16},{16,12},{20,24},{24,20},{28,32},{32,28... | collective-permute-start | bytes 184328 | tf_op jit(solution)/shard_map/ppermute | solution.py:287
  46.4 7.7 %collective-permute-start.7 = (f32[5,16,128]{2,1,0:T(8,128)S(1)}, f32[5,16,128]{2,1,0:T(8,128)S(1)}, u32[]{:S(2)}, u32[]{:S(2)}) collective-permute-start(f32[5,16,128]{2,1,0:T(8,128)S(1)} %add.12.refs_13_), channel_id=1, source_target_pairs={{0,2},{2,0},{1,3},{3,1},{4,6},{6,4},{5,7},{7,5},{8,10},{10,8},{9,1... | collective-permute-start | bytes 122888 | tf_op jit(solution)/shard_map/ppermute | solution.py:291

commit v3 on v2

v3 whole, which is shorter than its diff:
```python
import jax
import jax.numpy as jnp
from jax import lax
from jax.experimental import pallas as pl
from jax.experimental.pallas import tpu as pltpu
from jax.sharding import Mesh
from jax.sharding import PartitionSpec as P

VARS = 5
FACES = 6
SECTIONS = 2
ROWS = 3 * VARS
HARM = ("harm_0", "harm_1")
HARM_DEVICES = 4
LANES = 128
SUBS = 8
BASE_FREQ = 0.8
F32 = jnp.float32


def struct(*shape, dtype=F32):
    return pltpu.VMEM(shape, dtype)


def spread(row):
    return jnp.broadcast_to(row, (SUBS, LANES))


def packed(tile, first):
    sub = lax.broadcasted_iota(jnp.int32, (SUBS, LANES), 0)
    out = spread(tile(first))
    for i in range(1, SUBS):
        out = jnp.where(sub == i, spread(tile(first + i)), out)
    return out


def picked(row, fields, count, index):
    low = index & (LANES - 1)
    high = index >> 7
    out = [None] * len(fields)
    for h in range(count):
        hit = high == h
        for i, r in enumerate(fields):
            value = jnp.take_along_axis(spread(row(r, h)), low, axis=1)
            out[i] = jnp.where(hit, value, 0.0 if h == 0 else out[i])
    return out


def store_tiles(row, tile_index, pay_a, pay_b, rows):
    for pay, index in zip((pay_a, pay_b), tile_index):
        for r, value in enumerate(picked(row, range(ROWS), rows, index)):
            pay[r] = value


def native_row(mean_ref, harm_ref):
    def row(r, h):
        lanes = slice(h * LANES, (h + 1) * LANES)
        if r < VARS:
            return mean_ref[r : r + 1, lanes]
        part, var = divmod(r - VARS, VARS)
        return harm_ref[var, part : part + 1, lanes]

    return row


def fetch(sources, targets, sems):
    copies = [pltpu.make_async_copy(s, t, sems.at[i]) for i, (s, t) in enumerate(zip(sources, targets))]
    for copy in copies:
        copy.start()
    return [copy.wait for copy in copies]


def open_kernel(
    place_ref, mean_hbm, harm_hbm, tiles_hbm, pay_a, pay_b, tile_idx, tiles_ref, mean_ref, harm_ref, sems
):
    for wait in fetch((tiles_hbm, mean_hbm, harm_hbm), (tiles_ref, mean_ref, harm_ref), sems):
        wait()
    lowers_first = place_ref[0] % 2 == 1
    lower, upper = (
        packed(lambda t, k=k: tiles_ref[k : k + 1, t * LANES : (t + 1) * LANES], 0) for k in range(2)
    )
    first = jnp.where(lowers_first, lower, upper)
    second = jnp.where(lowers_first, upper, lower)
    tile_idx[0] = first
    tile_idx[1] = second
    row = native_row(mean_ref, harm_ref)
    store_tiles(row, (first, second), pay_a, pay_b, mean_ref.shape[1] // LANES)


def gather_into(row, fields, count, first, index_ref, weight_ref, begin, faces, start):
    def face(f, acc):
        values = picked(row, fields, count, index_ref[begin + f] - first)
        weight = weight_ref[begin + f]
        return tuple(a + weight * v for a, v in zip(acc, values))

    return lax.fori_loop(0, faces, face, tuple(start))


def share_of(place_ref, index_ref):
    count = index_ref.shape[0] // HARM_DEVICES
    begin = place_ref[0] // 2 * count
    return begin, count, begin // FACES


def gather_fields(row, fields, count, first, index_ref, weight_ref, start, out_ref):
    for g in range(index_ref.shape[0] // FACES):
        at = slice(g * SUBS, (g + 1) * SUBS)
        values = gather_into(
            row, fields, count, first, index_ref, weight_ref, g * FACES, FACES, [start(r, at) for r in fields]
        )
        for r, value in zip(fields, values):
            out_ref[r, at, :] = value


def zero_start(*_):
    return jnp.zeros((SUBS, LANES), F32)


def prepare_kernel(
    place_ref, mean_hbm, harm_hbm, flow_hbm, jac_hbm, weight_hbm, links_hbm, source_hbm, step_hbm,
    acc_ref, share_ref, index_ref, weight_ref, wsum_ref, mean_out, state_ref, jac_out, flow_out, source_out, step_out,
    links_ref, weight_in, mean_ref, harm_ref, flow_ref, source_ref, jac_ref, sems,
):
    waits = fetch(
        (links_hbm, weight_hbm, mean_hbm, harm_hbm, flow_hbm, source_hbm, jac_hbm, step_hbm),
        (links_ref, weight_in, mean_ref, harm_ref, flow_ref, source_ref, jac_ref, step_out),
        sems,
    )
    for wait in waits[:2]:
        wait()
    groups = mean_ref.shape[1] // LANES
    flips = place_ref[0] % 2 == 0
    rim = groups * LANES
    lane = lambda t: slice(t * LANES, (t + 1) * LANES)
    for g in range(groups // SUBS):
        total = None
        for f in range(FACES):
            link = packed(lambda t: links_ref[f : f + 1, lane(t)], g * SUBS)
            flipped = jnp.where(link >= rim, link ^ (rim // 2), link)
            index_ref[g * FACES + f] = jnp.where(flips, flipped, link)
            weight = packed(lambda t: weight_in[f : f + 1, lane(t)], g * SUBS)
            weight_ref[g * FACES + f] = weight
            total = weight if total is None else total + weight
        wsum_ref[g * SUBS : (g + 1) * SUBS, :] = total
    row = native_row(mean_ref, harm_ref)
    flow = native_row(mean_ref, flow_ref)
    for wait in waits[2:4]:
        wait()
    for g in range(0, groups, SUBS):
        at = slice(g, g + SUBS)
        for r in range(VARS):
            mean_out[r, at, :] = packed(lambda t: row(r, t), g)
        for r in range(2 * VARS):
            state_ref[r, at, :] = packed(lambda t: row(VARS + r, t), g)
    gather_fields(
        lambda r, h: state_ref[r, h : h + 1, :], range(2 * VARS), groups, 0, index_ref, weight_ref,
        zero_start, acc_ref,
    )
    begin, count, _ = share_of(place_ref, index_ref)
    values = gather_into(
        lambda r, h: mean_out[r, h : h + 1, :], range(VARS), groups, 0, index_ref, weight_ref,
        begin, count, [zero_start()] * VARS,
    )
    for r, value in enumerate(values):
        share_ref[r] = value
    for wait in waits[4:]:
        wait()
    for g in range(0, groups, SUBS):
        at = slice(g, g + SUBS)
        for r in range(2 * VARS):
            flow_out[r, at, :] = packed(lambda t: flow(VARS + r, t), g)
        for v in range(VARS):
            source_out[v, at, :] = packed(lambda t: source_ref[v : v + 1, lane(t)], g)
        for j in range(VARS):
            for i in range(VARS):
                jac_out[j * VARS + i, at, :] = packed(lambda t: jac_ref[j, i : i + 1, lane(t)], g)


def fields_row(mean_ref, harm_ref):
    def row(r, h):
        return mean_ref[r, h : h + 1, :] if r < VARS else harm_ref[r - VARS, h : h + 1, :]

    return row


def own_kernel(mean_ref, harm_ref, index_ref, weight_ref, acc_ref):
    gather_fields(
        fields_row(mean_ref, harm_ref), range(ROWS), mean_ref.shape[1], 0, index_ref, weight_ref,
        zero_start, acc_ref,
    )


def rim_row(rim_a, rim_b, lead=0):
    rows = rim_a.shape[1]

    def row(r, h):
        ref = rim_a if h < rows else rim_b
        h = h % rows
        return ref[lead + r, h : h + 1, :]

    return row


def transposed(jac_ref, at, flux):
    out = []
    for i in range(VARS):
        res = jac_ref[i, at, :] * flux[0]
        for j in range(1, VARS):
            res = res + jac_ref[j * VARS + i, at, :] * flux[j]
        out.append(res)
    return out


def harm_step(order_ref, at, mean, state, start, gathered, wsum, scale, jac_ref, flow_ref, out_ref):
    omega = BASE_FREQ * (order_ref[0].astype(F32) + 1.0)
    flux = [wsum * s - x for s, x in zip(state, gathered)]
    for part in range(2):
        res = transposed(jac_ref, at, flux[part * VARS : (part + 1) * VARS])
        for i in range(VARS):
            r = part * VARS + i
            turned = omega * state[(1 - part) * VARS + i]
            full = res[i] + turned if part == 0 else res[i] - turned
            full = full - mean[i] * flow_ref[r, at, :]
            out_ref[r, at, :] = start[r] - scale * full


def middle_kernel(
    place_ref, order_ref, acc_ref, share_ref, rim_a, rim_b, index_ref, weight_ref, wsum_ref, mean_ref, state_ref,
    jac_ref, flow_ref, source_ref, step_ref, out_ref, part_ref, full_ref, mean_acc, *, coeff,
):
    groups = acc_ref.shape[1]
    rim_rows = rim_a.shape[1]
    begin, count, half = share_of(place_ref, index_ref)
    lead = place_ref[0] // 2 == 0
    gather_fields(
        rim_row(rim_a, rim_b, VARS), range(2 * VARS), 2 * rim_rows, groups * LANES, index_ref, weight_ref,
        lambda r, at: acc_ref[r, at, :], full_ref,
    )
    values = gather_into(
        rim_row(rim_a, rim_b), range(VARS), 2 * rim_rows, groups * LANES, index_ref, weight_ref,
        begin, count, [share_ref[r] for r in range(VARS)],
    )
    mean_acc[...] = jnp.zeros(mean_acc.shape, F32)
    for r, value in enumerate(values):
        mean_acc[r, pl.ds(pl.multiple_of(half * SUBS, SUBS), SUBS), :] = value
    for g in range(groups // SUBS):
        at = slice(g * SUBS, (g + 1) * SUBS)
        mean = [mean_ref[v, at, :] for v in range(VARS)]
        state = [state_ref[r, at, :] for r in range(2 * VARS)]
        wsum = wsum_ref[at, :]
        scale = coeff * step_ref[at, :]
        flux = []
        for v in range(VARS):
            stress = state[v] * flow_ref[v, at, :] + state[VARS + v] * flow_ref[VARS + v, at, :]
            flux.append(jnp.where(lead, wsum * mean[v], 0.0) - mean_acc[v, at, :] - stress)
        for v, res in enumerate(transposed(jac_ref, at, flux)):
            own = jnp.where(lead, mean[v] + scale * source_ref[v, at, :], 0.0)
            part_ref[v, at, :] = own - scale * res
        gathered = [full_ref[r, at, :] for r in range(2 * VARS)]
        harm_step(order_ref, at, mean, state, state, gathered, wsum, scale, jac_ref, flow_ref, out_ref)
        for v in range(VARS):
            part_ref[VARS + v, at, :] = (
                out_ref[v, at, :] * flow_ref[v, at, :] + out_ref[VARS + v, at, :] * flow_ref[VARS + v, at, :]
            )


def join_kernel(parts_ref, state_ref, tile_idx, mean_ref, stress_ref, pay_a, pay_b):
    for v in range(VARS):
        for ref, r in ((mean_ref, v), (stress_ref, VARS + v)):
            total = parts_ref[0, r]
            for k in range(1, HARM_DEVICES):
                total = total + parts_ref[k, r]
            ref[v] = total
    row = fields_row(mean_ref, state_ref)
    store_tiles(row, (tile_idx[0], tile_idx[1]), pay_a, pay_b, mean_ref.shape[1])


def close_kernel(
    order_ref, acc_ref, rim_a, rim_b, index_ref, weight_ref, wsum_ref, mean_ref, state_ref, mean_start, harm_start,
    jac_ref, flow_ref, source_ref, step_ref, stress_ref,
    mean_hbm, harm_hbm, full_ref, new_mean, new_harm, mean_out, harm_out, sems, *, coeff,
):
    groups = acc_ref.shape[1]
    gather_fields(
        rim_row(rim_a, rim_b), range(ROWS), 2 * rim_a.shape[1], groups * LANES, index_ref, weight_ref,
        lambda r, at: acc_ref[r, at, :], full_ref,
    )
    for g in range(groups // SUBS):
        at = slice(g * SUBS, (g + 1) * SUBS)
        mean = [mean_ref[v, at, :] for v in range(VARS)]
        state = [state_ref[r, at, :] for r in range(2 * VARS)]
        wsum = wsum_ref[at, :]
        scale = coeff * step_ref[at, :]
        flux = [wsum * m - full_ref[v, at, :] - stress_ref[v, at, :] for v, m in enumerate(mean)]
        for v, res in enumerate(transposed(jac_ref, at, flux)):
            new_mean[v, at, :] = mean_start[v, at, :] - scale * (res - source_ref[v, at, :])
        gathered = [full_ref[VARS + r, at, :] for r in range(2 * VARS)]
        start = [harm_start[r, at, :] for r in range(2 * VARS)]
        harm_step(order_ref, at, mean, state, start, gathered, wsum, scale, jac_ref, flow_ref, new_harm)
    for t in range(groups):
        lanes = slice(t * LANES, (t + 1) * LANES)
        mean_out[:, lanes] = stacked(lambda i: new_mean[i, t : t + 1, :], VARS)
    mean_copy = pltpu.make_async_copy(mean_out, mean_hbm, sems.at[0])
    mean_copy.start()
    for t in range(groups):
        lanes = slice(t * LANES, (t + 1) * LANES)
        for v in range(VARS):
            harm_out[v, :, lanes] = stacked(lambda i: new_harm[i * VARS + v, t : t + 1, :], 2)
    harm_copy = pltpu.make_async_copy(harm_out, harm_hbm, sems.at[1])
    harm_copy.start()
    mean_copy.wait()
    harm_copy.wait()


def stacked(row, count):
    sub = lax.broadcasted_iota(jnp.int32, (count, LANES), 0)
    out = jnp.broadcast_to(row(0), (count, LANES))
    for i in range(1, count):
        out = jnp.where(sub == i, jnp.broadcast_to(row(i), (count, LANES)), out)
    return out


def held(*arrays):
    return [*(pltpu.VMEM(a.shape, a.dtype) for a in arrays), pltpu.SemaphoreType.DMA((SUBS,))]


def launch(body, name, out_shape, scalars, args, raw=(), scratch=()):
    smem = pl.BlockSpec(memory_space=pltpu.SMEM)
    vmem = pl.BlockSpec(memory_space=pltpu.VMEM)
    anywhere = pl.BlockSpec(memory_space=pl.ANY)
    return pl.pallas_call(
        body,
        name=name,
        out_shape=out_shape,
        in_specs=[smem] * len(scalars) + [anywhere] * len(raw) + [vmem] * len(args),
        out_specs=[anywhere if isinstance(s, jax.ShapeDtypeStruct) else vmem for s in out_shape],
        scratch_shapes=scratch,
    )(*scalars, *raw, *(pltpu.with_memory_space_constraint(a, pltpu.VMEM) for a in args))


def exchange(pay_a, pay_b):
    count = lax.axis_size("cells")
    near = [(b, b ^ 1) for b in range(count)]
    far = [(b, (b - 1 + 2 * (b % 2)) % count) for b in range(count)]
    return lax.ppermute(pay_a, "cells", far), lax.ppermute(pay_b, "cells", near)


def shards(
    mean_adjoint,
    harm_adjoint,
    harm_flow,
    flux_jacobian,
    face_weight,
    face_links,
    face_tiles,
    pseudo_step,
    mean_source,
    harm_order,
):
    cells = mean_adjoint.shape[1]
    groups = cells // LANES
    halves = groups // SUBS
    rim_rows = face_tiles.shape[1] // LANES
    harm_adjoint, harm_flow = (
        a[0].swapaxes(0, 1) for a in (harm_adjoint, harm_flow)
    )
    place = (1 - lax.axis_index("cells") % 2 + 2 * lax.axis_index(HARM)).astype(jnp.int32)[None]
    step = pseudo_step.reshape(groups, LANES)
    mean_fields, harm_fields = struct(VARS, groups, LANES), struct(2 * VARS, groups, LANES)
    pays = (struct(ROWS, rim_rows, LANES), struct(ROWS, rim_rows, LANES))
    pay_a, pay_b, tile_idx = launch(
        open_kernel, "open", pays + (struct(2, rim_rows, LANES, dtype=jnp.int32),), (place,), (),
        (mean_adjoint, harm_adjoint, face_tiles),
        held(face_tiles, mean_adjoint, harm_adjoint),
    )
    rim_a, rim_b = exchange(pay_a, pay_b)
    registers = FACES * halves
    acc, share, index, weight, wsum, mean_start, harm_start, jac, flow, source, step = launch(
        prepare_kernel, "prepare",
        (
            harm_fields,
            struct(VARS, SUBS, LANES),
            struct(registers, SUBS, LANES, dtype=jnp.int32),
            struct(registers, SUBS, LANES),
            struct(groups, LANES),
            mean_fields,
            harm_fields,
            struct(VARS * VARS, groups, LANES),
            harm_fields,
            mean_fields,
            struct(groups, LANES),
        ),
        (place,),
        (),
        (mean_adjoint, harm_adjoint, harm_flow, flux_jacobian, face_weight, face_links, mean_source, step),
        held(face_links, face_weight, mean_adjoint, harm_adjoint, harm_flow, mean_source, flux_jacobian),
    )
    state, part = launch(
        lambda *refs: middle_kernel(*refs, coeff=1.0 / SECTIONS), "middle", (harm_fields, harm_fields),
        (place, harm_order),
        (acc, share, rim_a, rim_b, index, weight, wsum, mean_start, harm_start, jac, flow, source, step),
        scratch=[harm_fields, mean_fields],
    )
    parts = lax.all_gather(part, HARM)
    mean, stress, pay_a, pay_b = launch(
        join_kernel, "join", (mean_fields, mean_fields) + pays, (), (parts, state, tile_idx)
    )
    rim_a, rim_b = exchange(pay_a, pay_b)
    fields = struct(ROWS, groups, LANES)
    (acc,) = launch(own_kernel, "own", (fields,), (), (mean, state, index, weight))
    outs = [jax.ShapeDtypeStruct(s, F32) for s in ((VARS, cells), (VARS, 2, cells))]
    mean_new, harm_new = launch(
        lambda *refs: close_kernel(*refs, coeff=1.0), "close", tuple(outs), (harm_order,),
        (acc, rim_a, rim_b, index, weight, wsum, mean, state, mean_start, harm_start,
         jac, flow, source, step, stress),
        scratch=[fields, mean_fields, harm_fields, *held(*outs)],
    )
    return mean_new, harm_new.swapaxes(0, 1)[None]


def solution(mesh):
    finer = Mesh(mesh.devices.reshape(mesh.shape["cells"], 2, 2), ("cells", *HARM))
    return jax.shard_map(
        shards,
        mesh=finer,
        in_specs=(
            P(None, "cells"),
            P(HARM, None, None, "cells"),
            P(HARM, None, None, "cells"),
            P(None, None, "cells"),
            P(None, "cells"),
            P(None, "cells"),
            P(None, "cells"),
            P("cells"),
            P(None, "cells"),
            P(HARM),
        ),
        out_specs=(P(None, "cells"), P(HARM, None, None, "cells")),
        check_vma=False,
    )
```

time: 59.3 us -> 52.6 us (0.89)
  starting transfers between devices: 37 us -> 23.5 us
  blocking collectives: 0 us -> 8.26 us
  Pallas kernels: 20.4 us -> 19.2 us
    ppermute x8 -> x4, starting transfers between devices: 37 us -> 23.5 us  [the longest x2 19.6 us: exchange(): lax.ppermute(pay_a, 'cells', far)]
    all_gather x0 -> x1, blocking collectives: none -> 8.26 us  [shards(): parts = lax.all_gather(part, HARM)]
    pallas_call x5 -> x6, Pallas kernels: 20.4 us -> 19.2 us  [launch(): pl.pallas_call(body, name=name, out_shape=out_shape, in_specs=[smem] * le...]
  transfers between devices with their start and end apart: 8 -> 4, of which waited for: 0 -> 0; matrix products, arithmetic and copies ran while one was open for 0% -> 0% of each run, Pallas kernels for 16% -> 17%
where the time goes in v3:
time: 52.6 us; the launch traced here: 52.3 us
  starting transfers between devices  23.5 us (45%)
  Pallas kernels  19.2 us (37%)
  blocking collectives  8.26 us (16%)
  between operations  1.39 us (3%)
    ppermute x2, starting transfers between devices, exchange(): lax.ppermute(pay_a, 'cells', far)  19.6 us
    pallas_call x6, Pallas kernels, launch(): pl.pallas_call(body, name=name, out_shape=out_shape, in_specs=[smem] * le...  19.2 us
    all_gather x1, blocking collectives, shards(): parts = lax.all_gather(part, HARM)  8.26 us
    ppermute x2, starting transfers between devices, exchange(): lax.ppermute(pay_b, 'cells', near)  3.84 us
  transfers between devices with their start and end apart: 4, of which 0 were waited for; matrix products, arithmetic and copies ran while one was open for 0% of the time, Pallas kernels for 17%

profile of v3, /device:TPU:1, one launch (start us, length us, event | category | flops | bytes accessed | tf_op | source)
XLA Modules:
  0.0 52.3 jit_solution(12034580789184353363)
XLA Ops:
  0.6 1.6 %open.1 = (f32[15,8,128]{2,1,0:T(8,128)S(1)}, f32[15,8,128]{2,1,0:T(8,128)S(1)}, s32[2,8,128]{2,1,0:T(8,128)S(1)}) custom-call(s32[1]{0:T(128)} %bitcast.place_ref.refs_0_, f32[5,2048]{1,0:T(8,128)} %mean_hbm.3, f32[5,2,2048]{2,1,0:T(2,128)} %bitcast.13, s32[2,1024]{1,0:T(2,128)} %tiles_hbm.1), custom_call_target="tpu_custom_call" | custom-call | tf_op jit(solution)/shard_map/open/pallas_call | solution.py:331
  2.3 15.3 %collective-permute-start = (f32[15,8,128]{2,1,0:T(8,128)S(1)}, f32[15,8,128]{2,1,0:T(8,128)S(1)}, u32[]{:S(2)}, u32[]{:S(2)}) collective-permute-start(f32[15,8,128]{2,1,0:T(8,128)S(1)} %get-tuple-element.26), channel_id=1, source_target_pairs={{0,508},{4,8},{8,4},{12,16},{16,12},{20,24},{24,20},{28,32},{32,28... | collective-permute-start | bytes 184328 | tf_op jit(solution)/shard_map/ppermute | solution.py:345
  17.6 1.9 %collective-permute-start.1 = (f32[15,8,128]{2,1,0:T(8,128)S(1)}, f32[15,8,128]{2,1,0:T(8,128)S(1)}, u32[]{:S(2)}, u32[]{:S(2)}) collective-permute-start(f32[15,8,128]{2,1,0:T(8,128)S(1)} %get-tuple-element.27), channel_id=1, source_target_pairs={{0,4},{4,0},{8,12},{12,8},{16,20},{20,16},{24,28},{28,24},{32,36},... | collective-permute-start | bytes 184328 | tf_op jit(solution)/shard_map/ppermute | solution.py:345
  20.2 4.7 %prepare.1 = (f32[10,16,128]{2,1,0:T(8,128)S(1)}, f32[5,8,128]{2,1,0:T(8,128)S(1)}, s32[12,8,128]{2,1,0:T(8,128)S(1)}, f32[12,8,128]{2,1,0:T(8,128)S(1)}, f32[16...) custom-call(s32[1]{0:T(128)} %bitcast.place_ref.refs_0_, ...), custom_call_target="tpu_custom_call" | custom-call | tf_op jit(solution)/shard_map/prepare/pallas_call | solution.py:331
  24.8 0.0 collective-permute-done.refs_4_
  24.8 0.0 collective-permute-done.1.refs_5_
  24.8 3.5 %middle.1 = (f32[10,16,128]{2,1,0:T(8,128)S(1)}, f32[10,16,128]{2,1,0:T(8,128)S(1)}) custom-call(s32[1]{0:T(128)} %bitcast.place_ref.refs_0_, s32[1]{0:T(128)S(6)} %copy.12.refs_1_.refs_0_, f32[10,16,128]{2,1,0:T(8,128)S(1)} %get-tuple-element.24.refs_2_, f32[5,8,128]{2,1,0:T(8,128)S(1)} %get-tuple-element.25.refs_3_, ...), custom_call_target="tpu_custom_call" | custom-call | tf_op jit(solution)/shard_map/middle/pallas_call | solution.py:331
  28.4 8.3 %all-gather = f32[40,16,128]{2,1,0:T(8,128)S(1)} all-gather(f32[10,16,128]{2,1,0:T(8,128)S(1)} %get-tuple-element.37), channel_id=2, replica_groups=mesh['cells'=128,'harm_0'=2,'harm_1'=2] {'harm_0','harm_1'}, dimensions={0}, use_global_device_ids=true | all-gather | bytes 409600 | tf_op jit(solution)/shard_map/all_gather | solution.py:404
  36.6 0.6 %join.1 = (f32[5,16,128]{2,1,0:T(8,128)S(1)}, f32[5,16,128]{2,1,0:T(8,128)S(1)}, f32[15,8,128]{2,1,0:T(8,128)S(1)}, f32[15,8,128]{2,1,0:T(8,128)S(1)}) custom-call(f32[4,10,16,128]{3,2,1,0:T(8,128)S(1)} %bitcast.12, f32[10,16,128]{2,1,0:T(8,128)S(1)} %get-tuple-element.38.state_ref.harm_ref.refs_8_, s32[2,8,128]{2,1,0:T(8,128)S(1)} %get-tuple-element.39.tile_idx), custom_call_target="tpu_custom_call" | custom-call | tf_op jit(solution)/shard_map/join/pallas_call | solution.py:331
  37.2 4.3 %collective-permute-start.2 = (f32[15,8,128]{2,1,0:T(8,128)S(1)}, f32[15,8,128]{2,1,0:T(8,128)S(1)}, u32[]{:S(2)}, u32[]{:S(2)}) collective-permute-start(f32[15,8,128]{2,1,0:T(8,128)S(1)} %get-tuple-element.41), channel_id=1, source_target_pairs={{0,508},{4,8},{8,4},{12,16},{16,12},{20,24},{24,20},{28,32},{32,28... | collective-permute-start | bytes 184328 | tf_op jit(solution)/shard_map/ppermute | solution.py:345
  41.6 1.9 %collective-permute-start.3 = (f32[15,8,128]{2,1,0:T(8,128)S(1)}, f32[15,8,128]{2,1,0:T(8,128)S(1)}, u32[]{:S(2)}, u32[]{:S(2)}) collective-permute-start(f32[15,8,128]{2,1,0:T(8,128)S(1)} %get-tuple-element.42), channel_id=1, source_target_pairs={{0,4},{4,0},{8,12},{12,8},{16,20},{20,16},{24,28},{28,24},{32,36},... | collective-permute-start | bytes 184328 | tf_op jit(solution)/shard_map/ppermute | solution.py:345
  43.5 4.0 %own.1.refs_1_ = f32[15,16,128]{2,1,0:T(8,128)S(1)} custom-call(f32[5,16,128]{2,1,0:T(8,128)S(1)} %get-tuple-element.40.mean_ref.refs_7_, f32[10,16,128]{2,1,0:T(8,128)S(1)} %get-tuple-element.38.state_ref.harm_ref.refs_8_, s32[12,8,128]{2,1,0:T(8,128)S(1)} %get-tuple-element.28.refs_6_.index_ref.refs_4_, ...), custom_call_target="tpu_custom_call" | custom-call | tf_op jit(solution)/shard_map/own/pallas_call | solution.py:331
  47.5 0.0 collective-permute-done.2.refs_2_
  47.5 0.0 collective-permute-done.3.refs_3_
  47.5 4.8 %close.1 = (f32[5,2048]{1,0:T(8,128)}, f32[5,2,2048]{2,1,0:T(2,128)}) custom-call(s32[1]{0:T(128)S(6)} %copy.12.refs_1_.refs_0_, f32[15,16,128]{2,1,0:T(8,128)S(1)} %own.1.refs_1_, f32[15,8,128]{2,1,0:T(8,128)S(1)} %collective-permute-done.2.refs_2_, f32[15,8,128]{2,1,0:T(8,128)S(1)} %collective-permute-done.3.refs_3_, ...), custom_call_target="tpu_custom_call" | custom-call | tf_op jit(solution)/shard_map/close/pallas_call | solution.py:331
Async XLA Ops:
  2.3 22.6 %collective-permute-start = (f32[15,8,128]{2,1,0:T(8,128)S(1)}, f32[15,8,128]{2,1,0:T(8,128)S(1)}, u32[]{:S(2)}, u32[]{:S(2)}) collective-permute-start(f32[15,8,128]{2,1,0:T(8,128)S(1)} %get-tuple-element.26), channel_id=1, source_target_pairs={{0,508},{4,8},{8,4},{12,16},{16,12},{20,24},{24,20},{28,32},{32,28... | collective-permute-start | bytes 184328 | tf_op jit(solution)/shard_map/ppermute | solution.py:345
  17.6 7.3 %collective-permute-start.1 = (f32[15,8,128]{2,1,0:T(8,128)S(1)}, f32[15,8,128]{2,1,0:T(8,128)S(1)}, u32[]{:S(2)}, u32[]{:S(2)}) collective-permute-start(f32[15,8,128]{2,1,0:T(8,128)S(1)} %get-tuple-element.27), channel_id=1, source_target_pairs={{0,4},{4,0},{8,12},{12,8},{16,20},{20,16},{24,28},{28,24},{32,36},... | collective-permute-start | bytes 184328 | tf_op jit(solution)/shard_map/ppermute | solution.py:345
  37.2 10.2 %collective-permute-start.2 = (f32[15,8,128]{2,1,0:T(8,128)S(1)}, f32[15,8,128]{2,1,0:T(8,128)S(1)}, u32[]{:S(2)}, u32[]{:S(2)}) collective-permute-start(f32[15,8,128]{2,1,0:T(8,128)S(1)} %get-tuple-element.41), channel_id=1, source_target_pairs={{0,508},{4,8},{8,4},{12,16},{16,12},{20,24},{24,20},{28,32},{32,28... | collective-permute-start | bytes 184328 | tf_op jit(solution)/shard_map/ppermute | solution.py:345
  41.6 5.9 %collective-permute-start.3 = (f32[15,8,128]{2,1,0:T(8,128)S(1)}, f32[15,8,128]{2,1,0:T(8,128)S(1)}, u32[]{:S(2)}, u32[]{:S(2)}) collective-permute-start(f32[15,8,128]{2,1,0:T(8,128)S(1)} %get-tuple-element.42), channel_id=1, source_target_pairs={{0,4},{4,0},{8,12},{12,8},{16,20},{20,16},{24,28},{28,24},{32,36},... | collective-permute-start | bytes 184328 | tf_op jit(solution)/shard_map/ppermute | solution.py:345

commit v4 on v3

--- a/solution.py
+++ b/solution.py
@@ -10,6 +10,9 @@
 FACES = 6
 SECTIONS = 2
 ROWS = 3 * VARS
+MEAN_FIELDS = range(VARS)
+HARM_FIELDS = range(VARS, ROWS)
+ALL_FIELDS = range(ROWS)
 HARM = ("harm_0", "harm_1")
 HARM_DEVICES = 4
 LANES = 128
@@ -42,7 +45,7 @@
         hit = high == h
         for i, r in enumerate(fields):
             value = jnp.take_along_axis(spread(row(r, h)), low, axis=1)
-            out[i] = jnp.where(hit, value, 0.0 if h == 0 else out[i])
+            out[i] = jnp.where(hit, value, jnp.zeros_like(value) if h == 0 else out[i])
     return out
 
 
@@ -71,9 +74,16 @@
 
 
 def open_kernel(
-    place_ref, mean_hbm, harm_hbm, tiles_hbm, pay_a, pay_b, tile_idx, tiles_ref, mean_ref, harm_ref, sems
+    place_ref, tiles_hbm, mean_hbm, harm_hbm, links_hbm, weight_hbm, flow_hbm, jac_hbm, source_hbm, step_hbm,
+    pay_a, pay_b, tile_idx, mean_ref, harm_ref, links_ref, weight_ref, flow_ref, jac_ref, source_ref, step_ref,
+    tiles_ref, sems,
 ):
-    for wait in fetch((tiles_hbm, mean_hbm, harm_hbm), (tiles_ref, mean_ref, harm_ref), sems):
+    waits = fetch(
+        (tiles_hbm, mean_hbm, harm_hbm, links_hbm, weight_hbm, flow_hbm, jac_hbm, source_hbm, step_hbm),
+        (tiles_ref, mean_ref, harm_ref, links_ref, weight_ref, flow_ref, jac_ref, source_ref, step_ref),
+        sems,
+    )
+    for wait in waits[:3]:
         wait()
     lowers_first = place_ref[0] % 2 == 1
     lower, upper = (
@@ -85,15 +95,62 @@
     tile_idx[1] = second
     row = native_row(mean_ref, harm_ref)
     store_tiles(row, (first, second), pay_a, pay_b, mean_ref.shape[1] // LANES)
-
-
-def gather_into(row, fields, count, first, index_ref, weight_ref, begin, faces, start):
+    for wait in waits[3:]:
+        wait()
+
+
+TOP = float(2**20 - 1)
+
+
+def largest(values):
+    top = jnp.abs(values[0])
+    for value in values[1:]:
+        top = jnp.maximum(top, jnp.abs(value))
+    top = jnp.max(jnp.max(top, axis=0, keepdims=True), axis=1, keepdims=True)
+    return jnp.maximum(jnp.broadcast_to(top, (SUBS, LANES)), 1e-30)
+
+
+def pack_table(load, blocks, fields, words_ref):
+    unit = {}
+    scale = {}
+    for kind in ([r for r in fields if r < VARS], [r for r in fields if r >= VARS]):
+        if kind:
+            top = largest([load(r, g) for r in kind for g in range(blocks)])
+            for r in kind:
+                unit[r] = top * (1.0 / TOP)
+                scale[r] = TOP / top
+    fixed = lambda r, g: jnp.floor(load(r, g) * scale[r] + 0.5).astype(jnp.int32)
+    for i in range(len(fields) // 3):
+        for g in range(blocks):
+            at = slice(g * SUBS, (g + 1) * SUBS)
+            first, second, third = (fixed(r, g) for r in fields[3 * i : 3 * i + 3])
+            words_ref[2 * i, at, :] = (first << 11) | ((third >> 10) & 0x7FF)
+            words_ref[2 * i + 1, at, :] = (second << 11) | (third & 0x3FF)
+    return unit
+
+
+def gather_into(row, fields, count, words_ref, first, index_ref, weight_ref, begin, faces, unit, start):
+    triples = len(fields) // 3
+    words = 2 * triples
+    rest = fields[3 * triples :]
+
+    def word(w, h):
+        return words_ref[w, h : h + 1, :] if w < words else row(rest[w - words], h)
+
     def face(f, acc):
-        values = picked(row, fields, count, index_ref[begin + f] - first)
+        found = picked(word, range(words + len(rest)), count, index_ref[begin + f] - first)
         weight = weight_ref[begin + f]
+        values = []
+        for i in range(triples):
+            one, two = found[2 * i], found[2 * i + 1]
+            values += [one >> 11, two >> 11, ((one << 21) >> 11) | (two & 0x3FF)]
+        values = [v.astype(F32) for v in values] + found[words:]
         return tuple(a + weight * v for a, v in zip(acc, values))
 
-    return lax.fori_loop(0, faces, face, tuple(start))
+    sums = lax.fori_loop(0, faces, face, (jnp.zeros((SUBS, LANES), F32),) * len(fields))
+    return [
+        s + (a if i >= 3 * triples else unit[r] * a) for i, (r, s, a) in enumerate(zip(fields, start, sums))
+    ]
 
 
 def share_of(place_ref, index_ref):
@@ -102,14 +159,15 @@
     return begin, count, begin // FACES
 
 
-def gather_fields(row, fields, count, first, index_ref, weight_ref, start, out_ref):
+def gather_fields(row, fields, count, words_ref, first, index_ref, weight_ref, unit, start, out_ref, lead=0):
     for g in range(index_ref.shape[0] // FACES):
         at = slice(g * SUBS, (g + 1) * SUBS)
         values = gather_into(
-            row, fields, count, first, index_ref, weight_ref, g * FACES, FACES, [start(r, at) for r in fields]
+            row, fields, count, words_ref, first, index_ref, weight_ref, g * FACES, FACES, unit,
+            [start(r - lead, at) for r in fields],
         )
         for r, value in zip(fields, values):
-            out_ref[r, at, :] = value
+            out_ref[r - lead, at, :] = value
 
 
 def zero_start(*_):
@@ -117,17 +175,10 @@
 
 
 def prepare_kernel(
-    place_ref, mean_hbm, harm_hbm, flow_hbm, jac_hbm, weight_hbm, links_hbm, source_hbm, step_hbm,
-    acc_ref, share_ref, index_ref, weight_ref, wsum_ref, mean_out, state_ref, jac_out, flow_out, source_out, step_out,
-    links_ref, weight_in, mean_ref, harm_ref, flow_ref, source_ref, jac_ref, sems,
+    place_ref, mean_ref, harm_ref, links_ref, weight_in, flow_ref, jac_ref, source_ref,
+    acc_ref, share_ref, index_ref, weight_ref, wsum_ref, mean_out, state_ref, jac_out, flow_out, source_out,
+    words_ref, mean_words,
 ):
-    waits = fetch(
-        (links_hbm, weight_hbm, mean_hbm, harm_hbm, flow_hbm, source_hbm, jac_hbm, step_hbm),
-        (links_ref, weight_in, mean_ref, harm_ref, flow_ref, source_ref, jac_ref, step_out),
-        sems,
-    )
-    for wait in waits[:2]:
-        wait()
     groups = mean_ref.shape[1] // LANES
     flips = place_ref[0] % 2 == 0
     rim = groups * LANES
@@ -144,27 +195,26 @@
         wsum_ref[g * SUBS : (g + 1) * SUBS, :] = total
     row = native_row(mean_ref, harm_ref)
     flow = native_row(mean_ref, flow_ref)
-    for wait in waits[2:4]:
-        wait()
     for g in range(0, groups, SUBS):
         at = slice(g, g + SUBS)
         for r in range(VARS):
             mean_out[r, at, :] = packed(lambda t: row(r, t), g)
         for r in range(2 * VARS):
             state_ref[r, at, :] = packed(lambda t: row(VARS + r, t), g)
+    row = fields_row(mean_out, state_ref)
+    load = fields_block(mean_out, state_ref)
+    unit = pack_table(load, groups // SUBS, HARM_FIELDS, words_ref)
+    mean_unit = pack_table(load, groups // SUBS, MEAN_FIELDS, mean_words)
     gather_fields(
-        lambda r, h: state_ref[r, h : h + 1, :], range(2 * VARS), groups, 0, index_ref, weight_ref,
-        zero_start, acc_ref,
+        row, HARM_FIELDS, groups, words_ref, 0, index_ref, weight_ref, unit, zero_start, acc_ref, VARS
     )
     begin, count, _ = share_of(place_ref, index_ref)
     values = gather_into(
-        lambda r, h: mean_out[r, h : h + 1, :], range(VARS), groups, 0, index_ref, weight_ref,
-        begin, count, [zero_start()] * VARS,
+        row, MEAN_FIELDS, groups, mean_words, 0, index_ref, weight_ref, begin, count, mean_unit,
+        [zero_start()] * VARS,
     )
     for r, value in enumerate(values):
         share_ref[r] = value
-    for wait in waits[4:]:
-        wait()
     for g in range(0, groups, SUBS):
         at = slice(g, g + SUBS)
         for r in range(2 * VARS):
@@ -183,22 +233,43 @@
     return row
 
 
-def own_kernel(mean_ref, harm_ref, index_ref, weight_ref, acc_ref):
+def fields_block(mean_ref, harm_ref):
+    def load(r, g):
+        at = slice(g * SUBS, (g + 1) * SUBS)
+        return mean_ref[r, at, :] if r < VARS else harm_ref[r - VARS, at, :]
+
+    return load
+
+
+def own_kernel(mean_ref, harm_ref, index_ref, weight_ref, acc_ref, words_ref):
+    groups = mean_ref.shape[1]
+    unit = pack_table(fields_block(mean_ref, harm_ref), groups // SUBS, ALL_FIELDS, words_ref)
     gather_fields(
-        fields_row(mean_ref, harm_ref), range(ROWS), mean_ref.shape[1], 0, index_ref, weight_ref,
+        fields_row(mean_ref, harm_ref), ALL_FIELDS, groups, words_ref, 0, index_ref, weight_ref, unit,
         zero_start, acc_ref,
     )
 
 
-def rim_row(rim_a, rim_b, lead=0):
+def rim_row(rim_a, rim_b):
     rows = rim_a.shape[1]
 
     def row(r, h):
         ref = rim_a if h < rows else rim_b
         h = h % rows
-        return ref[lead + r, h : h + 1, :]
+        return ref[r, h : h + 1, :]
 
     return row
+
+
+def rim_block(rim_a, rim_b):
+    blocks = rim_a.shape[1] // SUBS
+
+    def load(r, g):
+        ref = rim_a if g < blocks else rim_b
+        g = g % blocks
+        return ref[r, g * SUBS : (g + 1) * SUBS, :]
+
+    return load
 
 
 def transposed(jac_ref, at, flux):
@@ -226,19 +297,22 @@
 
 def middle_kernel(
     place_ref, order_ref, acc_ref, share_ref, rim_a, rim_b, index_ref, weight_ref, wsum_ref, mean_ref, state_ref,
-    jac_ref, flow_ref, source_ref, step_ref, out_ref, part_ref, full_ref, mean_acc, *, coeff,
+    jac_ref, flow_ref, source_ref, step_ref, out_ref, part_ref, full_ref, mean_acc, words_ref, mean_words, *, coeff,
 ):
     groups = acc_ref.shape[1]
     rim_rows = rim_a.shape[1]
     begin, count, half = share_of(place_ref, index_ref)
     lead = place_ref[0] // 2 == 0
+    row, load = rim_row(rim_a, rim_b), rim_block(rim_a, rim_b)
+    unit = pack_table(load, 2 * rim_rows // SUBS, HARM_FIELDS, words_ref)
+    mean_unit = pack_table(load, 2 * rim_rows // SUBS, MEAN_FIELDS, mean_words)
     gather_fields(
-        rim_row(rim_a, rim_b, VARS), range(2 * VARS), 2 * rim_rows, groups * LANES, index_ref, weight_ref,
-        lambda r, at: acc_ref[r, at, :], full_ref,
+        row, HARM_FIELDS, 2 * rim_rows, words_ref, groups * LANES, index_ref, weight_ref, unit,
+        lambda r, at: acc_ref[r, at, :], full_ref, VARS,
     )
     values = gather_into(
-        rim_row(rim_a, rim_b), range(VARS), 2 * rim_rows, groups * LANES, index_ref, weight_ref,
-        begin, count, [share_ref[r] for r in range(VARS)],
+        row, MEAN_FIELDS, 2 * rim_rows, mean_words, groups * LANES, index_ref, weight_ref,
+        begin, count, mean_unit, [share_ref[r] for r in range(VARS)],
     )
     mean_acc[...] = jnp.zeros(mean_acc.shape, F32)
     for r, value in enumerate(values):
@@ -278,11 +352,13 @@
 def close_kernel(
     order_ref, acc_ref, rim_a, rim_b, index_ref, weight_ref, wsum_ref, mean_ref, state_ref, mean_start, harm_start,
     jac_ref, flow_ref, source_ref, step_ref, stress_ref,
-    mean_hbm, harm_hbm, full_ref, new_mean, new_harm, mean_out, harm_out, sems, *, coeff,
+    mean_hbm, harm_hbm, full_ref, new_mean, new_harm, words_ref, mean_out, harm_out, sems, *, coeff,
 ):
     groups = acc_ref.shape[1]
+    rim_rows = rim_a.shape[1]
+    unit = pack_table(rim_block(rim_a, rim_b), 2 * rim_rows // SUBS, ALL_FIELDS, words_ref)
     gather_fields(
-        rim_row(rim_a, rim_b), range(ROWS), 2 * rim_a.shape[1], groups * LANES, index_ref, weight_ref,
+        rim_row(rim_a, rim_b), ALL_FIELDS, 2 * rim_rows, words_ref, groups * LANES, index_ref, weight_ref, unit,
         lambda r, at: acc_ref[r, at, :], full_ref,
     )
     for g in range(groups // SUBS):
@@ -368,14 +444,19 @@
     step = pseudo_step.reshape(groups, LANES)
     mean_fields, harm_fields = struct(VARS, groups, LANES), struct(2 * VARS, groups, LANES)
     pays = (struct(ROWS, rim_rows, LANES), struct(ROWS, rim_rows, LANES))
-    pay_a, pay_b, tile_idx = launch(
-        open_kernel, "open", pays + (struct(2, rim_rows, LANES, dtype=jnp.int32),), (place,), (),
-        (mean_adjoint, harm_adjoint, face_tiles),
-        held(face_tiles, mean_adjoint, harm_adjoint),
+    raw = (
+        mean_adjoint, harm_adjoint, face_links, face_weight, harm_flow, flux_jacobian, mean_source, step
+    )
+    held_raw = tuple(struct(*a.shape, dtype=a.dtype) for a in raw)
+    pay_a, pay_b, tile_idx, *inside, step = launch(
+        open_kernel, "open", pays + (struct(2, rim_rows, LANES, dtype=jnp.int32),) + held_raw, (place,), (),
+        (face_tiles, *raw), [pltpu.VMEM(face_tiles.shape, jnp.int32), pltpu.SemaphoreType.DMA((9,))],
     )
     rim_a, rim_b = exchange(pay_a, pay_b)
     registers = FACES * halves
-    acc, share, index, weight, wsum, mean_start, harm_start, jac, flow, source, step = launch(
+    words = lambda fields: struct(max(len(fields) // 3 * 2, 1), groups, LANES, dtype=jnp.int32)
+    harm_words, mean_words = words(HARM_FIELDS), words(MEAN_FIELDS)
+    acc, share, index, weight, wsum, mean_start, harm_start, jac, flow, source = launch(
         prepare_kernel, "prepare",
         (
             harm_fields,
@@ -388,18 +469,15 @@
             struct(VARS * VARS, groups, LANES),
             harm_fields,
             mean_fields,
-            struct(groups, LANES),
         ),
-        (place,),
-        (),
-        (mean_adjoint, harm_adjoint, harm_flow, flux_jacobian, face_weight, face_links, mean_source, step),
-        held(face_links, face_weight, mean_adjoint, harm_adjoint, harm_flow, mean_source, flux_jacobian),
+        (place,), inside,
+        scratch=[harm_words, mean_words],
     )
     state, part = launch(
         lambda *refs: middle_kernel(*refs, coeff=1.0 / SECTIONS), "middle", (harm_fields, harm_fields),
         (place, harm_order),
         (acc, share, rim_a, rim_b, index, weight, wsum, mean_start, harm_start, jac, flow, source, step),
-        scratch=[harm_fields, mean_fields],
+        scratch=[harm_fields, mean_fields, harm_words, mean_words],
     )
     parts = lax.all_gather(part, HARM)
     mean, stress, pay_a, pay_b = launch(
@@ -407,13 +485,13 @@
     )
     rim_a, rim_b = exchange(pay_a, pay_b)
     fields = struct(ROWS, groups, LANES)
-    (acc,) = launch(own_kernel, "own", (fields,), (), (mean, state, index, weight))
+    (acc,) = launch(own_kernel, "own", (fields,), (), (mean, state, index, weight), scratch=[words(ALL_FIELDS)])
     outs = [jax.ShapeDtypeStruct(s, F32) for s in ((VARS, cells), (VARS, 2, cells))]
     mean_new, harm_new = launch(
         lambda *refs: close_kernel(*refs, coeff=1.0), "close", tuple(outs), (harm_order,),
         (acc, rim_a, rim_b, index, weight, wsum, mean, state, mean_start, harm_start,
          jac, flow, source, step, stress),
-        scratch=[fields, mean_fields, harm_fields, *held(*outs)],
+        scratch=[fields, mean_fields, harm_fields, words(ALL_FIELDS), *held(*outs)],
     )
     return mean_new, harm_new.swapaxes(0, 1)[None]
 

time: 52.6 us -> 49.9 us (0.949)
  Pallas kernels: 19.2 us -> 15.4 us
  waiting for transfers between devices: 0.01 us -> 0.54 us
    pallas_call x6, Pallas kernels: 19.2 us -> 15.4 us  [launch(): pl.pallas_call(body, name=name, out_shape=out_shape, in_specs=[smem] * le...]
    ppermute x2, waiting for transfers between devices: 0.01 us -> 0.53 us  [exchange(): lax.ppermute(pay_a, 'cells', far)]
  transfers between devices with their start and end apart: 4 -> 4, of which waited for: 0 -> 1; matrix products, arithmetic and copies ran while one was open for 0% -> 0% of each run, Pallas kernels for 17% -> 13%
where the time goes in v4:
time: 49.9 us; the launch traced here: 49.1 us
  starting transfers between devices  23.1 us (46%)
  Pallas kernels  15.4 us (31%)
  blocking collectives  8.66 us (17%)
  between operations  1.38 us (3%)
  waiting for transfers between devices  0.54 us (1%)
    ppermute x2, starting transfers between devices, exchange(): lax.ppermute(pay_a, 'cells', far)  19.3 us
    pallas_call x6, Pallas kernels, launch(): pl.pallas_call(body, name=name, out_shape=out_shape, in_specs=[smem] * le...  15.4 us
    all_gather x1, blocking collectives, shards(): parts = lax.all_gather(part, HARM)  8.66 us
    ppermute x2, starting transfers between devices, exchange(): lax.ppermute(pay_b, 'cells', near)  3.84 us
  transfers between devices with their start and end apart: 4, of which 1 were waited for; matrix products, arithmetic and copies ran while one was open for 0% of the time, Pallas kernels for 13%

profile of v4, /device:TPU:1, one launch (start us, length us, event | category | flops | bytes accessed | tf_op | source)
XLA Modules:
  0.0 49.1 jit_solution(3296044119814898988)
XLA Ops:
  0.6 1.6 %open.1 = (f32[15,8,128]{2,1,0:T(8,128)S(1)}, f32[15,8,128]{2,1,0:T(8,128)S(1)}, s32[2,8,128]{2,1,0:T(8,128)S(1)}, f32[5,2048]{1,0:T(8,128)S(1)}, f32[5,2,2048]{...) custom-call(s32[1]{0:T(128)} %bitcast.place_ref.refs_0_, ...), custom_call_target="tpu_custom_call" | custom-call | tf_op jit(solution)/shard_map/open/pallas_call | solution.py:407
  2.3 15.3 %collective-permute-start = (f32[15,8,128]{2,1,0:T(8,128)S(1)}, f32[15,8,128]{2,1,0:T(8,128)S(1)}, u32[]{:S(2)}, u32[]{:S(2)}) collective-permute-start(f32[15,8,128]{2,1,0:T(8,128)S(1)} %get-tuple-element.40), channel_id=1, source_target_pairs={{0,508},{4,8},{8,4},{12,16},{16,12},{20,24},{24,20},{28,32},{32,28... | collective-permute-start | bytes 184328 | tf_op jit(solution)/shard_map/ppermute | solution.py:421
  17.6 1.9 %collective-permute-start.1 = (f32[15,8,128]{2,1,0:T(8,128)S(1)}, f32[15,8,128]{2,1,0:T(8,128)S(1)}, u32[]{:S(2)}, u32[]{:S(2)}) collective-permute-start(f32[15,8,128]{2,1,0:T(8,128)S(1)} %get-tuple-element.41), channel_id=1, source_target_pairs={{0,4},{4,0},{8,12},{12,8},{16,20},{20,16},{24,28},{28,24},{32,36},... | collective-permute-start | bytes 184328 | tf_op jit(solution)/shard_map/ppermute | solution.py:421
  20.2 3.1 %prepare.1 = (f32[10,16,128]{2,1,0:T(8,128)S(1)}, f32[5,8,128]{2,1,0:T(8,128)S(1)}, s32[12,8,128]{2,1,0:T(8,128)S(1)}, f32[12,8,128]{2,1,0:T(8,128)S(1)}, f32[16...) custom-call(s32[1]{0:T(128)} %bitcast.place_ref.refs_0_, ...), custom_call_target="tpu_custom_call" | custom-call | tf_op jit(solution)/shard_map/prepare/pallas_call | solution.py:407
  23.3 0.0 collective-permute-done.refs_4_
  23.3 0.0 collective-permute-done.1.refs_5_
  23.3 3.0 %middle.1 = (f32[10,16,128]{2,1,0:T(8,128)S(1)}, f32[10,16,128]{2,1,0:T(8,128)S(1)}) custom-call(s32[1]{0:T(128)} %bitcast.place_ref.refs_0_, s32[1]{0:T(128)S(6)} %copy.12.refs_1_.refs_0_, f32[10,16,128]{2,1,0:T(8,128)S(1)} %get-tuple-element.38.refs_2_, f32[5,8,128]{2,1,0:T(8,128)S(1)} %get-tuple-element.39.refs_3_, ...), custom_call_target="tpu_custom_call" | custom-call | tf_op jit(solution)/shard_map/middle/pallas_call | solution.py:407
  26.3 8.7 %all-gather = f32[40,16,128]{2,1,0:T(8,128)S(1)} all-gather(f32[10,16,128]{2,1,0:T(8,128)S(1)} %get-tuple-element.51), channel_id=2, replica_groups=mesh['cells'=128,'harm_0'=2,'harm_1'=2] {'harm_0','harm_1'}, dimensions={0}, use_global_device_ids=true | all-gather | bytes 409600 | tf_op jit(solution)/shard_map/all_gather | solution.py:482
  35.0 0.6 %join.1 = (f32[5,16,128]{2,1,0:T(8,128)S(1)}, f32[5,16,128]{2,1,0:T(8,128)S(1)}, f32[15,8,128]{2,1,0:T(8,128)S(1)}, f32[15,8,128]{2,1,0:T(8,128)S(1)}) custom-call(f32[4,10,16,128]{3,2,1,0:T(8,128)S(1)} %bitcast.12, f32[10,16,128]{2,1,0:T(8,128)S(1)} %get-tuple-element.52.state_ref.harm_ref.refs_8_, s32[2,8,128]{2,1,0:T(8,128)S(1)} %get-tuple-element.53.tile_idx), custom_call_target="tpu_custom_call" | custom-call | tf_op jit(solution)/shard_map/join/pallas_call | solution.py:407
  35.6 3.9 %collective-permute-start.2 = (f32[15,8,128]{2,1,0:T(8,128)S(1)}, f32[15,8,128]{2,1,0:T(8,128)S(1)}, u32[]{:S(2)}, u32[]{:S(2)}) collective-permute-start(f32[15,8,128]{2,1,0:T(8,128)S(1)} %get-tuple-element.55), channel_id=1, source_target_pairs={{0,508},{4,8},{8,4},{12,16},{16,12},{20,24},{24,20},{28,32},{32,28... | collective-permute-start | bytes 184328 | tf_op jit(solution)/shard_map/ppermute | solution.py:421
  39.5 1.9 %collective-permute-start.3 = (f32[15,8,128]{2,1,0:T(8,128)S(1)}, f32[15,8,128]{2,1,0:T(8,128)S(1)}, u32[]{:S(2)}, u32[]{:S(2)}) collective-permute-start(f32[15,8,128]{2,1,0:T(8,128)S(1)} %get-tuple-element.56), channel_id=1, source_target_pairs={{0,4},{4,0},{8,12},{12,8},{16,20},{20,16},{24,28},{28,24},{32,36},... | collective-permute-start | bytes 184328 | tf_op jit(solution)/shard_map/ppermute | solution.py:421
  41.5 3.1 %own.1.refs_1_ = f32[15,16,128]{2,1,0:T(8,128)S(1)} custom-call(f32[5,16,128]{2,1,0:T(8,128)S(1)} %get-tuple-element.54.mean_ref.refs_7_, f32[10,16,128]{2,1,0:T(8,128)S(1)} %get-tuple-element.52.state_ref.harm_ref.refs_8_, s32[12,8,128]{2,1,0:T(8,128)S(1)} %get-tuple-element.42.refs_6_.index_ref.refs_4_, ...), custom_call_target="tpu_custom_call" | custom-call | tf_op jit(solution)/shard_map/own/pallas_call | solution.py:407
  44.6 0.5 %collective-permute-done.2.refs_2_ = f32[15,8,128]{2,1,0:T(8,128)S(1)} collective-permute-done((f32[15,8,128]{2,1,0:T(8,128)S(1)}, f32[15,8,128]{2,1,0:T(8,128)S(1)}, u32[]{:S(2)}, u32[]{:S(2)}) %collective-permute-start.2) | collective-permute-done | bytes 61472 | tf_op jit(solution)/shard_map/ppermute | solution.py:421
  45.1 0.0 collective-permute-done.3.refs_3_
  45.1 4.0 %close.1 = (f32[5,2048]{1,0:T(8,128)}, f32[5,2,2048]{2,1,0:T(2,128)}) custom-call(s32[1]{0:T(128)S(6)} %copy.12.refs_1_.refs_0_, f32[15,16,128]{2,1,0:T(8,128)S(1)} %own.1.refs_1_, f32[15,8,128]{2,1,0:T(8,128)S(1)} %collective-permute-done.2.refs_2_, f32[15,8,128]{2,1,0:T(8,128)S(1)} %collective-permute-done.3.refs_3_, ...), custom_call_target="tpu_custom_call" | custom-call | tf_op jit(solution)/shard_map/close/pallas_call | solution.py:407
Async XLA Ops:
  2.3 21.0 %collective-permute-start = (f32[15,8,128]{2,1,0:T(8,128)S(1)}, f32[15,8,128]{2,1,0:T(8,128)S(1)}, u32[]{:S(2)}, u32[]{:S(2)}) collective-permute-start(f32[15,8,128]{2,1,0:T(8,128)S(1)} %get-tuple-element.40), channel_id=1, source_target_pairs={{0,508},{4,8},{8,4},{12,16},{16,12},{20,24},{24,20},{28,32},{32,28... | collective-permute-start | bytes 184328 | tf_op jit(solution)/shard_map/ppermute | solution.py:421
  17.6 5.7 %collective-permute-start.1 = (f32[15,8,128]{2,1,0:T(8,128)S(1)}, f32[15,8,128]{2,1,0:T(8,128)S(1)}, u32[]{:S(2)}, u32[]{:S(2)}) collective-permute-start(f32[15,8,128]{2,1,0:T(8,128)S(1)} %get-tuple-element.41), channel_id=1, source_target_pairs={{0,4},{4,0},{8,12},{12,8},{16,20},{20,16},{24,28},{28,24},{32,36},... | collective-permute-start | bytes 184328 | tf_op jit(solution)/shard_map/ppermute | solution.py:421
  35.6 9.5 %collective-permute-start.2 = (f32[15,8,128]{2,1,0:T(8,128)S(1)}, f32[15,8,128]{2,1,0:T(8,128)S(1)}, u32[]{:S(2)}, u32[]{:S(2)}) collective-permute-start(f32[15,8,128]{2,1,0:T(8,128)S(1)} %get-tuple-element.55), channel_id=1, source_target_pairs={{0,508},{4,8},{8,4},{12,16},{16,12},{20,24},{24,20},{28,32},{32,28... | collective-permute-start | bytes 184328 | tf_op jit(solution)/shard_map/ppermute | solution.py:421
  39.5 5.6 %collective-permute-start.3 = (f32[15,8,128]{2,1,0:T(8,128)S(1)}, f32[15,8,128]{2,1,0:T(8,128)S(1)}, u32[]{:S(2)}, u32[]{:S(2)}) collective-permute-start(f32[15,8,128]{2,1,0:T(8,128)S(1)} %get-tuple-element.56), channel_id=1, source_target_pairs={{0,4},{4,0},{8,12},{12,8},{16,20},{20,16},{24,28},{28,24},{32,36},... | collective-permute-start | bytes 184328 | tf_op jit(solution)/shard_map/ppermute | solution.py:421

commit v5 on v4

--- a/solution.py
+++ b/solution.py
@@ -147,7 +147,9 @@
         values = [v.astype(F32) for v in values] + found[words:]
         return tuple(a + weight * v for a, v in zip(acc, values))
 
-    sums = lax.fori_loop(0, faces, face, (jnp.zeros((SUBS, LANES), F32),) * len(fields))
+    sums = (jnp.zeros((SUBS, LANES), F32),) * len(fields)
+    for f in range(faces):
+        sums = face(f, sums)
     return [
         s + (a if i >= 3 * triples else unit[r] * a) for i, (r, s, a) in enumerate(zip(fields, start, sums))
     ]
@@ -241,15 +243,6 @@
     return load
 
 
-def own_kernel(mean_ref, harm_ref, index_ref, weight_ref, acc_ref, words_ref):
-    groups = mean_ref.shape[1]
-    unit = pack_table(fields_block(mean_ref, harm_ref), groups // SUBS, ALL_FIELDS, words_ref)
-    gather_fields(
-        fields_row(mean_ref, harm_ref), ALL_FIELDS, groups, words_ref, 0, index_ref, weight_ref, unit,
-        zero_start, acc_ref,
-    )
-
-
 def rim_row(rim_a, rim_b):
     rows = rim_a.shape[1]
 
@@ -349,17 +342,15 @@
     store_tiles(row, (tile_idx[0], tile_idx[1]), pay_a, pay_b, mean_ref.shape[1])
 
 
-def close_kernel(
-    order_ref, acc_ref, rim_a, rim_b, index_ref, weight_ref, wsum_ref, mean_ref, state_ref, mean_start, harm_start,
-    jac_ref, flow_ref, source_ref, step_ref, stress_ref,
-    mean_hbm, harm_hbm, full_ref, new_mean, new_harm, words_ref, mean_out, harm_out, sems, *, coeff,
+def own_kernel(
+    order_ref, index_ref, weight_ref, wsum_ref, mean_ref, state_ref, mean_start, harm_start,
+    jac_ref, flow_ref, source_ref, step_ref, stress_ref, mean_base, harm_base, full_ref, words_ref, *, coeff,
 ):
-    groups = acc_ref.shape[1]
-    rim_rows = rim_a.shape[1]
-    unit = pack_table(rim_block(rim_a, rim_b), 2 * rim_rows // SUBS, ALL_FIELDS, words_ref)
+    groups = mean_ref.shape[1]
+    unit = pack_table(fields_block(mean_ref, state_ref), groups // SUBS, ALL_FIELDS, words_ref)
     gather_fields(
-        rim_row(rim_a, rim_b), ALL_FIELDS, 2 * rim_rows, words_ref, groups * LANES, index_ref, weight_ref, unit,
-        lambda r, at: acc_ref[r, at, :], full_ref,
+        fields_row(mean_ref, state_ref), ALL_FIELDS, groups, words_ref, 0, index_ref, weight_ref, unit,
+        zero_start, full_ref,
     )
     for g in range(groups // SUBS):
         at = slice(g * SUBS, (g + 1) * SUBS)
@@ -369,19 +360,40 @@
         scale = coeff * step_ref[at, :]
         flux = [wsum * m - full_ref[v, at, :] - stress_ref[v, at, :] for v, m in enumerate(mean)]
         for v, res in enumerate(transposed(jac_ref, at, flux)):
-            new_mean[v, at, :] = mean_start[v, at, :] - scale * (res - source_ref[v, at, :])
+            mean_base[v, at, :] = mean_start[v, at, :] - scale * (res - source_ref[v, at, :])
         gathered = [full_ref[VARS + r, at, :] for r in range(2 * VARS)]
         start = [harm_start[r, at, :] for r in range(2 * VARS)]
-        harm_step(order_ref, at, mean, state, start, gathered, wsum, scale, jac_ref, flow_ref, new_harm)
+        harm_step(order_ref, at, mean, state, start, gathered, wsum, scale, jac_ref, flow_ref, harm_base)
+
+
+def close_kernel(
+    rim_a, rim_b, index_ref, weight_ref, jac_ref, step_ref, mean_base, harm_base,
+    mean_hbm, harm_hbm, full_ref, words_ref, mean_out, harm_out, sems, *, coeff,
+):
+    groups = mean_base.shape[1]
+    rim_rows = rim_a.shape[1]
+    unit = pack_table(rim_block(rim_a, rim_b), 2 * rim_rows // SUBS, ALL_FIELDS, words_ref)
+    gather_fields(
+        rim_row(rim_a, rim_b), ALL_FIELDS, 2 * rim_rows, words_ref, groups * LANES, index_ref, weight_ref, unit,
+        zero_start, full_ref,
+    )
+    base = fields_block(mean_base, harm_base)
+    for g in range(groups // SUBS):
+        at = slice(g * SUBS, (g + 1) * SUBS)
+        scale = coeff * step_ref[at, :]
+        for first in range(0, ROWS, VARS):
+            values = [full_ref[first + v, at, :] for v in range(VARS)]
+            for v, res in enumerate(transposed(jac_ref, at, values)):
+                full_ref[first + v, at, :] = base(first + v, g) + scale * res
     for t in range(groups):
         lanes = slice(t * LANES, (t + 1) * LANES)
-        mean_out[:, lanes] = stacked(lambda i: new_mean[i, t : t + 1, :], VARS)
+        mean_out[:, lanes] = stacked(lambda i: full_ref[i, t : t + 1, :], VARS)
     mean_copy = pltpu.make_async_copy(mean_out, mean_hbm, sems.at[0])
     mean_copy.start()
     for t in range(groups):
         lanes = slice(t * LANES, (t + 1) * LANES)
         for v in range(VARS):
-            harm_out[v, :, lanes] = stacked(lambda i: new_harm[i * VARS + v, t : t + 1, :], 2)
+            harm_out[v, :, lanes] = stacked(lambda i: full_ref[(i + 1) * VARS + v, t : t + 1, :], 2)
     harm_copy = pltpu.make_async_copy(harm_out, harm_hbm, sems.at[1])
     harm_copy.start()
     mean_copy.wait()
@@ -485,13 +497,16 @@
     )
     rim_a, rim_b = exchange(pay_a, pay_b)
     fields = struct(ROWS, groups, LANES)
-    (acc,) = launch(own_kernel, "own", (fields,), (), (mean, state, index, weight), scratch=[words(ALL_FIELDS)])
+    mean_base, harm_base = launch(
+        lambda *refs: own_kernel(*refs, coeff=1.0), "own", (mean_fields, harm_fields), (harm_order,),
+        (index, weight, wsum, mean, state, mean_start, harm_start, jac, flow, source, step, stress),
+        scratch=[fields, words(ALL_FIELDS)],
+    )
     outs = [jax.ShapeDtypeStruct(s, F32) for s in ((VARS, cells), (VARS, 2, cells))]
     mean_new, harm_new = launch(
-        lambda *refs: close_kernel(*refs, coeff=1.0), "close", tuple(outs), (harm_order,),
-        (acc, rim_a, rim_b, index, weight, wsum, mean, state, mean_start, harm_start,
-         jac, flow, source, step, stress),
-        scratch=[fields, mean_fields, harm_fields, words(ALL_FIELDS), *held(*outs)],
+        lambda *refs: close_kernel(*refs, coeff=1.0), "close", tuple(outs), (),
+        (rim_a, rim_b, index, weight, jac, step, mean_base, harm_base),
+        scratch=[fields, words(ALL_FIELDS), *held(*outs)],
     )
     return mean_new, harm_new.swapaxes(0, 1)[None]
 

time: 49.9 us -> 48 us (0.962)
  Pallas kernels: 15.4 us -> 11.7 us
  waiting for transfers between devices: 0.54 us -> 1.58 us
  blocking collectives: 8.66 us -> 9.4 us
    pallas_call x6, Pallas kernels: 15.4 us -> 11.7 us  [launch(): pl.pallas_call(body, name=name, out_shape=out_shape, in_specs=[smem] * le...]
    ppermute x2, waiting for transfers between devices: 0.53 us -> 1.3 us  [exchange(): lax.ppermute(pay_a, 'cells', far)]
    all_gather x1, blocking collectives: 8.66 us -> 9.4 us  [shards(): parts = lax.all_gather(part, HARM)]
  transfers between devices with their start and end apart: 4 -> 4, of which waited for: 1 -> 2; matrix products, arithmetic and copies ran while one was open for 0% -> 0% of each run, Pallas kernels for 13% -> 9%
where the time goes in v5:
time: 48 us; the launch traced here: 47.1 us
  starting transfers between devices  23.1 us (48%)
  Pallas kernels  11.7 us (24%)
  blocking collectives  9.4 us (20%)
  waiting for transfers between devices  1.58 us (3%)
  between operations  1.38 us (3%)
    ppermute x2, starting transfers between devices, exchange(): lax.ppermute(pay_a, 'cells', far)  19.3 us
    pallas_call x6, Pallas kernels, launch(): pl.pallas_call(body, name=name, out_shape=out_shape, in_specs=[smem] * le...  11.7 us
    all_gather x1, blocking collectives, shards(): parts = lax.all_gather(part, HARM)  9.4 us
    ppermute x2, starting transfers between devices, exchange(): lax.ppermute(pay_b, 'cells', near)  3.84 us
    ppermute x2, waiting for transfers between devices, exchange(): lax.ppermute(pay_a, 'cells', far)  1.3 us
  transfers between devices with their start and end apart: 4, of which 2 were waited for; matrix products, arithmetic and copies ran while one was open for 0% of the time, Pallas kernels for 9%

profile of v5, /device:TPU:1, one launch (start us, length us, event | category | flops | bytes accessed | tf_op | source)
XLA Modules:
  0.0 47.1 jit_solution(8052868894747422519)
XLA Ops:
  0.6 1.6 %open.1 = (f32[15,8,128]{2,1,0:T(8,128)S(1)}, f32[15,8,128]{2,1,0:T(8,128)S(1)}, s32[2,8,128]{2,1,0:T(8,128)S(1)}, f32[5,2048]{1,0:T(8,128)S(1)}, f32[5,2,2048]{...) custom-call(s32[1]{0:T(128)} %bitcast.place_ref.refs_0_, ...), custom_call_target="tpu_custom_call" | custom-call | tf_op jit(solution)/shard_map/open/pallas_call | solution.py:419
  2.3 15.3 %collective-permute-start = (f32[15,8,128]{2,1,0:T(8,128)S(1)}, f32[15,8,128]{2,1,0:T(8,128)S(1)}, u32[]{:S(2)}, u32[]{:S(2)}) collective-permute-start(f32[15,8,128]{2,1,0:T(8,128)S(1)} %get-tuple-element.42), channel_id=1, source_target_pairs={{0,508},{4,8},{8,4},{12,16},{16,12},{20,24},{24,20},{28,32},{32,28... | collective-permute-start | bytes 184328 | tf_op jit(solution)/shard_map/ppermute | solution.py:433
  17.6 1.9 %collective-permute-start.1 = (f32[15,8,128]{2,1,0:T(8,128)S(1)}, f32[15,8,128]{2,1,0:T(8,128)S(1)}, u32[]{:S(2)}, u32[]{:S(2)}) collective-permute-start(f32[15,8,128]{2,1,0:T(8,128)S(1)} %get-tuple-element.43), channel_id=1, source_target_pairs={{0,4},{4,0},{8,12},{12,8},{16,20},{20,16},{24,28},{28,24},{32,36},... | collective-permute-start | bytes 184328 | tf_op jit(solution)/shard_map/ppermute | solution.py:433
  20.2 2.1 %prepare.1 = (f32[10,16,128]{2,1,0:T(8,128)S(1)}, f32[5,8,128]{2,1,0:T(8,128)S(1)}, s32[12,8,128]{2,1,0:T(8,128)S(1)}, f32[12,8,128]{2,1,0:T(8,128)S(1)}, f32[16...) custom-call(s32[1]{0:T(128)} %bitcast.place_ref.refs_0_, ...), custom_call_target="tpu_custom_call" | custom-call | tf_op jit(solution)/shard_map/prepare/pallas_call | solution.py:419
  22.3 0.0 collective-permute-done.refs_4_
  22.3 0.3 collective-permute-done.1.refs_5_
  22.6 1.9 %middle.1 = (f32[10,16,128]{2,1,0:T(8,128)S(1)}, f32[10,16,128]{2,1,0:T(8,128)S(1)}) custom-call(s32[1]{0:T(128)} %bitcast.place_ref.refs_0_, s32[1]{0:T(128)S(6)} %copy.12.refs_1_.refs_0_, f32[10,16,128]{2,1,0:T(8,128)S(1)} %get-tuple-element.40.refs_2_, f32[5,8,128]{2,1,0:T(8,128)S(1)} %get-tuple-element.41.refs_3_, ...), custom_call_target="tpu_custom_call" | custom-call | tf_op jit(solution)/shard_map/middle/pallas_call | solution.py:419
  24.5 9.4 %all-gather = f32[40,16,128]{2,1,0:T(8,128)S(1)} all-gather(f32[10,16,128]{2,1,0:T(8,128)S(1)} %get-tuple-element.53), channel_id=2, replica_groups=mesh['cells'=128,'harm_0'=2,'harm_1'=2] {'harm_0','harm_1'}, dimensions={0}, use_global_device_ids=true | all-gather | bytes 409600 | tf_op jit(solution)/shard_map/all_gather | solution.py:494
  33.9 0.6 %join.1 = (f32[5,16,128]{2,1,0:T(8,128)S(1)}, f32[5,16,128]{2,1,0:T(8,128)S(1)}, f32[15,8,128]{2,1,0:T(8,128)S(1)}, f32[15,8,128]{2,1,0:T(8,128)S(1)}) custom-call(f32[4,10,16,128]{3,2,1,0:T(8,128)S(1)} %bitcast.12, f32[10,16,128]{2,1,0:T(8,128)S(1)} %get-tuple-element.54.state_ref.refs_5_, s32[2,8,128]{2,1,0:T(8,128)S(1)} %get-tuple-element.55.tile_idx), custom_call_target="tpu_custom_call" | custom-call | tf_op jit(solution)/shard_map/join/pallas_call | solution.py:419
  34.5 3.9 %collective-permute-start.2 = (f32[15,8,128]{2,1,0:T(8,128)S(1)}, f32[15,8,128]{2,1,0:T(8,128)S(1)}, u32[]{:S(2)}, u32[]{:S(2)}) collective-permute-start(f32[15,8,128]{2,1,0:T(8,128)S(1)} %get-tuple-element.56), channel_id=1, source_target_pairs={{0,508},{4,8},{8,4},{12,16},{16,12},{20,24},{24,20},{28,32},{32,28... | collective-permute-start | bytes 184328 | tf_op jit(solution)/shard_map/ppermute | solution.py:433
  38.5 1.9 %collective-permute-start.3 = (f32[15,8,128]{2,1,0:T(8,128)S(1)}, f32[15,8,128]{2,1,0:T(8,128)S(1)}, u32[]{:S(2)}, u32[]{:S(2)}) collective-permute-start(f32[15,8,128]{2,1,0:T(8,128)S(1)} %get-tuple-element.57), channel_id=1, source_target_pairs={{0,4},{4,0},{8,12},{12,8},{16,20},{20,16},{24,28},{28,24},{32,36},... | collective-permute-start | bytes 184328 | tf_op jit(solution)/shard_map/ppermute | solution.py:433
  40.4 2.3 %own.1 = (f32[5,16,128]{2,1,0:T(8,128)S(1)}, f32[10,16,128]{2,1,0:T(8,128)S(1)}) custom-call(s32[1]{0:T(128)S(6)} %copy.12.refs_1_.refs_0_, s32[12,8,128]{2,1,0:T(8,128)S(1)} %get-tuple-element.44.refs_6_.refs_1_.refs_2_, f32[12,8,128]{2,1,0:T(8,128)S(1)} %get-tuple-element.45.refs_7_.refs_2_.refs_3_, f32[16,128]{1,0:T(8,128)S(1)} %get-tuple-element.46.refs_8_.refs_3_, ...), custom_call_target="tpu_custom_call" | custom-call | tf_op jit(solution)/shard_map/own/pallas_call | solution.py:419
  42.8 1.3 %collective-permute-done.2.refs_0_ = f32[15,8,128]{2,1,0:T(8,128)S(1)} collective-permute-done((f32[15,8,128]{2,1,0:T(8,128)S(1)}, f32[15,8,128]{2,1,0:T(8,128)S(1)}, u32[]{:S(2)}, u32[]{:S(2)}) %collective-permute-start.2) | collective-permute-done | bytes 61472 | tf_op jit(solution)/shard_map/ppermute | solution.py:433
  44.1 0.0 collective-permute-done.3.refs_1_
  44.1 3.1 %close.1 = (f32[5,2048]{1,0:T(8,128)}, f32[5,2,2048]{2,1,0:T(2,128)}) custom-call(f32[15,8,128]{2,1,0:T(8,128)S(1)} %collective-permute-done.2.refs_0_, f32[15,8,128]{2,1,0:T(8,128)S(1)} %collective-permute-done.3.refs_1_, s32[12,8,128]{2,1,0:T(8,128)S(1)} %get-tuple-element.44.refs_6_.refs_1_.refs_2_, ...), custom_call_target="tpu_custom_call" | custom-call | tf_op jit(solution)/shard_map/close/pallas_call | solution.py:419
Async XLA Ops:
  2.3 20.0 %collective-permute-start = (f32[15,8,128]{2,1,0:T(8,128)S(1)}, f32[15,8,128]{2,1,0:T(8,128)S(1)}, u32[]{:S(2)}, u32[]{:S(2)}) collective-permute-start(f32[15,8,128]{2,1,0:T(8,128)S(1)} %get-tuple-element.42), channel_id=1, source_target_pairs={{0,508},{4,8},{8,4},{12,16},{16,12},{20,24},{24,20},{28,32},{32,28... | collective-permute-start | bytes 184328 | tf_op jit(solution)/shard_map/ppermute | solution.py:433
  17.6 5.0 %collective-permute-start.1 = (f32[15,8,128]{2,1,0:T(8,128)S(1)}, f32[15,8,128]{2,1,0:T(8,128)S(1)}, u32[]{:S(2)}, u32[]{:S(2)}) collective-permute-start(f32[15,8,128]{2,1,0:T(8,128)S(1)} %get-tuple-element.43), channel_id=1, source_target_pairs={{0,4},{4,0},{8,12},{12,8},{16,20},{20,16},{24,28},{28,24},{32,36},... | collective-permute-start | bytes 184328 | tf_op jit(solution)/shard_map/ppermute | solution.py:433
  34.5 9.5 %collective-permute-start.2 = (f32[15,8,128]{2,1,0:T(8,128)S(1)}, f32[15,8,128]{2,1,0:T(8,128)S(1)}, u32[]{:S(2)}, u32[]{:S(2)}) collective-permute-start(f32[15,8,128]{2,1,0:T(8,128)S(1)} %get-tuple-element.56), channel_id=1, source_target_pairs={{0,508},{4,8},{8,4},{12,16},{16,12},{20,24},{24,20},{28,32},{32,28... | collective-permute-start | bytes 184328 | tf_op jit(solution)/shard_map/ppermute | solution.py:433
  38.5 5.6 %collective-permute-start.3 = (f32[15,8,128]{2,1,0:T(8,128)S(1)}, f32[15,8,128]{2,1,0:T(8,128)S(1)}, u32[]{:S(2)}, u32[]{:S(2)}) collective-permute-start(f32[15,8,128]{2,1,0:T(8,128)S(1)} %get-tuple-element.57), channel_id=1, source_target_pairs={{0,4},{4,0},{8,12},{12,8},{16,20},{20,16},{24,28},{28,24},{32,36},... | collective-permute-start | bytes 184328 | tf_op jit(solution)/shard_map/ppermute | solution.py:433

commit v6 on v5

--- a/solution.py
+++ b/solution.py
@@ -243,26 +243,48 @@
     return load
 
 
-def rim_row(rim_a, rim_b):
-    rows = rim_a.shape[1]
-
-    def row(r, h):
-        ref = rim_a if h < rows else rim_b
-        h = h % rows
-        return ref[r, h : h + 1, :]
-
-    return row
-
-
-def rim_block(rim_a, rim_b):
-    blocks = rim_a.shape[1] // SUBS
-
-    def load(r, g):
-        ref = rim_a if g < blocks else rim_b
-        g = g % blocks
-        return ref[r, g * SUBS : (g + 1) * SUBS, :]
-
-    return load
+def rim_row(rim):
+    return lambda r, h: rim[r, h : h + 1, :]
+
+
+def rim_block(rim):
+    return lambda r, g: rim[r, g * SUBS : (g + 1) * SUBS, :]
+
+
+def shared_rim(place_ref, acc_ref, share_ref, rim, first, index_ref, weight_ref, words_ref, mean_words, out_ref):
+    rows = rim.shape[1]
+    row, load = rim_row(rim), rim_block(rim)
+    unit = pack_table(load, rows // SUBS, HARM_FIELDS, words_ref)
+    mean_unit = pack_table(load, rows // SUBS, MEAN_FIELDS, mean_words)
+    gather_fields(
+        row, HARM_FIELDS, rows, words_ref, first, index_ref, weight_ref, unit,
+        lambda r, at: acc_ref[r, at, :], out_ref, VARS,
+    )
+    begin, count, _ = share_of(place_ref, index_ref)
+    return gather_into(
+        row, MEAN_FIELDS, rows, mean_words, first, index_ref, weight_ref,
+        begin, count, mean_unit, [share_ref[r] for r in range(VARS)],
+    )
+
+
+def near_share_kernel(
+    place_ref, acc_ref, share_ref, rim, index_ref, weight_ref, out_ref, share_out, words_ref, mean_words
+):
+    first = (acc_ref.shape[1] + rim.shape[1]) * LANES
+    values = shared_rim(
+        place_ref, acc_ref, share_ref, rim, first, index_ref, weight_ref, words_ref, mean_words, out_ref
+    )
+    for r, value in enumerate(values):
+        share_out[r] = value
+
+
+def near_kernel(rim, index_ref, weight_ref, out_ref, words_ref):
+    rows = rim.shape[1]
+    first = (out_ref.shape[1] + rows) * LANES
+    unit = pack_table(rim_block(rim), rows // SUBS, ALL_FIELDS, words_ref)
+    gather_fields(
+        rim_row(rim), ALL_FIELDS, rows, words_ref, first, index_ref, weight_ref, unit, zero_start, out_ref
+    )
 
 
 def transposed(jac_ref, at, flux):
@@ -289,23 +311,14 @@
 
 
 def middle_kernel(
-    place_ref, order_ref, acc_ref, share_ref, rim_a, rim_b, index_ref, weight_ref, wsum_ref, mean_ref, state_ref,
+    place_ref, order_ref, acc_ref, share_ref, rim, index_ref, weight_ref, wsum_ref, mean_ref, state_ref,
     jac_ref, flow_ref, source_ref, step_ref, out_ref, part_ref, full_ref, mean_acc, words_ref, mean_words, *, coeff,
 ):
     groups = acc_ref.shape[1]
-    rim_rows = rim_a.shape[1]
-    begin, count, half = share_of(place_ref, index_ref)
+    _, _, half = share_of(place_ref, index_ref)
     lead = place_ref[0] // 2 == 0
-    row, load = rim_row(rim_a, rim_b), rim_block(rim_a, rim_b)
-    unit = pack_table(load, 2 * rim_rows // SUBS, HARM_FIELDS, words_ref)
-    mean_unit = pack_table(load, 2 * rim_rows // SUBS, MEAN_FIELDS, mean_words)
-    gather_fields(
-        row, HARM_FIELDS, 2 * rim_rows, words_ref, groups * LANES, index_ref, weight_ref, unit,
-        lambda r, at: acc_ref[r, at, :], full_ref, VARS,
-    )
-    values = gather_into(
-        row, MEAN_FIELDS, 2 * rim_rows, mean_words, groups * LANES, index_ref, weight_ref,
-        begin, count, mean_unit, [share_ref[r] for r in range(VARS)],
+    values = shared_rim(
+        place_ref, acc_ref, share_ref, rim, groups * LANES, index_ref, weight_ref, words_ref, mean_words, full_ref
     )
     mean_acc[...] = jnp.zeros(mean_acc.shape, F32)
     for r, value in enumerate(values):
@@ -367,37 +380,37 @@
 
 
 def close_kernel(
-    rim_a, rim_b, index_ref, weight_ref, jac_ref, step_ref, mean_base, harm_base,
+    rim, index_ref, weight_ref, jac_ref, step_ref, mean_base, harm_base, near_ref,
     mean_hbm, harm_hbm, full_ref, words_ref, mean_out, harm_out, sems, *, coeff,
 ):
     groups = mean_base.shape[1]
-    rim_rows = rim_a.shape[1]
-    unit = pack_table(rim_block(rim_a, rim_b), 2 * rim_rows // SUBS, ALL_FIELDS, words_ref)
-    gather_fields(
-        rim_row(rim_a, rim_b), ALL_FIELDS, 2 * rim_rows, words_ref, groups * LANES, index_ref, weight_ref, unit,
-        zero_start, full_ref,
-    )
+    rows = rim.shape[1]
+    unit = pack_table(rim_block(rim), rows // SUBS, ALL_FIELDS, words_ref)
     base = fields_block(mean_base, harm_base)
+    copies = []
     for g in range(groups // SUBS):
         at = slice(g * SUBS, (g + 1) * SUBS)
+        full = gather_into(
+            rim_row(rim), ALL_FIELDS, rows, words_ref, groups * LANES, index_ref, weight_ref, g * FACES, FACES,
+            unit, [near_ref[r, at, :] for r in ALL_FIELDS],
+        )
         scale = coeff * step_ref[at, :]
         for first in range(0, ROWS, VARS):
-            values = [full_ref[first + v, at, :] for v in range(VARS)]
-            for v, res in enumerate(transposed(jac_ref, at, values)):
+            for v, res in enumerate(transposed(jac_ref, at, full[first : first + VARS])):
                 full_ref[first + v, at, :] = base(first + v, g) + scale * res
-    for t in range(groups):
-        lanes = slice(t * LANES, (t + 1) * LANES)
-        mean_out[:, lanes] = stacked(lambda i: full_ref[i, t : t + 1, :], VARS)
-    mean_copy = pltpu.make_async_copy(mean_out, mean_hbm, sems.at[0])
-    mean_copy.start()
-    for t in range(groups):
-        lanes = slice(t * LANES, (t + 1) * LANES)
-        for v in range(VARS):
-            harm_out[v, :, lanes] = stacked(lambda i: full_ref[(i + 1) * VARS + v, t : t + 1, :], 2)
-    harm_copy = pltpu.make_async_copy(harm_out, harm_hbm, sems.at[1])
-    harm_copy.start()
-    mean_copy.wait()
-    harm_copy.wait()
+        for t in range(g * SUBS, (g + 1) * SUBS):
+            lanes = slice(t * LANES, (t + 1) * LANES)
+            mean_out[:, lanes] = stacked(lambda i: full_ref[i, t : t + 1, :], VARS)
+            for v in range(VARS):
+                harm_out[v, :, lanes] = stacked(lambda i: full_ref[(i + 1) * VARS + v, t : t + 1, :], 2)
+        part = pl.ds(g * SUBS * LANES, SUBS * LANES)
+        for i, (out, hbm) in enumerate(
+            ((mean_out.at[:, part], mean_hbm.at[:, part]), (harm_out.at[:, :, part], harm_hbm.at[:, :, part]))
+        ):
+            copies.append(pltpu.make_async_copy(out, hbm, sems.at[2 * g + i]))
+            copies[-1].start()
+    for copy in copies:
+        copy.wait()
 
 
 def stacked(row, count):
@@ -412,13 +425,12 @@
     return [*(pltpu.VMEM(a.shape, a.dtype) for a in arrays), pltpu.SemaphoreType.DMA((SUBS,))]
 
 
-def launch(body, name, out_shape, scalars, args, raw=(), scratch=()):
+def launch(body, out_shape, scalars, args, raw=(), scratch=()):
     smem = pl.BlockSpec(memory_space=pltpu.SMEM)
     vmem = pl.BlockSpec(memory_space=pltpu.VMEM)
     anywhere = pl.BlockSpec(memory_space=pl.ANY)
     return pl.pallas_call(
         body,
-        name=name,
         out_shape=out_shape,
         in_specs=[smem] * len(scalars) + [anywhere] * len(raw) + [vmem] * len(args),
         out_specs=[anywhere if isinstance(s, jax.ShapeDtypeStruct) else vmem for s in out_shape],
@@ -430,7 +442,9 @@
     count = lax.axis_size("cells")
     near = [(b, b ^ 1) for b in range(count)]
     far = [(b, (b - 1 + 2 * (b % 2)) % count) for b in range(count)]
-    return lax.ppermute(pay_a, "cells", far), lax.ppermute(pay_b, "cells", near)
+    rim_a = lax.ppermute(pay_a, "cells", far)
+    rim_b = lax.ppermute(pay_b, "cells", near)
+    return rim_a, rim_b
 
 
 def shards(
@@ -461,7 +475,7 @@
     )
     held_raw = tuple(struct(*a.shape, dtype=a.dtype) for a in raw)
     pay_a, pay_b, tile_idx, *inside, step = launch(
-        open_kernel, "open", pays + (struct(2, rim_rows, LANES, dtype=jnp.int32),) + held_raw, (place,), (),
+        open_kernel, pays + (struct(2, rim_rows, LANES, dtype=jnp.int32),) + held_raw, (place,), (),
         (face_tiles, *raw), [pltpu.VMEM(face_tiles.shape, jnp.int32), pltpu.SemaphoreType.DMA((9,))],
     )
     rim_a, rim_b = exchange(pay_a, pay_b)
@@ -469,7 +483,7 @@
     words = lambda fields: struct(max(len(fields) // 3 * 2, 1), groups, LANES, dtype=jnp.int32)
     harm_words, mean_words = words(HARM_FIELDS), words(MEAN_FIELDS)
     acc, share, index, weight, wsum, mean_start, harm_start, jac, flow, source = launch(
-        prepare_kernel, "prepare",
+        prepare_kernel,
         (
             harm_fields,
             struct(VARS, SUBS, LANES),
@@ -485,27 +499,30 @@
         (place,), inside,
         scratch=[harm_words, mean_words],
     )
+    acc, share = launch(
+        near_share_kernel, (harm_fields, struct(VARS, SUBS, LANES)), (place,),
+        (acc, share, rim_b, index, weight), scratch=[harm_words, mean_words],
+    )
     state, part = launch(
-        lambda *refs: middle_kernel(*refs, coeff=1.0 / SECTIONS), "middle", (harm_fields, harm_fields),
+        lambda *refs: middle_kernel(*refs, coeff=1.0 / SECTIONS), (harm_fields, harm_fields),
         (place, harm_order),
-        (acc, share, rim_a, rim_b, index, weight, wsum, mean_start, harm_start, jac, flow, source, step),
+        (acc, share, rim_a, index, weight, wsum, mean_start, harm_start, jac, flow, source, step),
         scratch=[harm_fields, mean_fields, harm_words, mean_words],
     )
     parts = lax.all_gather(part, HARM)
-    mean, stress, pay_a, pay_b = launch(
-        join_kernel, "join", (mean_fields, mean_fields) + pays, (), (parts, state, tile_idx)
-    )
+    mean, stress, pay_a, pay_b = launch(join_kernel, (mean_fields, mean_fields) + pays, (), (parts, state, tile_idx))
     rim_a, rim_b = exchange(pay_a, pay_b)
     fields = struct(ROWS, groups, LANES)
     mean_base, harm_base = launch(
-        lambda *refs: own_kernel(*refs, coeff=1.0), "own", (mean_fields, harm_fields), (harm_order,),
+        lambda *refs: own_kernel(*refs, coeff=1.0), (mean_fields, harm_fields), (harm_order,),
         (index, weight, wsum, mean, state, mean_start, harm_start, jac, flow, source, step, stress),
         scratch=[fields, words(ALL_FIELDS)],
     )
+    (near,) = launch(near_kernel, (fields,), (), (rim_b, index, weight), scratch=[words(ALL_FIELDS)])
     outs = [jax.ShapeDtypeStruct(s, F32) for s in ((VARS, cells), (VARS, 2, cells))]
     mean_new, harm_new = launch(
-        lambda *refs: close_kernel(*refs, coeff=1.0), "close", tuple(outs), (),
-        (rim_a, rim_b, index, weight, jac, step, mean_base, harm_base),
+        lambda *refs: close_kernel(*refs, coeff=1.0), tuple(outs), (),
+        (rim_a, index, weight, jac, step, mean_base, harm_base, near),
         scratch=[fields, words(ALL_FIELDS), *held(*outs)],
     )
     return mean_new, harm_new.swapaxes(0, 1)[None]

time: 48 us -> 48.8 us (1.017); the launches traced: 47.1 us -> 48.5 us
  starting transfers between devices: 23.1 us -> 26.4 us
  waiting for transfers between devices: 1.58 us -> 0.01 us
  blocking collectives: 9.4 us -> 8.54 us
  Pallas kernels: 11.7 us -> 12.2 us
    ppermute x4, starting transfers between devices: 23.1 us -> 26.4 us  [the longest x2 20.4 us: exchange(): rim_a = lax.ppermute(pay_a, 'cells', far)]
    ppermute x4, waiting for transfers between devices: 1.58 us -> 0.01 us  [the longest x2 0.01 us: exchange(): rim_a = lax.ppermute(pay_a, 'cells', far)]
    all_gather x1, blocking collectives: 9.4 us -> 8.54 us  [shards(): parts = lax.all_gather(part, HARM)]
    pallas_call x6 -> x8, Pallas kernels: 11.7 us -> 12.2 us  [launch(): pl.pallas_call(body, out_shape=out_shape, in_specs=[smem] * len(scalars)...]
  transfers between devices with their start and end apart: 4 -> 4, of which waited for: 2 -> 0; matrix products, arithmetic and copies ran while one was open for 0% -> 0% of each run, Pallas kernels for 9% -> 14%
where the time goes in v6:
time: 48.8 us; the launch traced here: 48.5 us
  starting transfers between devices  26.4 us (54%)
  Pallas kernels  12.2 us (25%)
  blocking collectives  8.54 us (18%)
  between operations  1.41 us (3%)
    ppermute x2, starting transfers between devices, exchange(): rim_a = lax.ppermute(pay_a, 'cells', far)  20.4 us
    pallas_call x8, Pallas kernels, launch(): pl.pallas_call(body, out_shape=out_shape, in_specs=[smem] * len(scalars)...  12.2 us
    all_gather x1, blocking collectives, shards(): parts = lax.all_gather(part, HARM)  8.54 us
    ppermute x2, starting transfers between devices, exchange(): rim_b = lax.ppermute(pay_b, 'cells', near)  5.94 us
  transfers between devices with their start and end apart: 4, of which 0 were waited for; matrix products, arithmetic and copies ran while one was open for 0% of the time, Pallas kernels for 14%

profile of v6, /device:TPU:1, one launch (start us, length us, event | category | flops | bytes accessed | tf_op | source)
XLA Modules:
  0.0 48.5 jit_solution(622855027793584031)
XLA Ops:
  0.6 1.6 %shard_map.113 = (f32[15,8,128]{2,1,0:T(8,128)S(1)}, f32[15,8,128]{2,1,0:T(8,128)S(1)}, s32[2,8,128]{2,1,0:T(8,128)S(1)}, f32[5,2048]{1,0:T(8,128)S(1)}, f32[5,2...) custom-call(s32[1]{0:T(128)} %bitcast.place_ref.refs_0_, ...), custom_call_target="tpu_custom_call" | custom-call | tf_op jit(solution)/shard_map/pallas_call | solution.py:432
  2.3 4.0 %collective-permute-start = (f32[15,8,128]{2,1,0:T(8,128)S(1)}, f32[15,8,128]{2,1,0:T(8,128)S(1)}, u32[]{:S(2)}, u32[]{:S(2)}) collective-permute-start(f32[15,8,128]{2,1,0:T(8,128)S(1)} %get-tuple-element.44), channel_id=1, source_target_pairs={{0,4},{4,0},{8,12},{12,8},{16,20},{20,16},{24,28},{28,24},{32,36},... | collective-permute-start | bytes 184328 | tf_op jit(solution)/shard_map/ppermute | solution.py:446
  6.3 14.3 %collective-permute-start.1 = (f32[15,8,128]{2,1,0:T(8,128)S(1)}, f32[15,8,128]{2,1,0:T(8,128)S(1)}, u32[]{:S(2)}, u32[]{:S(2)}) collective-permute-start(f32[15,8,128]{2,1,0:T(8,128)S(1)} %get-tuple-element.49), channel_id=1, source_target_pairs={{0,508},{4,8},{8,4},{12,16},{16,12},{20,24},{24,20},{28,32},{32,28... | collective-permute-start | bytes 184328 | tf_op jit(solution)/shard_map/ppermute | solution.py:445
  21.2 2.1 %shard_map.114 = (f32[10,16,128]{2,1,0:T(8,128)S(1)}, f32[5,8,128]{2,1,0:T(8,128)S(1)}, s32[12,8,128]{2,1,0:T(8,128)S(1)}, f32[12,8,128]{2,1,0:T(8,128)S(1)}, f3...) custom-call(s32[1]{0:T(128)} %bitcast.place_ref.refs_0_, ...), custom_call_target="tpu_custom_call" | custom-call | tf_op jit(solution)/shard_map/pallas_call | solution.py:432
  23.4 0.0 collective-permute-done.rim
  23.4 1.1 %shard_map.115 = (f32[10,16,128]{2,1,0:T(8,128)S(1)}, f32[5,8,128]{2,1,0:T(8,128)S(1)}) custom-call(s32[1]{0:T(128)} %bitcast.place_ref.refs_0_, f32[10,16,128]{2,1,0:T(8,128)S(1)} %get-tuple-element.42.acc_ref, f32[5,8,128]{2,1,0:T(8,128)S(1)} %get-tuple-element.43.share_ref, f32[15,8,128]{2,1,0:T(8,128)S(1)} %collective-permute-done.rim, ...), custom_call_target="tpu_custom_call" | custom-call | tf_op jit(solution)/shard_map/pallas_call | solution.py:432
  24.5 0.0 collective-permute-done.1.refs_4_
  24.5 1.1 %shard_map.116 = (f32[10,16,128]{2,1,0:T(8,128)S(1)}, f32[10,16,128]{2,1,0:T(8,128)S(1)}) custom-call(s32[1]{0:T(128)} %bitcast.place_ref.refs_0_, s32[1]{0:T(128)S(6)} %copy.12.refs_1_.refs_0_, f32[10,16,128]{2,1,0:T(8,128)S(1)} %get-tuple-element.47.refs_2_, f32[5,8,128]{2,1,0:T(8,128)S(1)} %get-tuple-element.48.refs_3_, ...), custom_call_target="tpu_custom_call" | custom-call | tf_op jit(solution)/shard_map/pallas_call | solution.py:432
  25.6 8.5 %all-gather = f32[40,16,128]{2,1,0:T(8,128)S(1)} all-gather(f32[10,16,128]{2,1,0:T(8,128)S(1)} %get-tuple-element.57), channel_id=2, replica_groups=mesh['cells'=128,'harm_0'=2,'harm_1'=2] {'harm_0','harm_1'}, dimensions={0}, use_global_device_ids=true | all-gather | bytes 409600 | tf_op jit(solution)/shard_map/all_gather | solution.py:512
  34.2 0.6 %shard_map.117 = (f32[5,16,128]{2,1,0:T(8,128)S(1)}, f32[5,16,128]{2,1,0:T(8,128)S(1)}, f32[15,8,128]{2,1,0:T(8,128)S(1)}, f32[15,8,128]{2,1,0:T(8,128)S(1)}) custom-call(f32[4,10,16,128]{3,2,1,0:T(8,128)S(1)} %bitcast.12, f32[10,16,128]{2,1,0:T(8,128)S(1)} %get-tuple-element.58.state_ref.refs_5_, s32[2,8,128]{2,1,0:T(8,128)S(1)} %get-tuple-element.59.tile_idx), custom_call_target="tpu_custom_call" | custom-call | tf_op jit(solution)/shard_map/pallas_call | solution.py:432
  34.8 1.9 %collective-permute-start.3 = (f32[15,8,128]{2,1,0:T(8,128)S(1)}, f32[15,8,128]{2,1,0:T(8,128)S(1)}, u32[]{:S(2)}, u32[]{:S(2)}) collective-permute-start(f32[15,8,128]{2,1,0:T(8,128)S(1)} %get-tuple-element.65), channel_id=1, source_target_pairs={{0,4},{4,0},{8,12},{12,8},{16,20},{20,16},{24,28},{28,24},{32,36},... | collective-permute-start | bytes 184328 | tf_op jit(solution)/shard_map/ppermute | solution.py:446
  36.7 6.2 %collective-permute-start.2 = (f32[15,8,128]{2,1,0:T(8,128)S(1)}, f32[15,8,128]{2,1,0:T(8,128)S(1)}, u32[]{:S(2)}, u32[]{:S(2)}) collective-permute-start(f32[15,8,128]{2,1,0:T(8,128)S(1)} %get-tuple-element.60), channel_id=1, source_target_pairs={{0,508},{4,8},{8,4},{12,16},{16,12},{20,24},{24,20},{28,32},{32,28... | collective-permute-start | bytes 184328 | tf_op jit(solution)/shard_map/ppermute | solution.py:445
  42.9 2.3 %shard_map.118 = (f32[5,16,128]{2,1,0:T(8,128)S(1)}, f32[10,16,128]{2,1,0:T(8,128)S(1)}) custom-call(s32[1]{0:T(128)S(6)} %copy.12.refs_1_.refs_0_, s32[12,8,128]{2,1,0:T(8,128)S(1)} %get-tuple-element.45.index_ref.refs_5_.refs_1_, f32[12,8,128]{2,1,0:T(8,128)S(1)} %get-tuple-element.46.weight_ref.refs_6_.refs_2_, ...), custom_call_target="tpu_custom_call" | custom-call | tf_op jit(solution)/shard_map/pallas_call | solution.py:432
  45.2 0.0 collective-permute-done.3.rim
  45.2 1.3 %shard_map.119.refs_7_ = f32[15,16,128]{2,1,0:T(8,128)S(1)} custom-call(f32[15,8,128]{2,1,0:T(8,128)S(1)} %collective-permute-done.3.rim, s32[12,8,128]{2,1,0:T(8,128)S(1)} %get-tuple-element.45.index_ref.refs_5_.refs_1_, f32[12,8,128]{2,1,0:T(8,128)S(1)} %get-tuple-element.46.weight_ref.refs_6_.refs_2_), custom_call_target="tpu_custom_call" | custom-call | tf_op jit(solution)/shard_map/pallas_call | solution.py:432
  46.5 0.0 collective-permute-done.2.refs_0_
  46.5 2.0 %shard_map.120 = (f32[5,2048]{1,0:T(8,128)}, f32[5,2,2048]{2,1,0:T(2,128)}) custom-call(f32[15,8,128]{2,1,0:T(8,128)S(1)} %collective-permute-done.2.refs_0_, s32[12,8,128]{2,1,0:T(8,128)S(1)} %get-tuple-element.45.index_ref.refs_5_.refs_1_, f32[12,8,128]{2,1,0:T(8,128)S(1)} %get-tuple-element.46.weight_ref.refs_6_.refs_2_, ...), custom_call_target="tpu_custom_call" | custom-call | tf_op jit(solution)/shard_map/pallas_call | solution.py:432
Async XLA Ops:
  2.3 21.1 %collective-permute-start = (f32[15,8,128]{2,1,0:T(8,128)S(1)}, f32[15,8,128]{2,1,0:T(8,128)S(1)}, u32[]{:S(2)}, u32[]{:S(2)}) collective-permute-start(f32[15,8,128]{2,1,0:T(8,128)S(1)} %get-tuple-element.44), channel_id=1, source_target_pairs={{0,4},{4,0},{8,12},{12,8},{16,20},{20,16},{24,28},{28,24},{32,36},... | collective-permute-start | bytes 184328 | tf_op jit(solution)/shard_map/ppermute | solution.py:446
  6.3 18.1 %collective-permute-start.1 = (f32[15,8,128]{2,1,0:T(8,128)S(1)}, f32[15,8,128]{2,1,0:T(8,128)S(1)}, u32[]{:S(2)}, u32[]{:S(2)}) collective-permute-start(f32[15,8,128]{2,1,0:T(8,128)S(1)} %get-tuple-element.49), channel_id=1, source_target_pairs={{0,508},{4,8},{8,4},{12,16},{16,12},{20,24},{24,20},{28,32},{32,28... | collective-permute-start | bytes 184328 | tf_op jit(solution)/shard_map/ppermute | solution.py:445
  34.8 10.5 %collective-permute-start.3 = (f32[15,8,128]{2,1,0:T(8,128)S(1)}, f32[15,8,128]{2,1,0:T(8,128)S(1)}, u32[]{:S(2)}, u32[]{:S(2)}) collective-permute-start(f32[15,8,128]{2,1,0:T(8,128)S(1)} %get-tuple-element.65), channel_id=1, source_target_pairs={{0,4},{4,0},{8,12},{12,8},{16,20},{20,16},{24,28},{28,24},{32,36},... | collective-permute-start | bytes 184328 | tf_op jit(solution)/shard_map/ppermute | solution.py:446
  36.7 9.8 %collective-permute-start.2 = (f32[15,8,128]{2,1,0:T(8,128)S(1)}, f32[15,8,128]{2,1,0:T(8,128)S(1)}, u32[]{:S(2)}, u32[]{:S(2)}) collective-permute-start(f32[15,8,128]{2,1,0:T(8,128)S(1)} %get-tuple-element.60), channel_id=1, source_target_pairs={{0,508},{4,8},{8,4},{12,16},{16,12},{20,24},{24,20},{28,32},{32,28... | collective-permute-start | bytes 184328 | tf_op jit(solution)/shard_map/ppermute | solution.py:445

commit v7 on v6

--- a/solution.py
+++ b/solution.py
@@ -14,7 +14,6 @@
 HARM_FIELDS = range(VARS, ROWS)
 ALL_FIELDS = range(ROWS)
 HARM = ("harm_0", "harm_1")
-HARM_DEVICES = 4
 LANES = 128
 SUBS = 8
 BASE_FREQ = 0.8
@@ -74,13 +73,13 @@
 
 
 def open_kernel(
-    place_ref, tiles_hbm, mean_hbm, harm_hbm, links_hbm, weight_hbm, flow_hbm, jac_hbm, source_hbm, step_hbm,
-    pay_a, pay_b, tile_idx, mean_ref, harm_ref, links_ref, weight_ref, flow_ref, jac_ref, source_ref, step_ref,
-    tiles_ref, sems,
+    place_ref, tiles_hbm, mean_hbm, harm_hbm, flow_hbm, links_hbm, weight_hbm, jac_hbm, source_hbm, step_hbm,
+    pay_a, pay_b, stress_ref, tile_idx, mean_ref, harm_ref, flow_ref, links_ref, weight_ref, jac_ref, source_ref,
+    step_ref, tiles_ref, sems,
 ):
     waits = fetch(
-        (tiles_hbm, mean_hbm, harm_hbm, links_hbm, weight_hbm, flow_hbm, jac_hbm, source_hbm, step_hbm),
-        (tiles_ref, mean_ref, harm_ref, links_ref, weight_ref, flow_ref, jac_ref, source_ref, step_ref),
+        (tiles_hbm, mean_hbm, harm_hbm, flow_hbm, links_hbm, weight_hbm, jac_hbm, source_hbm, step_hbm),
+        (tiles_ref, mean_ref, harm_ref, flow_ref, links_ref, weight_ref, jac_ref, source_ref, step_ref),
         sems,
     )
     for wait in waits[:3]:
@@ -94,8 +93,17 @@
     tile_idx[0] = first
     tile_idx[1] = second
     row = native_row(mean_ref, harm_ref)
-    store_tiles(row, (first, second), pay_a, pay_b, mean_ref.shape[1] // LANES)
-    for wait in waits[3:]:
+    groups = mean_ref.shape[1] // LANES
+    store_tiles(row, (first, second), pay_a, pay_b, groups)
+    waits[3]()
+    flow = native_row(mean_ref, flow_ref)
+    product = lambda r, t: row(r, t) * flow(r, t)
+    for v in range(VARS):
+        for g in range(0, groups, SUBS):
+            stress_ref[v, g : g + SUBS, :] = packed(
+                lambda t: product(VARS + v, t) + product(2 * VARS + v, t), g
+            )
+    for wait in waits[4:]:
         wait()
 
 
@@ -155,10 +163,8 @@
     ]
 
 
-def share_of(place_ref, index_ref):
-    count = index_ref.shape[0] // HARM_DEVICES
-    begin = place_ref[0] // 2 * count
-    return begin, count, begin // FACES
+def core_of(place_ref):
+    return place_ref[0] // 2
 
 
 def gather_fields(row, fields, count, words_ref, first, index_ref, weight_ref, unit, start, out_ref, lead=0):
@@ -177,7 +183,7 @@
 
 
 def prepare_kernel(
-    place_ref, mean_ref, harm_ref, links_ref, weight_in, flow_ref, jac_ref, source_ref,
+    place_ref, mean_ref, harm_ref, flow_ref, links_ref, weight_in, jac_ref, source_ref,
     acc_ref, share_ref, index_ref, weight_ref, wsum_ref, mean_out, state_ref, jac_out, flow_out, source_out,
     words_ref, mean_words,
 ):
@@ -210,9 +216,8 @@
     gather_fields(
         row, HARM_FIELDS, groups, words_ref, 0, index_ref, weight_ref, unit, zero_start, acc_ref, VARS
     )
-    begin, count, _ = share_of(place_ref, index_ref)
     values = gather_into(
-        row, MEAN_FIELDS, groups, mean_words, 0, index_ref, weight_ref, begin, count, mean_unit,
+        row, MEAN_FIELDS, groups, mean_words, 0, index_ref, weight_ref, core_of(place_ref) * FACES, FACES, mean_unit,
         [zero_start()] * VARS,
     )
     for r, value in enumerate(values):
@@ -243,39 +248,14 @@
     return load
 
 
-def rim_row(rim):
-    return lambda r, h: rim[r, h : h + 1, :]
-
-
-def rim_block(rim):
-    return lambda r, g: rim[r, g * SUBS : (g + 1) * SUBS, :]
-
-
-def shared_rim(place_ref, acc_ref, share_ref, rim, first, index_ref, weight_ref, words_ref, mean_words, out_ref):
-    rows = rim.shape[1]
-    row, load = rim_row(rim), rim_block(rim)
-    unit = pack_table(load, rows // SUBS, HARM_FIELDS, words_ref)
-    mean_unit = pack_table(load, rows // SUBS, MEAN_FIELDS, mean_words)
-    gather_fields(
-        row, HARM_FIELDS, rows, words_ref, first, index_ref, weight_ref, unit,
-        lambda r, at: acc_ref[r, at, :], out_ref, VARS,
-    )
-    begin, count, _ = share_of(place_ref, index_ref)
-    return gather_into(
-        row, MEAN_FIELDS, rows, mean_words, first, index_ref, weight_ref,
-        begin, count, mean_unit, [share_ref[r] for r in range(VARS)],
-    )
-
-
-def near_share_kernel(
-    place_ref, acc_ref, share_ref, rim, index_ref, weight_ref, out_ref, share_out, words_ref, mean_words
-):
-    first = (acc_ref.shape[1] + rim.shape[1]) * LANES
-    values = shared_rim(
-        place_ref, acc_ref, share_ref, rim, first, index_ref, weight_ref, words_ref, mean_words, out_ref
-    )
-    for r, value in enumerate(values):
-        share_out[r] = value
+def rim_row(*rims):
+    rows = rims[0].shape[1]
+    return lambda r, h: rims[h // rows][r, h % rows : h % rows + 1, :]
+
+
+def rim_block(*rims):
+    blocks = rims[0].shape[1] // SUBS
+    return lambda r, g: rims[g // blocks][r, g % blocks * SUBS : (g % blocks + 1) * SUBS, :]
 
 
 def near_kernel(rim, index_ref, weight_ref, out_ref, words_ref):
@@ -311,14 +291,23 @@
 
 
 def middle_kernel(
-    place_ref, order_ref, acc_ref, share_ref, rim, index_ref, weight_ref, wsum_ref, mean_ref, state_ref,
+    place_ref, order_ref, acc_ref, share_ref, rim_a, rim_b, stress_a, stress_b, index_ref, weight_ref, wsum_ref, mean_ref, state_ref,
     jac_ref, flow_ref, source_ref, step_ref, out_ref, part_ref, full_ref, mean_acc, words_ref, mean_words, *, coeff,
 ):
     groups = acc_ref.shape[1]
-    _, _, half = share_of(place_ref, index_ref)
-    lead = place_ref[0] // 2 == 0
-    values = shared_rim(
-        place_ref, acc_ref, share_ref, rim, groups * LANES, index_ref, weight_ref, words_ref, mean_words, full_ref
+    rows = 2 * rim_a.shape[1]
+    row, load = rim_row(rim_a, rim_b), rim_block(rim_a, rim_b)
+    unit = pack_table(load, rows // SUBS, HARM_FIELDS, words_ref)
+    mean_unit = pack_table(load, rows // SUBS, MEAN_FIELDS, mean_words)
+    gather_fields(
+        row, HARM_FIELDS, rows, words_ref, groups * LANES, index_ref, weight_ref, unit,
+        lambda r, at: acc_ref[r, at, :], full_ref, VARS,
+    )
+    half = core_of(place_ref)
+    lead = half == 0
+    values = gather_into(
+        row, MEAN_FIELDS, rows, mean_words, groups * LANES, index_ref, weight_ref, half * FACES, FACES,
+        mean_unit, [share_ref[r] for r in range(VARS)],
     )
     mean_acc[...] = jnp.zeros(mean_acc.shape, F32)
     for r, value in enumerate(values):
@@ -331,7 +320,7 @@
         scale = coeff * step_ref[at, :]
         flux = []
         for v in range(VARS):
-            stress = state[v] * flow_ref[v, at, :] + state[VARS + v] * flow_ref[VARS + v, at, :]
+            stress = stress_a[v, at, :] + stress_b[v, at, :]
             flux.append(jnp.where(lead, wsum * mean[v], 0.0) - mean_acc[v, at, :] - stress)
         for v, res in enumerate(transposed(jac_ref, at, flux)):
             own = jnp.where(lead, mean[v] + scale * source_ref[v, at, :], 0.0)
@@ -347,17 +336,14 @@
 def join_kernel(parts_ref, state_ref, tile_idx, mean_ref, stress_ref, pay_a, pay_b):
     for v in range(VARS):
         for ref, r in ((mean_ref, v), (stress_ref, VARS + v)):
-            total = parts_ref[0, r]
-            for k in range(1, HARM_DEVICES):
-                total = total + parts_ref[k, r]
-            ref[v] = total
+            ref[v] = parts_ref[0, r] + parts_ref[1, r]
     row = fields_row(mean_ref, state_ref)
     store_tiles(row, (tile_idx[0], tile_idx[1]), pay_a, pay_b, mean_ref.shape[1])
 
 
 def own_kernel(
     order_ref, index_ref, weight_ref, wsum_ref, mean_ref, state_ref, mean_start, harm_start,
-    jac_ref, flow_ref, source_ref, step_ref, stress_ref, mean_base, harm_base, full_ref, words_ref, *, coeff,
+    jac_ref, flow_ref, source_ref, step_ref, mean_base, harm_base, full_ref, words_ref, *, coeff,
 ):
     groups = mean_ref.shape[1]
     unit = pack_table(fields_block(mean_ref, state_ref), groups // SUBS, ALL_FIELDS, words_ref)
@@ -371,7 +357,7 @@
         state = [state_ref[r, at, :] for r in range(2 * VARS)]
         wsum = wsum_ref[at, :]
         scale = coeff * step_ref[at, :]
-        flux = [wsum * m - full_ref[v, at, :] - stress_ref[v, at, :] for v, m in enumerate(mean)]
+        flux = [wsum * m - full_ref[v, at, :] for v, m in enumerate(mean)]
         for v, res in enumerate(transposed(jac_ref, at, flux)):
             mean_base[v, at, :] = mean_start[v, at, :] - scale * (res - source_ref[v, at, :])
         gathered = [full_ref[VARS + r, at, :] for r in range(2 * VARS)]
@@ -380,7 +366,7 @@
 
 
 def close_kernel(
-    rim, index_ref, weight_ref, jac_ref, step_ref, mean_base, harm_base, near_ref,
+    rim, index_ref, weight_ref, jac_ref, step_ref, mean_base, harm_base, near_ref, stress_a, stress_b,
     mean_hbm, harm_hbm, full_ref, words_ref, mean_out, harm_out, sems, *, coeff,
 ):
     groups = mean_base.shape[1]
@@ -394,6 +380,8 @@
             rim_row(rim), ALL_FIELDS, rows, words_ref, groups * LANES, index_ref, weight_ref, g * FACES, FACES,
             unit, [near_ref[r, at, :] for r in ALL_FIELDS],
         )
+        for v in range(VARS):
+            full[v] = full[v] + (stress_a[v, at, :] + stress_b[v, at, :])
         scale = coeff * step_ref[at, :]
         for first in range(0, ROWS, VARS):
             for v, res in enumerate(transposed(jac_ref, at, full[first : first + VARS])):
@@ -438,13 +426,14 @@
     )(*scalars, *raw, *(pltpu.with_memory_space_constraint(a, pltpu.VMEM) for a in args))
 
 
-def exchange(pay_a, pay_b):
+def exchange(pay_a, pay_b, stress):
     count = lax.axis_size("cells")
     near = [(b, b ^ 1) for b in range(count)]
     far = [(b, (b - 1 + 2 * (b % 2)) % count) for b in range(count)]
     rim_a = lax.ppermute(pay_a, "cells", far)
     rim_b = lax.ppermute(pay_b, "cells", near)
-    return rim_a, rim_b
+    other = lax.ppermute(stress, HARM[0], [(0, 1), (1, 0)])
+    return rim_a, rim_b, other
 
 
 def shards(
@@ -466,19 +455,19 @@
     harm_adjoint, harm_flow = (
         a[0].swapaxes(0, 1) for a in (harm_adjoint, harm_flow)
     )
-    place = (1 - lax.axis_index("cells") % 2 + 2 * lax.axis_index(HARM)).astype(jnp.int32)[None]
+    place = (1 - lax.axis_index("cells") % 2 + 2 * lax.axis_index(HARM[1])).astype(jnp.int32)[None]
     step = pseudo_step.reshape(groups, LANES)
     mean_fields, harm_fields = struct(VARS, groups, LANES), struct(2 * VARS, groups, LANES)
     pays = (struct(ROWS, rim_rows, LANES), struct(ROWS, rim_rows, LANES))
     raw = (
-        mean_adjoint, harm_adjoint, face_links, face_weight, harm_flow, flux_jacobian, mean_source, step
+        mean_adjoint, harm_adjoint, harm_flow, face_links, face_weight, flux_jacobian, mean_source, step
     )
     held_raw = tuple(struct(*a.shape, dtype=a.dtype) for a in raw)
-    pay_a, pay_b, tile_idx, *inside, step = launch(
-        open_kernel, pays + (struct(2, rim_rows, LANES, dtype=jnp.int32),) + held_raw, (place,), (),
+    pay_a, pay_b, stress, tile_idx, *inside, step = launch(
+        open_kernel, pays + (mean_fields, struct(2, rim_rows, LANES, dtype=jnp.int32),) + held_raw, (place,), (),
         (face_tiles, *raw), [pltpu.VMEM(face_tiles.shape, jnp.int32), pltpu.SemaphoreType.DMA((9,))],
     )
-    rim_a, rim_b = exchange(pay_a, pay_b)
+    rim_a, rim_b, other = exchange(pay_a, pay_b, stress)
     registers = FACES * halves
     words = lambda fields: struct(max(len(fields) // 3 * 2, 1), groups, LANES, dtype=jnp.int32)
     harm_words, mean_words = words(HARM_FIELDS), words(MEAN_FIELDS)
@@ -499,30 +488,26 @@
         (place,), inside,
         scratch=[harm_words, mean_words],
     )
-    acc, share = launch(
-        near_share_kernel, (harm_fields, struct(VARS, SUBS, LANES)), (place,),
-        (acc, share, rim_b, index, weight), scratch=[harm_words, mean_words],
-    )
     state, part = launch(
         lambda *refs: middle_kernel(*refs, coeff=1.0 / SECTIONS), (harm_fields, harm_fields),
         (place, harm_order),
-        (acc, share, rim_a, index, weight, wsum, mean_start, harm_start, jac, flow, source, step),
+        (acc, share, rim_a, rim_b, stress, other, index, weight, wsum, mean_start, harm_start, jac, flow, source, step),
         scratch=[harm_fields, mean_fields, harm_words, mean_words],
     )
-    parts = lax.all_gather(part, HARM)
+    parts = lax.all_gather(part, HARM[1])
     mean, stress, pay_a, pay_b = launch(join_kernel, (mean_fields, mean_fields) + pays, (), (parts, state, tile_idx))
-    rim_a, rim_b = exchange(pay_a, pay_b)
+    rim_a, rim_b, other = exchange(pay_a, pay_b, stress)
     fields = struct(ROWS, groups, LANES)
     mean_base, harm_base = launch(
         lambda *refs: own_kernel(*refs, coeff=1.0), (mean_fields, harm_fields), (harm_order,),
-        (index, weight, wsum, mean, state, mean_start, harm_start, jac, flow, source, step, stress),
+        (index, weight, wsum, mean, state, mean_start, harm_start, jac, flow, source, step),
         scratch=[fields, words(ALL_FIELDS)],
     )
     (near,) = launch(near_kernel, (fields,), (), (rim_b, index, weight), scratch=[words(ALL_FIELDS)])
     outs = [jax.ShapeDtypeStruct(s, F32) for s in ((VARS, cells), (VARS, 2, cells))]
     mean_new, harm_new = launch(
         lambda *refs: close_kernel(*refs, coeff=1.0), tuple(outs), (),
-        (rim_a, index, weight, jac, step, mean_base, harm_base, near),
+        (rim_a, index, weight, jac, step, mean_base, harm_base, near, stress, other),
         scratch=[fields, words(ALL_FIELDS), *held(*outs)],
     )
     return mean_new, harm_new.swapaxes(0, 1)[None]

time: 48.8 us -> 48.9 us (level)
  blocking collectives: 8.54 us -> 2.8 us
  starting transfers between devices: 26.4 us -> 32 us
    ppermute x0 -> x2, starting transfers between devices: none -> 8.72 us  [exchange(): other = lax.ppermute(stress, HARM[0], [(0, 1), (1, 0)])]
    all_gather x1, blocking collectives: 8.54 us -> 2.8 us  [shards(): parts = lax.all_gather(part, HARM[1])]
    ppermute x2, starting transfers between devices: 20.4 us -> 17.7 us  [exchange(): rim_a = lax.ppermute(pay_a, 'cells', far)]
    pallas_call x8 -> x7, Pallas kernels: 12.2 us -> 12.4 us  [launch(): pl.pallas_call(body, out_shape=out_shape, in_specs=[smem] * len(scalars)...]
  transfers between devices with their start and end apart: 4 -> 6, of which waited for: 0 -> 0; matrix products, arithmetic and copies ran while one was open for 0% -> 0% of each run, Pallas kernels for 14% -> 12%
where the time goes in v7:
time: 48.9 us; the launch traced here: 48.6 us
  starting transfers between devices  32 us (65%)
  Pallas kernels  12.4 us (25%)
  blocking collectives  2.8 us (6%)
  between operations  1.44 us (3%)
    ppermute x2, starting transfers between devices, exchange(): rim_a = lax.ppermute(pay_a, 'cells', far)  17.7 us
    pallas_call x7, Pallas kernels, launch(): pl.pallas_call(body, out_shape=out_shape, in_specs=[smem] * len(scalars)...  12.4 us
    ppermute x2, starting transfers between devices, exchange(): other = lax.ppermute(stress, HARM[0], [(0, 1), (1, 0)])  8.72 us
    ppermute x2, starting transfers between devices, exchange(): rim_b = lax.ppermute(pay_b, 'cells', near)  5.56 us
    all_gather x1, blocking collectives, shards(): parts = lax.all_gather(part, HARM[1])  2.8 us
  transfers between devices with their start and end apart: 6, of which 0 were waited for; matrix products, arithmetic and copies ran while one was open for 0% of the time, Pallas kernels for 12%

profile of v7, /device:TPU:1, one launch (start us, length us, event | category | flops | bytes accessed | tf_op | source)
XLA Modules:
  0.0 48.6 jit_solution(13031510359129707415)
XLA Ops:
  0.6 1.7 %shard_map.113 = (f32[15,8,128]{2,1,0:T(8,128)S(1)}, f32[15,8,128]{2,1,0:T(8,128)S(1)}, f32[5,16,128]{2,1,0:T(8,128)S(1)}, s32[2,8,128]{2,1,0:T(8,128)S(1)}, f32...) custom-call(s32[1]{0:T(128)} %bitcast.place_ref.refs_0_, ...), custom_call_target="tpu_custom_call" | custom-call | tf_op jit(solution)/shard_map/pallas_call | solution.py:420
  2.4 15.3 %collective-permute-start = (f32[15,8,128]{2,1,0:T(8,128)S(1)}, f32[15,8,128]{2,1,0:T(8,128)S(1)}, u32[]{:S(2)}, u32[]{:S(2)}) collective-permute-start(f32[15,8,128]{2,1,0:T(8,128)S(1)} %get-tuple-element.43), channel_id=1, source_target_pairs={{0,508},{4,8},{8,4},{12,16},{16,12},{20,24},{24,20},{28,32},{32,28... | collective-permute-start | bytes 184328 | tf_op jit(solution)/shard_map/ppermute | solution.py:433
  17.7 1.9 %collective-permute-start.1 = (f32[15,8,128]{2,1,0:T(8,128)S(1)}, f32[15,8,128]{2,1,0:T(8,128)S(1)}, u32[]{:S(2)}, u32[]{:S(2)}) collective-permute-start(f32[15,8,128]{2,1,0:T(8,128)S(1)} %get-tuple-element.44), channel_id=1, source_target_pairs={{0,4},{4,0},{8,12},{12,8},{16,20},{20,16},{24,28},{28,24},{32,36},... | collective-permute-start | bytes 184328 | tf_op jit(solution)/shard_map/ppermute | solution.py:434
  19.6 4.4 %collective-permute-start.2 = (f32[5,16,128]{2,1,0:T(8,128)S(1)}, f32[5,16,128]{2,1,0:T(8,128)S(1)}, u32[]{:S(2)}, u32[]{:S(2)}) collective-permute-start(f32[5,16,128]{2,1,0:T(8,128)S(1)} %get-tuple-element.45.refs_6_), channel_id=1, source_target_pairs={{0,2},{2,0},{1,3},{3,1},{4,6},{6,4},{5,7},{7,5},{8,10},{10,8},{9,1... | collective-permute-start | bytes 122888 | tf_op jit(solution)/shard_map/ppermute | solution.py:435
  24.6 2.3 %shard_map.114 = (f32[10,16,128]{2,1,0:T(8,128)S(1)}, f32[5,8,128]{2,1,0:T(8,128)S(1)}, s32[12,8,128]{2,1,0:T(8,128)S(1)}, f32[12,8,128]{2,1,0:T(8,128)S(1)}, f3...) custom-call(s32[1]{0:T(128)} %bitcast.place_ref.refs_0_, ...), custom_call_target="tpu_custom_call" | custom-call | tf_op jit(solution)/shard_map/pallas_call | solution.py:420
  26.9 0.0 collective-permute-done.2.refs_7_
  26.9 0.0 collective-permute-done.refs_4_
  27.0 0.0 collective-permute-done.1.refs_5_
  27.0 2.2 %shard_map.115 = (f32[10,16,128]{2,1,0:T(8,128)S(1)}, f32[10,16,128]{2,1,0:T(8,128)S(1)}) custom-call(s32[1]{0:T(128)} %bitcast.place_ref.refs_0_, s32[1]{0:T(128)S(6)} %copy.12.refs_1_.refs_0_, f32[10,16,128]{2,1,0:T(8,128)S(1)} %get-tuple-element.41.refs_2_, f32[5,8,128]{2,1,0:T(8,128)S(1)} %get-tuple-element.42.refs_3_, ...), custom_call_target="tpu_custom_call" | custom-call | tf_op jit(solution)/shard_map/pallas_call | solution.py:420
  29.1 2.8 %all-gather = f32[20,16,128]{2,1,0:T(8,128)S(1)} all-gather(f32[10,16,128]{2,1,0:T(8,128)S(1)} %get-tuple-element.55), channel_id=2, replica_groups=mesh['cells'=128,'harm_0'=2,'harm_1'=2] {'harm_1'}, dimensions={0}, use_global_device_ids=true | all-gather | bytes 245760 | tf_op jit(solution)/shard_map/all_gather | solution.py:497
  31.9 0.6 %shard_map.116 = (f32[5,16,128]{2,1,0:T(8,128)S(1)}, f32[5,16,128]{2,1,0:T(8,128)S(1)}, f32[15,8,128]{2,1,0:T(8,128)S(1)}, f32[15,8,128]{2,1,0:T(8,128)S(1)}) custom-call(f32[2,10,16,128]{3,2,1,0:T(8,128)S(1)} %bitcast.12, f32[10,16,128]{2,1,0:T(8,128)S(1)} %get-tuple-element.56.state_ref.refs_5_, s32[2,8,128]{2,1,0:T(8,128)S(1)} %get-tuple-element.57.tile_idx), custom_call_target="tpu_custom_call" | custom-call | tf_op jit(solution)/shard_map/pallas_call | solution.py:420
  32.6 3.6 %collective-permute-start.4 = (f32[15,8,128]{2,1,0:T(8,128)S(1)}, f32[15,8,128]{2,1,0:T(8,128)S(1)}, u32[]{:S(2)}, u32[]{:S(2)}) collective-permute-start(f32[15,8,128]{2,1,0:T(8,128)S(1)} %get-tuple-element.62), channel_id=1, source_target_pairs={{0,4},{4,0},{8,12},{12,8},{16,20},{20,16},{24,28},{28,24},{32,36},... | collective-permute-start | bytes 184328 | tf_op jit(solution)/shard_map/ppermute | solution.py:434
  36.2 2.4 %collective-permute-start.3 = (f32[15,8,128]{2,1,0:T(8,128)S(1)}, f32[15,8,128]{2,1,0:T(8,128)S(1)}, u32[]{:S(2)}, u32[]{:S(2)}) collective-permute-start(f32[15,8,128]{2,1,0:T(8,128)S(1)} %get-tuple-element.58), channel_id=1, source_target_pairs={{0,508},{4,8},{8,4},{12,16},{16,12},{20,24},{24,20},{28,32},{32,28... | collective-permute-start | bytes 184328 | tf_op jit(solution)/shard_map/ppermute | solution.py:433
  38.6 4.4 %collective-permute-start.5 = (f32[5,16,128]{2,1,0:T(8,128)S(1)}, f32[5,16,128]{2,1,0:T(8,128)S(1)}, u32[]{:S(2)}, u32[]{:S(2)}) collective-permute-start(f32[5,16,128]{2,1,0:T(8,128)S(1)} %get-tuple-element.63.refs_8_), channel_id=1, source_target_pairs={{0,2},{2,0},{1,3},{3,1},{4,6},{6,4},{5,7},{7,5},{8,10},{10,8},{9,1... | collective-permute-start | bytes 122888 | tf_op jit(solution)/shard_map/ppermute | solution.py:435
  42.9 2.3 %shard_map.117 = (f32[5,16,128]{2,1,0:T(8,128)S(1)}, f32[10,16,128]{2,1,0:T(8,128)S(1)}) custom-call(s32[1]{0:T(128)S(6)} %copy.12.refs_1_.refs_0_, s32[12,8,128]{2,1,0:T(8,128)S(1)} %get-tuple-element.46.refs_8_.refs_1_.index_ref, f32[12,8,128]{2,1,0:T(8,128)S(1)} %get-tuple-element.47.refs_9_.refs_2_.weight_ref, ...), custom_call_target="tpu_custom_call" | custom-call | tf_op jit(solution)/shard_map/pallas_call | solution.py:420
  45.3 0.0 collective-permute-done.4.rim
  45.3 1.3 %shard_map.118.refs_7_ = f32[15,16,128]{2,1,0:T(8,128)S(1)} custom-call(f32[15,8,128]{2,1,0:T(8,128)S(1)} %collective-permute-done.4.rim, s32[12,8,128]{2,1,0:T(8,128)S(1)} %get-tuple-element.46.refs_8_.refs_1_.index_ref, f32[12,8,128]{2,1,0:T(8,128)S(1)} %get-tuple-element.47.refs_9_.refs_2_.weight_ref), custom_call_target="tpu_custom_call" | custom-call | tf_op jit(solution)/shard_map/pallas_call | solution.py:420
  46.6 0.0 collective-permute-done.5.refs_9_
  46.6 0.0 collective-permute-done.3.refs_0_
  46.6 2.0 %shard_map.119 = (f32[5,2048]{1,0:T(8,128)}, f32[5,2,2048]{2,1,0:T(2,128)}) custom-call(f32[15,8,128]{2,1,0:T(8,128)S(1)} %collective-permute-done.3.refs_0_, s32[12,8,128]{2,1,0:T(8,128)S(1)} %get-tuple-element.46.refs_8_.refs_1_.index_ref, f32[12,8,128]{2,1,0:T(8,128)S(1)} %get-tuple-element.47.refs_9_.refs_2_.weight_ref, ...), custom_call_target="tpu_custom_call" | custom-call | tf_op jit(solution)/shard_map/pallas_call | solution.py:420
Async XLA Ops:
  2.4 24.6 %collective-permute-start = (f32[15,8,128]{2,1,0:T(8,128)S(1)}, f32[15,8,128]{2,1,0:T(8,128)S(1)}, u32[]{:S(2)}, u32[]{:S(2)}) collective-permute-start(f32[15,8,128]{2,1,0:T(8,128)S(1)} %get-tuple-element.43), channel_id=1, source_target_pairs={{0,508},{4,8},{8,4},{12,16},{16,12},{20,24},{24,20},{28,32},{32,28... | collective-permute-start | bytes 184328 | tf_op jit(solution)/shard_map/ppermute | solution.py:433
  17.7 9.3 %collective-permute-start.1 = (f32[15,8,128]{2,1,0:T(8,128)S(1)}, f32[15,8,128]{2,1,0:T(8,128)S(1)}, u32[]{:S(2)}, u32[]{:S(2)}) collective-permute-start(f32[15,8,128]{2,1,0:T(8,128)S(1)} %get-tuple-element.44), channel_id=1, source_target_pairs={{0,4},{4,0},{8,12},{12,8},{16,20},{20,16},{24,28},{28,24},{32,36},... | collective-permute-start | bytes 184328 | tf_op jit(solution)/shard_map/ppermute | solution.py:434
  19.6 7.3 %collective-permute-start.2 = (f32[5,16,128]{2,1,0:T(8,128)S(1)}, f32[5,16,128]{2,1,0:T(8,128)S(1)}, u32[]{:S(2)}, u32[]{:S(2)}) collective-permute-start(f32[5,16,128]{2,1,0:T(8,128)S(1)} %get-tuple-element.45.refs_6_), channel_id=1, source_target_pairs={{0,2},{2,0},{1,3},{3,1},{4,6},{6,4},{5,7},{7,5},{8,10},{10,8},{9,1... | collective-permute-start | bytes 122888 | tf_op jit(solution)/shard_map/ppermute | solution.py:435
  32.6 12.7 %collective-permute-start.4 = (f32[15,8,128]{2,1,0:T(8,128)S(1)}, f32[15,8,128]{2,1,0:T(8,128)S(1)}, u32[]{:S(2)}, u32[]{:S(2)}) collective-permute-start(f32[15,8,128]{2,1,0:T(8,128)S(1)} %get-tuple-element.62), channel_id=1, source_target_pairs={{0,4},{4,0},{8,12},{12,8},{16,20},{20,16},{24,28},{28,24},{32,36},... | collective-permute-start | bytes 184328 | tf_op jit(solution)/shard_map/ppermute | solution.py:434
  36.2 10.4 %collective-permute-start.3 = (f32[15,8,128]{2,1,0:T(8,128)S(1)}, f32[15,8,128]{2,1,0:T(8,128)S(1)}, u32[]{:S(2)}, u32[]{:S(2)}) collective-permute-start(f32[15,8,128]{2,1,0:T(8,128)S(1)} %get-tuple-element.58), channel_id=1, source_target_pairs={{0,508},{4,8},{8,4},{12,16},{16,12},{20,24},{24,20},{28,32},{32,28... | collective-permute-start | bytes 184328 | tf_op jit(solution)/shard_map/ppermute | solution.py:433
  38.6 8.0 %collective-permute-start.5 = (f32[5,16,128]{2,1,0:T(8,128)S(1)}, f32[5,16,128]{2,1,0:T(8,128)S(1)}, u32[]{:S(2)}, u32[]{:S(2)}) collective-permute-start(f32[5,16,128]{2,1,0:T(8,128)S(1)} %get-tuple-element.63.refs_8_), channel_id=1, source_target_pairs={{0,2},{2,0},{1,3},{3,1},{4,6},{6,4},{5,7},{7,5},{8,10},{10,8},{9,1... | collective-permute-start | bytes 122888 | tf_op jit(solution)/shard_map/ppermute | solution.py:435

commit v8 on v7

--- a/solution.py
+++ b/solution.py
@@ -290,9 +290,8 @@
             out_ref[r, at, :] = start[r] - scale * full
 
 
-def middle_kernel(
-    place_ref, order_ref, acc_ref, share_ref, rim_a, rim_b, stress_a, stress_b, index_ref, weight_ref, wsum_ref, mean_ref, state_ref,
-    jac_ref, flow_ref, source_ref, step_ref, out_ref, part_ref, full_ref, mean_acc, words_ref, mean_words, *, coeff,
+def rims_kernel(
+    place_ref, acc_ref, share_ref, rim_a, rim_b, index_ref, weight_ref, full_ref, mean_acc, words_ref, mean_words
 ):
     groups = acc_ref.shape[1]
     rows = 2 * rim_a.shape[1]
@@ -304,7 +303,6 @@
         lambda r, at: acc_ref[r, at, :], full_ref, VARS,
     )
     half = core_of(place_ref)
-    lead = half == 0
     values = gather_into(
         row, MEAN_FIELDS, rows, mean_words, groups * LANES, index_ref, weight_ref, half * FACES, FACES,
         mean_unit, [share_ref[r] for r in range(VARS)],
@@ -312,6 +310,14 @@
     mean_acc[...] = jnp.zeros(mean_acc.shape, F32)
     for r, value in enumerate(values):
         mean_acc[r, pl.ds(pl.multiple_of(half * SUBS, SUBS), SUBS), :] = value
+
+
+def middle_kernel(
+    place_ref, order_ref, full_ref, mean_acc, stress_a, stress_b, wsum_ref, mean_ref, state_ref,
+    jac_ref, flow_ref, source_ref, step_ref, out_ref, part_ref, *, coeff,
+):
+    groups = full_ref.shape[1]
+    lead = core_of(place_ref) == 0
     for g in range(groups // SUBS):
         at = slice(g * SUBS, (g + 1) * SUBS)
         mean = [mean_ref[v, at, :] for v in range(VARS)]
@@ -488,11 +494,14 @@
         (place,), inside,
         scratch=[harm_words, mean_words],
     )
+    full, mean_acc = launch(
+        rims_kernel, (harm_fields, mean_fields), (place,), (acc, share, rim_a, rim_b, index, weight),
+        scratch=[harm_words, mean_words],
+    )
     state, part = launch(
         lambda *refs: middle_kernel(*refs, coeff=1.0 / SECTIONS), (harm_fields, harm_fields),
         (place, harm_order),
-        (acc, share, rim_a, rim_b, stress, other, index, weight, wsum, mean_start, harm_start, jac, flow, source, step),
-        scratch=[harm_fields, mean_fields, harm_words, mean_words],
+        (full, mean_acc, stress, other, wsum, mean_start, harm_start, jac, flow, source, step),
     )
     parts = lax.all_gather(part, HARM[1])
     mean, stress, pay_a, pay_b = launch(join_kernel, (mean_fields, mean_fields) + pays, (), (parts, state, tile_idx))

time: 48.9 us -> 47.9 us (0.980)
  starting transfers between devices: 32 us -> 30.9 us
    ppermute x2, starting transfers between devices: 8.72 us -> 8 us  [exchange(): other = lax.ppermute(stress, HARM[0], [(0, 1), (1, 0)])]
    pallas_call x7 -> x8, Pallas kernels: 12.4 us -> 12.4 us  [launch(): pl.pallas_call(body, out_shape=out_shape, in_specs=[smem] * len(scalars)...]
  transfers between devices with their start and end apart: 6 -> 6, of which waited for: 0 -> 0; matrix products, arithmetic and copies ran while one was open for 0% -> 0% of each run, Pallas kernels for 12% -> 17%
where the time goes in v8:
time: 47.9 us; the launch traced here: 47.6 us
  starting transfers between devices  30.9 us (65%)
  Pallas kernels  12.4 us (26%)
  blocking collectives  2.8 us (6%)
  between operations  1.44 us (3%)
    ppermute x2, starting transfers between devices, exchange(): rim_a = lax.ppermute(pay_a, 'cells', far)  17.3 us
    pallas_call x8, Pallas kernels, launch(): pl.pallas_call(body, out_shape=out_shape, in_specs=[smem] * len(scalars)...  12.4 us
    ppermute x2, starting transfers between devices, exchange(): other = lax.ppermute(stress, HARM[0], [(0, 1), (1, 0)])  8 us
    ppermute x2, starting transfers between devices, exchange(): rim_b = lax.ppermute(pay_b, 'cells', near)  5.56 us
    all_gather x1, blocking collectives, shards(): parts = lax.all_gather(part, HARM[1])  2.8 us
  transfers between devices with their start and end apart: 6, of which 0 were waited for; matrix products, arithmetic and copies ran while one was open for 0% of the time, Pallas kernels for 17%

profile of v8, /device:TPU:1, one launch (start us, length us, event | category | flops | bytes accessed | tf_op | source)
XLA Modules:
  0.0 47.6 jit_solution(10694480973718509329)
XLA Ops:
  0.6 1.7 %shard_map.113 = (f32[15,8,128]{2,1,0:T(8,128)S(1)}, f32[15,8,128]{2,1,0:T(8,128)S(1)}, f32[5,16,128]{2,1,0:T(8,128)S(1)}, s32[2,8,128]{2,1,0:T(8,128)S(1)}, f32...) custom-call(s32[1]{0:T(128)} %bitcast.place_ref.refs_0_, ...), custom_call_target="tpu_custom_call" | custom-call | tf_op jit(solution)/shard_map/pallas_call | solution.py:426
  2.4 15.3 %collective-permute-start = (f32[15,8,128]{2,1,0:T(8,128)S(1)}, f32[15,8,128]{2,1,0:T(8,128)S(1)}, u32[]{:S(2)}, u32[]{:S(2)}) collective-permute-start(f32[15,8,128]{2,1,0:T(8,128)S(1)} %get-tuple-element.45), channel_id=1, source_target_pairs={{0,508},{4,8},{8,4},{12,16},{16,12},{20,24},{24,20},{28,32},{32,28... | collective-permute-start | bytes 184328 | tf_op jit(solution)/shard_map/ppermute | solution.py:439
  17.7 1.9 %collective-permute-start.1 = (f32[15,8,128]{2,1,0:T(8,128)S(1)}, f32[15,8,128]{2,1,0:T(8,128)S(1)}, u32[]{:S(2)}, u32[]{:S(2)}) collective-permute-start(f32[15,8,128]{2,1,0:T(8,128)S(1)} %get-tuple-element.46), channel_id=1, source_target_pairs={{0,4},{4,0},{8,12},{12,8},{16,20},{20,16},{24,28},{28,24},{32,36},... | collective-permute-start | bytes 184328 | tf_op jit(solution)/shard_map/ppermute | solution.py:440
  19.6 4.4 %collective-permute-start.2 = (f32[5,16,128]{2,1,0:T(8,128)S(1)}, f32[5,16,128]{2,1,0:T(8,128)S(1)}, u32[]{:S(2)}, u32[]{:S(2)}) collective-permute-start(f32[5,16,128]{2,1,0:T(8,128)S(1)} %get-tuple-element.51.refs_4_), channel_id=1, source_target_pairs={{0,2},{2,0},{1,3},{3,1},{4,6},{6,4},{5,7},{7,5},{8,10},{10,8},{9,1... | collective-permute-start | bytes 122888 | tf_op jit(solution)/shard_map/ppermute | solution.py:441
  24.6 2.3 %shard_map.114 = (f32[10,16,128]{2,1,0:T(8,128)S(1)}, f32[5,8,128]{2,1,0:T(8,128)S(1)}, s32[12,8,128]{2,1,0:T(8,128)S(1)}, f32[12,8,128]{2,1,0:T(8,128)S(1)}, f3...) custom-call(s32[1]{0:T(128)} %bitcast.place_ref.refs_0_, ...), custom_call_target="tpu_custom_call" | custom-call | tf_op jit(solution)/shard_map/pallas_call | solution.py:426
  26.9 0.0 collective-permute-done.rim_a
  26.9 0.0 collective-permute-done.1.rim_b
  27.0 2.1 %shard_map.115 = (f32[10,16,128]{2,1,0:T(8,128)S(1)}, f32[5,16,128]{2,1,0:T(8,128)S(1)}) custom-call(s32[1]{0:T(128)} %bitcast.place_ref.refs_0_, f32[10,16,128]{2,1,0:T(8,128)S(1)} %get-tuple-element.43.acc_ref, f32[5,8,128]{2,1,0:T(8,128)S(1)} %get-tuple-element.44.share_ref, f32[15,8,128]{2,1,0:T(8,128)S(1)} %collective-permute-done.rim_a, ...), custom_call_target="tpu_custom_call" | custom-call | tf_op jit(solution)/shard_map/pallas_call | solution.py:426
  29.1 0.0 collective-permute-done.2.refs_5_
  29.1 0.1 shard_map.116
  29.2 2.8 %all-gather = f32[20,16,128]{2,1,0:T(8,128)S(1)} all-gather(f32[10,16,128]{2,1,0:T(8,128)S(1)} %get-tuple-element.59), channel_id=2, replica_groups=mesh['cells'=128,'harm_0'=2,'harm_1'=2] {'harm_1'}, dimensions={0}, use_global_device_ids=true | all-gather | bytes 245760 | tf_op jit(solution)/shard_map/all_gather | solution.py:506
  32.0 0.6 %shard_map.117 = (f32[5,16,128]{2,1,0:T(8,128)S(1)}, f32[5,16,128]{2,1,0:T(8,128)S(1)}, f32[15,8,128]{2,1,0:T(8,128)S(1)}, f32[15,8,128]{2,1,0:T(8,128)S(1)}) custom-call(f32[2,10,16,128]{3,2,1,0:T(8,128)S(1)} %bitcast.12, f32[10,16,128]{2,1,0:T(8,128)S(1)} %get-tuple-element.60.state_ref.refs_5_, s32[2,8,128]{2,1,0:T(8,128)S(1)} %get-tuple-element.61.tile_idx), custom_call_target="tpu_custom_call" | custom-call | tf_op jit(solution)/shard_map/pallas_call | solution.py:426
  32.6 3.6 %collective-permute-start.4 = (f32[15,8,128]{2,1,0:T(8,128)S(1)}, f32[15,8,128]{2,1,0:T(8,128)S(1)}, u32[]{:S(2)}, u32[]{:S(2)}) collective-permute-start(f32[15,8,128]{2,1,0:T(8,128)S(1)} %get-tuple-element.66), channel_id=1, source_target_pairs={{0,4},{4,0},{8,12},{12,8},{16,20},{20,16},{24,28},{28,24},{32,36},... | collective-permute-start | bytes 184328 | tf_op jit(solution)/shard_map/ppermute | solution.py:440
  36.3 2.0 %collective-permute-start.3 = (f32[15,8,128]{2,1,0:T(8,128)S(1)}, f32[15,8,128]{2,1,0:T(8,128)S(1)}, u32[]{:S(2)}, u32[]{:S(2)}) collective-permute-start(f32[15,8,128]{2,1,0:T(8,128)S(1)} %get-tuple-element.62), channel_id=1, source_target_pairs={{0,508},{4,8},{8,4},{12,16},{16,12},{20,24},{24,20},{28,32},{32,28... | collective-permute-start | bytes 184328 | tf_op jit(solution)/shard_map/ppermute | solution.py:439
  38.2 3.6 %collective-permute-start.5 = (f32[5,16,128]{2,1,0:T(8,128)S(1)}, f32[5,16,128]{2,1,0:T(8,128)S(1)}, u32[]{:S(2)}, u32[]{:S(2)}) collective-permute-start(f32[5,16,128]{2,1,0:T(8,128)S(1)} %get-tuple-element.67.refs_8_), channel_id=1, source_target_pairs={{0,2},{2,0},{1,3},{3,1},{4,6},{6,4},{5,7},{7,5},{8,10},{10,8},{9,1... | collective-permute-start | bytes 122888 | tf_op jit(solution)/shard_map/ppermute | solution.py:441
  41.9 2.3 %shard_map.118 = (f32[5,16,128]{2,1,0:T(8,128)S(1)}, f32[10,16,128]{2,1,0:T(8,128)S(1)}) custom-call(s32[1]{0:T(128)S(6)} %copy.12.refs_1_.refs_0_, s32[12,8,128]{2,1,0:T(8,128)S(1)} %get-tuple-element.47.index_ref.refs_1_, f32[12,8,128]{2,1,0:T(8,128)S(1)} %get-tuple-element.48.weight_ref.refs_2_, f32[16,128]{1,0:T(8,128)S(1)} %get-tuple-element.52.refs_6_.refs_3_, ...), custom_call_target="tpu_custom_call" | custom-call | tf_op jit(solution)/shard_map/pallas_call | solution.py:426
  44.2 0.0 collective-permute-done.4.rim
  44.2 1.3 %shard_map.119.refs_7_ = f32[15,16,128]{2,1,0:T(8,128)S(1)} custom-call(f32[15,8,128]{2,1,0:T(8,128)S(1)} %collective-permute-done.4.rim, s32[12,8,128]{2,1,0:T(8,128)S(1)} %get-tuple-element.47.index_ref.refs_1_, f32[12,8,128]{2,1,0:T(8,128)S(1)} %get-tuple-element.48.weight_ref.refs_2_), custom_call_target="tpu_custom_call" | custom-call | tf_op jit(solution)/shard_map/pallas_call | solution.py:426
  45.5 0.0 collective-permute-done.5.refs_9_
  45.5 0.0 collective-permute-done.3.refs_0_
  45.5 2.0 %shard_map.120 = (f32[5,2048]{1,0:T(8,128)}, f32[5,2,2048]{2,1,0:T(2,128)}) custom-call(f32[15,8,128]{2,1,0:T(8,128)S(1)} %collective-permute-done.3.refs_0_, s32[12,8,128]{2,1,0:T(8,128)S(1)} %get-tuple-element.47.index_ref.refs_1_, f32[12,8,128]{2,1,0:T(8,128)S(1)} %get-tuple-element.48.weight_ref.refs_2_, ...), custom_call_target="tpu_custom_call" | custom-call | tf_op jit(solution)/shard_map/pallas_call | solution.py:426
Async XLA Ops:
  2.4 24.6 %collective-permute-start = (f32[15,8,128]{2,1,0:T(8,128)S(1)}, f32[15,8,128]{2,1,0:T(8,128)S(1)}, u32[]{:S(2)}, u32[]{:S(2)}) collective-permute-start(f32[15,8,128]{2,1,0:T(8,128)S(1)} %get-tuple-element.45), channel_id=1, source_target_pairs={{0,508},{4,8},{8,4},{12,16},{16,12},{20,24},{24,20},{28,32},{32,28... | collective-permute-start | bytes 184328 | tf_op jit(solution)/shard_map/ppermute | solution.py:439
  17.7 9.3 %collective-permute-start.1 = (f32[15,8,128]{2,1,0:T(8,128)S(1)}, f32[15,8,128]{2,1,0:T(8,128)S(1)}, u32[]{:S(2)}, u32[]{:S(2)}) collective-permute-start(f32[15,8,128]{2,1,0:T(8,128)S(1)} %get-tuple-element.46), channel_id=1, source_target_pairs={{0,4},{4,0},{8,12},{12,8},{16,20},{20,16},{24,28},{28,24},{32,36},... | collective-permute-start | bytes 184328 | tf_op jit(solution)/shard_map/ppermute | solution.py:440
  19.6 9.4 %collective-permute-start.2 = (f32[5,16,128]{2,1,0:T(8,128)S(1)}, f32[5,16,128]{2,1,0:T(8,128)S(1)}, u32[]{:S(2)}, u32[]{:S(2)}) collective-permute-start(f32[5,16,128]{2,1,0:T(8,128)S(1)} %get-tuple-element.51.refs_4_), channel_id=1, source_target_pairs={{0,2},{2,0},{1,3},{3,1},{4,6},{6,4},{5,7},{7,5},{8,10},{10,8},{9,1... | collective-permute-start | bytes 122888 | tf_op jit(solution)/shard_map/ppermute | solution.py:441
  32.6 11.6 %collective-permute-start.4 = (f32[15,8,128]{2,1,0:T(8,128)S(1)}, f32[15,8,128]{2,1,0:T(8,128)S(1)}, u32[]{:S(2)}, u32[]{:S(2)}) collective-permute-start(f32[15,8,128]{2,1,0:T(8,128)S(1)} %get-tuple-element.66), channel_id=1, source_target_pairs={{0,4},{4,0},{8,12},{12,8},{16,20},{20,16},{24,28},{28,24},{32,36},... | collective-permute-start | bytes 184328 | tf_op jit(solution)/shard_map/ppermute | solution.py:440
  36.3 9.3 %collective-permute-start.3 = (f32[15,8,128]{2,1,0:T(8,128)S(1)}, f32[15,8,128]{2,1,0:T(8,128)S(1)}, u32[]{:S(2)}, u32[]{:S(2)}) collective-permute-start(f32[15,8,128]{2,1,0:T(8,128)S(1)} %get-tuple-element.62), channel_id=1, source_target_pairs={{0,508},{4,8},{8,4},{12,16},{16,12},{20,24},{24,20},{28,32},{32,28... | collective-permute-start | bytes 184328 | tf_op jit(solution)/shard_map/ppermute | solution.py:439
  38.2 7.3 %collective-permute-start.5 = (f32[5,16,128]{2,1,0:T(8,128)S(1)}, f32[5,16,128]{2,1,0:T(8,128)S(1)}, u32[]{:S(2)}, u32[]{:S(2)}) collective-permute-start(f32[5,16,128]{2,1,0:T(8,128)S(1)} %get-tuple-element.67.refs_8_), channel_id=1, source_target_pairs={{0,2},{2,0},{1,3},{3,1},{4,6},{6,4},{5,7},{7,5},{8,10},{10,8},{9,1... | collective-permute-start | bytes 122888 | tf_op jit(solution)/shard_map/ppermute | solution.py:441

commit v9 on v6

--- a/solution.py
+++ b/solution.py
@@ -172,14 +172,18 @@
             out_ref[r - lead, at, :] = value
 
 
+def half_rows(half):
+    return pl.ds(pl.multiple_of(half * SUBS, SUBS), SUBS)
+
+
 def zero_start(*_):
     return jnp.zeros((SUBS, LANES), F32)
 
 
 def prepare_kernel(
-    place_ref, mean_ref, harm_ref, links_ref, weight_in, flow_ref, jac_ref, source_ref,
-    acc_ref, share_ref, index_ref, weight_ref, wsum_ref, mean_out, state_ref, jac_out, flow_out, source_out,
-    words_ref, mean_words,
+    place_ref, order_ref, mean_ref, harm_ref, links_ref, weight_in, flow_ref, jac_ref, source_ref, step_ref,
+    mean_base, harm_base, index_ref, weight_ref, wsum_ref, mean_out, state_ref, jac_out, flow_out, source_out,
+    full_ref, mean_acc, words_ref, mean_words, *, coeff,
 ):
     groups = mean_ref.shape[1] // LANES
     flips = place_ref[0] % 2 == 0
@@ -203,20 +207,6 @@
             mean_out[r, at, :] = packed(lambda t: row(r, t), g)
         for r in range(2 * VARS):
             state_ref[r, at, :] = packed(lambda t: row(VARS + r, t), g)
-    row = fields_row(mean_out, state_ref)
-    load = fields_block(mean_out, state_ref)
-    unit = pack_table(load, groups // SUBS, HARM_FIELDS, words_ref)
-    mean_unit = pack_table(load, groups // SUBS, MEAN_FIELDS, mean_words)
-    gather_fields(
-        row, HARM_FIELDS, groups, words_ref, 0, index_ref, weight_ref, unit, zero_start, acc_ref, VARS
-    )
-    begin, count, _ = share_of(place_ref, index_ref)
-    values = gather_into(
-        row, MEAN_FIELDS, groups, mean_words, 0, index_ref, weight_ref, begin, count, mean_unit,
-        [zero_start()] * VARS,
-    )
-    for r, value in enumerate(values):
-        share_ref[r] = value
     for g in range(0, groups, SUBS):
         at = slice(g, g + SUBS)
         for r in range(2 * VARS):
@@ -226,6 +216,37 @@
         for j in range(VARS):
             for i in range(VARS):
                 jac_out[j * VARS + i, at, :] = packed(lambda t: jac_ref[j, i : i + 1, lane(t)], g)
+    row = fields_row(mean_out, state_ref)
+    load = fields_block(mean_out, state_ref)
+    unit = pack_table(load, groups // SUBS, HARM_FIELDS, words_ref)
+    mean_unit = pack_table(load, groups // SUBS, MEAN_FIELDS, mean_words)
+    gather_fields(
+        row, HARM_FIELDS, groups, words_ref, 0, index_ref, weight_ref, unit, zero_start, full_ref, VARS
+    )
+    begin, count, half = share_of(place_ref, index_ref)
+    values = gather_into(
+        row, MEAN_FIELDS, groups, mean_words, 0, index_ref, weight_ref, begin, count, mean_unit,
+        [zero_start()] * VARS,
+    )
+    mean_acc[...] = jnp.zeros(mean_acc.shape, F32)
+    for r, value in enumerate(values):
+        mean_acc[r, half_rows(half), :] = value
+    lead = place_ref[0] // 2 == 0
+    for g in range(groups // SUBS):
+        at = slice(g * SUBS, (g + 1) * SUBS)
+        mean = [mean_out[v, at, :] for v in range(VARS)]
+        state = [state_ref[r, at, :] for r in range(2 * VARS)]
+        wsum = wsum_ref[at, :]
+        scale = coeff * step_ref[at, :]
+        flux = []
+        for v in range(VARS):
+            stress = state[v] * flow_out[v, at, :] + state[VARS + v] * flow_out[VARS + v, at, :]
+            flux.append(jnp.where(lead, wsum * mean[v], 0.0) - mean_acc[v, at, :] - stress)
+        for v, res in enumerate(transposed(jac_out, at, flux)):
+            own = jnp.where(lead, mean[v] + scale * source_out[v, at, :], 0.0)
+            mean_base[v, at, :] = own - scale * res
+        gathered = [full_ref[r, at, :] for r in range(2 * VARS)]
+        harm_step(order_ref, at, mean, state, state, gathered, wsum, scale, jac_out, flow_out, harm_base)
 
 
 def fields_row(mean_ref, harm_ref):
@@ -243,39 +264,14 @@
     return load
 
 
-def rim_row(rim):
-    return lambda r, h: rim[r, h : h + 1, :]
-
-
-def rim_block(rim):
-    return lambda r, g: rim[r, g * SUBS : (g + 1) * SUBS, :]
-
-
-def shared_rim(place_ref, acc_ref, share_ref, rim, first, index_ref, weight_ref, words_ref, mean_words, out_ref):
-    rows = rim.shape[1]
-    row, load = rim_row(rim), rim_block(rim)
-    unit = pack_table(load, rows // SUBS, HARM_FIELDS, words_ref)
-    mean_unit = pack_table(load, rows // SUBS, MEAN_FIELDS, mean_words)
-    gather_fields(
-        row, HARM_FIELDS, rows, words_ref, first, index_ref, weight_ref, unit,
-        lambda r, at: acc_ref[r, at, :], out_ref, VARS,
-    )
-    begin, count, _ = share_of(place_ref, index_ref)
-    return gather_into(
-        row, MEAN_FIELDS, rows, mean_words, first, index_ref, weight_ref,
-        begin, count, mean_unit, [share_ref[r] for r in range(VARS)],
-    )
-
-
-def near_share_kernel(
-    place_ref, acc_ref, share_ref, rim, index_ref, weight_ref, out_ref, share_out, words_ref, mean_words
-):
-    first = (acc_ref.shape[1] + rim.shape[1]) * LANES
-    values = shared_rim(
-        place_ref, acc_ref, share_ref, rim, first, index_ref, weight_ref, words_ref, mean_words, out_ref
-    )
-    for r, value in enumerate(values):
-        share_out[r] = value
+def rim_row(*rims):
+    rows = rims[0].shape[1]
+    return lambda r, h: rims[h // rows][r, h % rows : h % rows + 1, :]
+
+
+def rim_block(*rims):
+    blocks = rims[0].shape[1] // SUBS
+    return lambda r, g: rims[g // blocks][r, g % blocks * SUBS : (g % blocks + 1) * SUBS, :]
 
 
 def near_kernel(rim, index_ref, weight_ref, out_ref, words_ref):
@@ -311,37 +307,40 @@
 
 
 def middle_kernel(
-    place_ref, order_ref, acc_ref, share_ref, rim, index_ref, weight_ref, wsum_ref, mean_ref, state_ref,
-    jac_ref, flow_ref, source_ref, step_ref, out_ref, part_ref, full_ref, mean_acc, words_ref, mean_words, *, coeff,
+    place_ref, rim_a, rim_b, index_ref, weight_ref, mean_base, harm_base, jac_ref, flow_ref, step_ref,
+    out_ref, part_ref, words_ref, mean_words, *, coeff,
 ):
-    groups = acc_ref.shape[1]
-    _, _, half = share_of(place_ref, index_ref)
-    lead = place_ref[0] // 2 == 0
-    values = shared_rim(
-        place_ref, acc_ref, share_ref, rim, groups * LANES, index_ref, weight_ref, words_ref, mean_words, full_ref
-    )
-    mean_acc[...] = jnp.zeros(mean_acc.shape, F32)
-    for r, value in enumerate(values):
-        mean_acc[r, pl.ds(pl.multiple_of(half * SUBS, SUBS), SUBS), :] = value
+    groups = mean_base.shape[1]
+    rows = 2 * rim_a.shape[1]
+    row, load = rim_row(rim_a, rim_b), rim_block(rim_a, rim_b)
+    unit = pack_table(load, rows // SUBS, HARM_FIELDS, words_ref)
+    mean_unit = pack_table(load, rows // SUBS, MEAN_FIELDS, mean_words)
+    begin, count, half = share_of(place_ref, index_ref)
+    values = gather_into(
+        row, MEAN_FIELDS, rows, mean_words, groups * LANES, index_ref, weight_ref, begin, count, mean_unit,
+        [zero_start()] * VARS,
+    )
+    for v in range(VARS):
+        part_ref[v] = mean_base[v]
+    at = half_rows(half)
+    scale = coeff * step_ref[at, :]
+    for v, res in enumerate(transposed(jac_ref, at, values)):
+        part_ref[v, at, :] = mean_base[v, at, :] + scale * res
     for g in range(groups // SUBS):
         at = slice(g * SUBS, (g + 1) * SUBS)
-        mean = [mean_ref[v, at, :] for v in range(VARS)]
-        state = [state_ref[r, at, :] for r in range(2 * VARS)]
-        wsum = wsum_ref[at, :]
+        values = gather_into(
+            row, HARM_FIELDS, rows, words_ref, groups * LANES, index_ref, weight_ref, g * FACES, FACES, unit,
+            [zero_start()] * (2 * VARS),
+        )
         scale = coeff * step_ref[at, :]
-        flux = []
+        new = []
+        for first in range(0, 2 * VARS, VARS):
+            for v, res in enumerate(transposed(jac_ref, at, values[first : first + VARS])):
+                new.append(harm_base[first + v, at, :] + scale * res)
+        for r, value in enumerate(new):
+            out_ref[r, at, :] = value
         for v in range(VARS):
-            stress = state[v] * flow_ref[v, at, :] + state[VARS + v] * flow_ref[VARS + v, at, :]
-            flux.append(jnp.where(lead, wsum * mean[v], 0.0) - mean_acc[v, at, :] - stress)
-        for v, res in enumerate(transposed(jac_ref, at, flux)):
-            own = jnp.where(lead, mean[v] + scale * source_ref[v, at, :], 0.0)
-            part_ref[v, at, :] = own - scale * res
-        gathered = [full_ref[r, at, :] for r in range(2 * VARS)]
-        harm_step(order_ref, at, mean, state, state, gathered, wsum, scale, jac_ref, flow_ref, out_ref)
-        for v in range(VARS):
-            part_ref[VARS + v, at, :] = (
-                out_ref[v, at, :] * flow_ref[v, at, :] + out_ref[VARS + v, at, :] * flow_ref[VARS + v, at, :]
-            )
+            part_ref[VARS + v, at, :] = new[v] * flow_ref[v, at, :] + new[VARS + v] * flow_ref[VARS + v, at, :]
 
 
 def join_kernel(parts_ref, state_ref, tile_idx, mean_ref, stress_ref, pay_a, pay_b):
@@ -482,11 +481,11 @@
     registers = FACES * halves
     words = lambda fields: struct(max(len(fields) // 3 * 2, 1), groups, LANES, dtype=jnp.int32)
     harm_words, mean_words = words(HARM_FIELDS), words(MEAN_FIELDS)
-    acc, share, index, weight, wsum, mean_start, harm_start, jac, flow, source = launch(
-        prepare_kernel,
+    mean_base, harm_base, index, weight, wsum, mean_start, harm_start, jac, flow, source = launch(
+        lambda *refs: prepare_kernel(*refs, coeff=1.0 / SECTIONS),
         (
+            mean_fields,
             harm_fields,
-            struct(VARS, SUBS, LANES),
             struct(registers, SUBS, LANES, dtype=jnp.int32),
             struct(registers, SUBS, LANES),
             struct(groups, LANES),
@@ -496,18 +495,13 @@
             harm_fields,
             mean_fields,
         ),
-        (place,), inside,
+        (place, harm_order), (*inside, step),
+        scratch=[harm_fields, mean_fields, harm_words, mean_words],
+    )
+    state, part = launch(
+        lambda *refs: middle_kernel(*refs, coeff=1.0 / SECTIONS), (harm_fields, harm_fields), (place,),
+        (rim_a, rim_b, index, weight, mean_base, harm_base, jac, flow, step),
         scratch=[harm_words, mean_words],
-    )
-    acc, share = launch(
-        near_share_kernel, (harm_fields, struct(VARS, SUBS, LANES)), (place,),
-        (acc, share, rim_b, index, weight), scratch=[harm_words, mean_words],
-    )
-    state, part = launch(
-        lambda *refs: middle_kernel(*refs, coeff=1.0 / SECTIONS), (harm_fields, harm_fields),
-        (place, harm_order),
-        (acc, share, rim_a, index, weight, wsum, mean_start, harm_start, jac, flow, source, step),
-        scratch=[harm_fields, mean_fields, harm_words, mean_words],
     )
     parts = lax.all_gather(part, HARM)
     mean, stress, pay_a, pay_b = launch(join_kernel, (mean_fields, mean_fields) + pays, (), (parts, state, tile_idx))

time: 48.8 us -> 48.1 us (0.986)
  starting transfers between devices: 26.4 us -> 23.2 us
  waiting for transfers between devices: 0.01 us -> 2.12 us
  blocking collectives: 8.54 us -> 9.4 us
  Pallas kernels: 12.2 us -> 11.7 us
    ppermute x2, starting transfers between devices: 5.94 us -> 4.08 us  [exchange(): rim_b = lax.ppermute(pay_b, 'cells', near)]
    ppermute x2, waiting for transfers between devices: 0.01 us -> 1.77 us  [exchange(): rim_a = lax.ppermute(pay_a, 'cells', far)]
    ppermute x2, starting transfers between devices: 20.4 us -> 19.1 us  [exchange(): rim_a = lax.ppermute(pay_a, 'cells', far)]
    all_gather x1, blocking collectives: 8.54 us -> 9.4 us  [shards(): parts = lax.all_gather(part, HARM)]
    pallas_call x8 -> x7, Pallas kernels: 12.2 us -> 11.7 us  [launch(): pl.pallas_call(body, out_shape=out_shape, in_specs=[smem] * len(scalars)...]
  transfers between devices with their start and end apart: 4 -> 4, of which waited for: 0 -> 2; matrix products, arithmetic and copies ran while one was open for 0% -> 0% of each run, Pallas kernels for 14% -> 12%
where the time goes in v9:
time: 48.1 us; the launch traced here: 47.8 us
  starting transfers between devices  23.2 us (48%)
  Pallas kernels  11.7 us (24%)
  blocking collectives  9.4 us (20%)
  waiting for transfers between devices  2.12 us (4%)
  between operations  1.39 us (3%)
    ppermute x2, starting transfers between devices, exchange(): rim_a = lax.ppermute(pay_a, 'cells', far)  19.1 us
    pallas_call x7, Pallas kernels, launch(): pl.pallas_call(body, out_shape=out_shape, in_specs=[smem] * len(scalars)...  11.7 us
    all_gather x1, blocking collectives, shards(): parts = lax.all_gather(part, HARM)  9.4 us
    ppermute x2, starting transfers between devices, exchange(): rim_b = lax.ppermute(pay_b, 'cells', near)  4.08 us
    ppermute x2, waiting for transfers between devices, exchange(): rim_a = lax.ppermute(pay_a, 'cells', far)  1.77 us
  transfers between devices with their start and end apart: 4, of which 2 were waited for; matrix products, arithmetic and copies ran while one was open for 0% of the time, Pallas kernels for 12%

profile of v9, /device:TPU:1, one launch (start us, length us, event | category | flops | bytes accessed | tf_op | source)
XLA Modules:
  0.0 47.8 jit_solution(12383290944843933022)
XLA Ops:
  0.6 1.6 %shard_map.113 = (f32[15,8,128]{2,1,0:T(8,128)S(1)}, f32[15,8,128]{2,1,0:T(8,128)S(1)}, s32[2,8,128]{2,1,0:T(8,128)S(1)}, f32[5,2048]{1,0:T(8,128)S(1)}, f32[5,2...) custom-call(s32[1]{0:T(128)} %bitcast.place_ref.refs_0_, ...), custom_call_target="tpu_custom_call" | custom-call | tf_op jit(solution)/shard_map/pallas_call | solution.py:431
  2.3 15.3 %collective-permute-start = (f32[15,8,128]{2,1,0:T(8,128)S(1)}, f32[15,8,128]{2,1,0:T(8,128)S(1)}, u32[]{:S(2)}, u32[]{:S(2)}) collective-permute-start(f32[15,8,128]{2,1,0:T(8,128)S(1)} %get-tuple-element.33), channel_id=1, source_target_pairs={{0,508},{4,8},{8,4},{12,16},{16,12},{20,24},{24,20},{28,32},{32,28... | collective-permute-start | bytes 184328 | tf_op jit(solution)/shard_map/ppermute | solution.py:444
  17.6 1.9 %collective-permute-start.1 = (f32[15,8,128]{2,1,0:T(8,128)S(1)}, f32[15,8,128]{2,1,0:T(8,128)S(1)}, u32[]{:S(2)}, u32[]{:S(2)}) collective-permute-start(f32[15,8,128]{2,1,0:T(8,128)S(1)} %get-tuple-element.34), channel_id=1, source_target_pairs={{0,4},{4,0},{8,12},{12,8},{16,20},{20,16},{24,28},{28,24},{32,36},... | collective-permute-start | bytes 184328 | tf_op jit(solution)/shard_map/ppermute | solution.py:445
  20.2 2.0 %shard_map.114 = (f32[5,16,128]{2,1,0:T(8,128)S(1)}, f32[10,16,128]{2,1,0:T(8,128)S(1)}, s32[12,8,128]{2,1,0:T(8,128)S(1)}, f32[12,8,128]{2,1,0:T(8,128)S(1)}, f...) custom-call(s32[1]{0:T(128)} %bitcast.place_ref.refs_0_, ...), custom_call_target="tpu_custom_call" | custom-call | tf_op jit(solution)/shard_map/pallas_call | solution.py:431
  22.2 0.0 collective-permute-done.refs_1_
  22.2 0.4 collective-permute-done.1.refs_2_
  22.6 1.8 %shard_map.115 = (f32[10,16,128]{2,1,0:T(8,128)S(1)}, f32[10,16,128]{2,1,0:T(8,128)S(1)}) custom-call(s32[1]{0:T(128)} %bitcast.place_ref.refs_0_, f32[15,8,128]{2,1,0:T(8,128)S(1)} %collective-permute-done.refs_1_, f32[15,8,128]{2,1,0:T(8,128)S(1)} %collective-permute-done.1.refs_2_, s32[12,8,128]{2,1,0:T(8,128)S(1)} %get-tuple-element.43.refs_3_.refs_1_.index_ref, ...), custom_call_target="tpu_custom_call" | custom-call | tf_op jit(solution)/shard_map/pallas_call | solution.py:431
  24.4 9.4 %all-gather = f32[40,16,128]{2,1,0:T(8,128)S(1)} all-gather(f32[10,16,128]{2,1,0:T(8,128)S(1)} %get-tuple-element.49), channel_id=2, replica_groups=mesh['cells'=128,'harm_0'=2,'harm_1'=2] {'harm_0','harm_1'}, dimensions={0}, use_global_device_ids=true | all-gather | bytes 409600 | tf_op jit(solution)/shard_map/all_gather | solution.py:506
  33.8 0.6 %shard_map.116 = (f32[5,16,128]{2,1,0:T(8,128)S(1)}, f32[5,16,128]{2,1,0:T(8,128)S(1)}, f32[15,8,128]{2,1,0:T(8,128)S(1)}, f32[15,8,128]{2,1,0:T(8,128)S(1)}) custom-call(f32[4,10,16,128]{3,2,1,0:T(8,128)S(1)} %bitcast.12, f32[10,16,128]{2,1,0:T(8,128)S(1)} %get-tuple-element.50.state_ref.refs_5_, s32[2,8,128]{2,1,0:T(8,128)S(1)} %get-tuple-element.51.tile_idx), custom_call_target="tpu_custom_call" | custom-call | tf_op jit(solution)/shard_map/pallas_call | solution.py:431
  34.4 2.2 %collective-permute-start.3 = (f32[15,8,128]{2,1,0:T(8,128)S(1)}, f32[15,8,128]{2,1,0:T(8,128)S(1)}, u32[]{:S(2)}, u32[]{:S(2)}) collective-permute-start(f32[15,8,128]{2,1,0:T(8,128)S(1)} %get-tuple-element.61), channel_id=1, source_target_pairs={{0,4},{4,0},{8,12},{12,8},{16,20},{20,16},{24,28},{28,24},{32,36},... | collective-permute-start | bytes 184328 | tf_op jit(solution)/shard_map/ppermute | solution.py:445
  36.6 3.8 %collective-permute-start.2 = (f32[15,8,128]{2,1,0:T(8,128)S(1)}, f32[15,8,128]{2,1,0:T(8,128)S(1)}, u32[]{:S(2)}, u32[]{:S(2)}) collective-permute-start(f32[15,8,128]{2,1,0:T(8,128)S(1)} %get-tuple-element.52), channel_id=1, source_target_pairs={{0,508},{4,8},{8,4},{12,16},{16,12},{20,24},{24,20},{28,32},{32,28... | collective-permute-start | bytes 184328 | tf_op jit(solution)/shard_map/ppermute | solution.py:444
  40.4 2.3 %shard_map.117 = (f32[5,16,128]{2,1,0:T(8,128)S(1)}, f32[10,16,128]{2,1,0:T(8,128)S(1)}) custom-call(s32[1]{0:T(128)S(6)} %copy.12.refs_1_.refs_0_, s32[12,8,128]{2,1,0:T(8,128)S(1)} %get-tuple-element.43.refs_3_.refs_1_.index_ref, f32[12,8,128]{2,1,0:T(8,128)S(1)} %get-tuple-element.44.refs_4_.refs_2_.weight_ref, f32[16,128]{1,0:T(8,128)S(1)} %get-tuple-element.53.refs_3_, ...), custom_call_target="tpu_custom_call" | custom-call | tf_op jit(solution)/shard_map/pallas_call | solution.py:431
  42.7 0.0 collective-permute-done.3.rim
  42.7 1.3 %shard_map.118.refs_7_ = f32[15,16,128]{2,1,0:T(8,128)S(1)} custom-call(f32[15,8,128]{2,1,0:T(8,128)S(1)} %collective-permute-done.3.rim, s32[12,8,128]{2,1,0:T(8,128)S(1)} %get-tuple-element.43.refs_3_.refs_1_.index_ref, f32[12,8,128]{2,1,0:T(8,128)S(1)} %get-tuple-element.44.refs_4_.refs_2_.weight_ref), custom_call_target="tpu_custom_call" | custom-call | tf_op jit(solution)/shard_map/pallas_call | solution.py:431
  44.0 1.8 %collective-permute-done.2.refs_0_ = f32[15,8,128]{2,1,0:T(8,128)S(1)} collective-permute-done((f32[15,8,128]{2,1,0:T(8,128)S(1)}, f32[15,8,128]{2,1,0:T(8,128)S(1)}, u32[]{:S(2)}, u32[]{:S(2)}) %collective-permute-start.2) | collective-permute-done | bytes 61472 | tf_op jit(solution)/shard_map/ppermute | solution.py:444
  45.8 2.0 %shard_map.119 = (f32[5,2048]{1,0:T(8,128)}, f32[5,2,2048]{2,1,0:T(2,128)}) custom-call(f32[15,8,128]{2,1,0:T(8,128)S(1)} %collective-permute-done.2.refs_0_, s32[12,8,128]{2,1,0:T(8,128)S(1)} %get-tuple-element.43.refs_3_.refs_1_.index_ref, f32[12,8,128]{2,1,0:T(8,128)S(1)} %get-tuple-element.44.refs_4_.refs_2_.weight_ref, ...), custom_call_target="tpu_custom_call" | custom-call | tf_op jit(solution)/shard_map/pallas_call | solution.py:431
Async XLA Ops:
  2.3 19.9 %collective-permute-start = (f32[15,8,128]{2,1,0:T(8,128)S(1)}, f32[15,8,128]{2,1,0:T(8,128)S(1)}, u32[]{:S(2)}, u32[]{:S(2)}) collective-permute-start(f32[15,8,128]{2,1,0:T(8,128)S(1)} %get-tuple-element.33), channel_id=1, source_target_pairs={{0,508},{4,8},{8,4},{12,16},{16,12},{20,24},{24,20},{28,32},{32,28... | collective-permute-start | bytes 184328 | tf_op jit(solution)/shard_map/ppermute | solution.py:444
  17.6 5.0 %collective-permute-start.1 = (f32[15,8,128]{2,1,0:T(8,128)S(1)}, f32[15,8,128]{2,1,0:T(8,128)S(1)}, u32[]{:S(2)}, u32[]{:S(2)}) collective-permute-start(f32[15,8,128]{2,1,0:T(8,128)S(1)} %get-tuple-element.34), channel_id=1, source_target_pairs={{0,4},{4,0},{8,12},{12,8},{16,20},{20,16},{24,28},{28,24},{32,36},... | collective-permute-start | bytes 184328 | tf_op jit(solution)/shard_map/ppermute | solution.py:445
  34.4 8.3 %collective-permute-start.3 = (f32[15,8,128]{2,1,0:T(8,128)S(1)}, f32[15,8,128]{2,1,0:T(8,128)S(1)}, u32[]{:S(2)}, u32[]{:S(2)}) collective-permute-start(f32[15,8,128]{2,1,0:T(8,128)S(1)} %get-tuple-element.61), channel_id=1, source_target_pairs={{0,4},{4,0},{8,12},{12,8},{16,20},{20,16},{24,28},{28,24},{32,36},... | collective-permute-start | bytes 184328 | tf_op jit(solution)/shard_map/ppermute | solution.py:445
  36.6 9.2 %collective-permute-start.2 = (f32[15,8,128]{2,1,0:T(8,128)S(1)}, f32[15,8,128]{2,1,0:T(8,128)S(1)}, u32[]{:S(2)}, u32[]{:S(2)}) collective-permute-start(f32[15,8,128]{2,1,0:T(8,128)S(1)} %get-tuple-element.52), channel_id=1, source_target_pairs={{0,508},{4,8},{8,4},{12,16},{16,12},{20,24},{24,20},{28,32},{32,28... | collective-permute-start | bytes 184328 | tf_op jit(solution)/shard_map/ppermute | solution.py:444

commit v10 on v9

--- a/solution.py
+++ b/solution.py
@@ -306,19 +306,36 @@
             out_ref[r, at, :] = start[r] - scale * full
 
 
+def far_kernel(place_ref, rim, index_ref, weight_ref, full_ref, share_ref, words_ref, mean_words):
+    rows = rim.shape[1]
+    first = full_ref.shape[1] * LANES
+    row, load = rim_row(rim), rim_block(rim)
+    unit = pack_table(load, rows // SUBS, HARM_FIELDS, words_ref)
+    mean_unit = pack_table(load, rows // SUBS, MEAN_FIELDS, mean_words)
+    gather_fields(row, HARM_FIELDS, rows, words_ref, first, index_ref, weight_ref, unit, zero_start, full_ref, VARS)
+    begin, count, _ = share_of(place_ref, index_ref)
+    values = gather_into(
+        row, MEAN_FIELDS, rows, mean_words, first, index_ref, weight_ref, begin, count, mean_unit,
+        [zero_start()] * VARS,
+    )
+    for r, value in enumerate(values):
+        share_ref[r] = value
+
+
 def middle_kernel(
-    place_ref, rim_a, rim_b, index_ref, weight_ref, mean_base, harm_base, jac_ref, flow_ref, step_ref,
+    place_ref, rim, full_ref, share_ref, index_ref, weight_ref, mean_base, harm_base, jac_ref, flow_ref, step_ref,
     out_ref, part_ref, words_ref, mean_words, *, coeff,
 ):
     groups = mean_base.shape[1]
-    rows = 2 * rim_a.shape[1]
-    row, load = rim_row(rim_a, rim_b), rim_block(rim_a, rim_b)
+    rows = rim.shape[1]
+    near = (groups + rows) * LANES
+    row, load = rim_row(rim), rim_block(rim)
     unit = pack_table(load, rows // SUBS, HARM_FIELDS, words_ref)
     mean_unit = pack_table(load, rows // SUBS, MEAN_FIELDS, mean_words)
     begin, count, half = share_of(place_ref, index_ref)
     values = gather_into(
-        row, MEAN_FIELDS, rows, mean_words, groups * LANES, index_ref, weight_ref, begin, count, mean_unit,
-        [zero_start()] * VARS,
+        row, MEAN_FIELDS, rows, mean_words, near, index_ref, weight_ref, begin, count, mean_unit,
+        [share_ref[r] for r in range(VARS)],
     )
     for v in range(VARS):
         part_ref[v] = mean_base[v]
@@ -329,8 +346,8 @@
     for g in range(groups // SUBS):
         at = slice(g * SUBS, (g + 1) * SUBS)
         values = gather_into(
-            row, HARM_FIELDS, rows, words_ref, groups * LANES, index_ref, weight_ref, g * FACES, FACES, unit,
-            [zero_start()] * (2 * VARS),
+            row, HARM_FIELDS, rows, words_ref, near, index_ref, weight_ref, g * FACES, FACES, unit,
+            [full_ref[r, at, :] for r in range(2 * VARS)],
         )
         scale = coeff * step_ref[at, :]
         new = []
@@ -498,9 +515,13 @@
         (place, harm_order), (*inside, step),
         scratch=[harm_fields, mean_fields, harm_words, mean_words],
     )
+    full, share = launch(
+        far_kernel, (harm_fields, struct(VARS, SUBS, LANES)), (place,), (rim_a, index, weight),
+        scratch=[harm_words, mean_words],
+    )
     state, part = launch(
         lambda *refs: middle_kernel(*refs, coeff=1.0 / SECTIONS), (harm_fields, harm_fields), (place,),
-        (rim_a, rim_b, index, weight, mean_base, harm_base, jac, flow, step),
+        (rim_b, full, share, index, weight, mean_base, harm_base, jac, flow, step),
         scratch=[harm_words, mean_words],
     )
     parts = lax.all_gather(part, HARM)

time: 48.1 us -> 48.4 us (level)
  starting transfers between devices: 23.2 us -> 24.2 us
  blocking collectives: 9.4 us -> 8.64 us
    ppermute x2, starting transfers between devices: 4.08 us -> 5.18 us  [exchange(): rim_b = lax.ppermute(pay_b, 'cells', near)]
    all_gather x1, blocking collectives: 9.4 us -> 8.64 us  [shards(): parts = lax.all_gather(part, HARM)]
    pallas_call x7 -> x8, Pallas kernels: 11.7 us -> 12 us  [launch(): pl.pallas_call(body, out_shape=out_shape, in_specs=[smem] * len(scalars)...]
  transfers between devices with their start and end apart: 4 -> 4, of which waited for: 2 -> 1; matrix products, arithmetic and copies ran while one was open for 0% -> 0% of each run, Pallas kernels for 12% -> 14%
where the time goes in v10:
time: 48.4 us; the launch traced here: 48.1 us
  starting transfers between devices  24.2 us (50%)
  Pallas kernels  12 us (25%)
  blocking collectives  8.64 us (18%)
  waiting for transfers between devices  1.88 us (4%)
  between operations  1.4 us (3%)
    ppermute x2, starting transfers between devices, exchange(): rim_a = lax.ppermute(pay_a, 'cells', far)  19 us
    pallas_call x8, Pallas kernels, launch(): pl.pallas_call(body, out_shape=out_shape, in_specs=[smem] * len(scalars)...  12 us
    all_gather x1, blocking collectives, shards(): parts = lax.all_gather(part, HARM)  8.64 us
    ppermute x2, starting transfers between devices, exchange(): rim_b = lax.ppermute(pay_b, 'cells', near)  5.18 us
    ppermute x2, waiting for transfers between devices, exchange(): rim_a = lax.ppermute(pay_a, 'cells', far)  1.87 us
  transfers between devices with their start and end apart: 4, of which 1 were waited for; matrix products, arithmetic and copies ran while one was open for 0% of the time, Pallas kernels for 14%

profile of v10, /device:TPU:1, one launch (start us, length us, event | category | flops | bytes accessed | tf_op | source)
XLA Modules:
  0.0 48.1 jit_solution(9753771921751023263)
XLA Ops:
  0.6 1.6 %shard_map.113 = (f32[15,8,128]{2,1,0:T(8,128)S(1)}, f32[15,8,128]{2,1,0:T(8,128)S(1)}, s32[2,8,128]{2,1,0:T(8,128)S(1)}, f32[5,2048]{1,0:T(8,128)S(1)}, f32[5,2...) custom-call(s32[1]{0:T(128)} %bitcast.place_ref.refs_0_, ...), custom_call_target="tpu_custom_call" | custom-call | tf_op jit(solution)/shard_map/pallas_call | solution.py:448
  2.3 15.3 %collective-permute-start.1 = (f32[15,8,128]{2,1,0:T(8,128)S(1)}, f32[15,8,128]{2,1,0:T(8,128)S(1)}, u32[]{:S(2)}, u32[]{:S(2)}) collective-permute-start(f32[15,8,128]{2,1,0:T(8,128)S(1)} %get-tuple-element.36), channel_id=1, source_target_pairs={{0,508},{4,8},{8,4},{12,16},{16,12},{20,24},{24,20},{28,32},{32,28... | collective-permute-start | bytes 184328 | tf_op jit(solution)/shard_map/ppermute | solution.py:461
  17.6 1.9 %collective-permute-start = (f32[15,8,128]{2,1,0:T(8,128)S(1)}, f32[15,8,128]{2,1,0:T(8,128)S(1)}, u32[]{:S(2)}, u32[]{:S(2)}) collective-permute-start(f32[15,8,128]{2,1,0:T(8,128)S(1)} %get-tuple-element.35), channel_id=1, source_target_pairs={{0,4},{4,0},{8,12},{12,8},{16,20},{20,16},{24,28},{28,24},{32,36},... | collective-permute-start | bytes 184328 | tf_op jit(solution)/shard_map/ppermute | solution.py:462
  20.2 2.0 %shard_map.114 = (f32[5,16,128]{2,1,0:T(8,128)S(1)}, f32[10,16,128]{2,1,0:T(8,128)S(1)}, s32[12,8,128]{2,1,0:T(8,128)S(1)}, f32[12,8,128]{2,1,0:T(8,128)S(1)}, f...) custom-call(s32[1]{0:T(128)} %bitcast.place_ref.refs_0_, ...), custom_call_target="tpu_custom_call" | custom-call | tf_op jit(solution)/shard_map/pallas_call | solution.py:448
  22.2 0.0 collective-permute-done.1.rim
  22.2 1.1 %shard_map.115 = (f32[10,16,128]{2,1,0:T(8,128)S(1)}, f32[5,8,128]{2,1,0:T(8,128)S(1)}) custom-call(s32[1]{0:T(128)} %bitcast.place_ref.refs_0_, f32[15,8,128]{2,1,0:T(8,128)S(1)} %collective-permute-done.1.rim, s32[12,8,128]{2,1,0:T(8,128)S(1)} %get-tuple-element.45.index_ref.refs_4_.refs_1_, f32[12,8,128]{2,1,0:T(8,128)S(1)} %get-tuple-element.46.weight_ref.refs_5_.refs_2_), custom_call_target="tpu_custom_call" | custom-call | tf_op jit(solution)/shard_map/pallas_call | solution.py:448
  23.3 0.0 collective-permute-done.refs_1_
  23.3 1.0 %shard_map.116 = (f32[10,16,128]{2,1,0:T(8,128)S(1)}, f32[10,16,128]{2,1,0:T(8,128)S(1)}) custom-call(s32[1]{0:T(128)} %bitcast.place_ref.refs_0_, f32[15,8,128]{2,1,0:T(8,128)S(1)} %collective-permute-done.refs_1_, f32[10,16,128]{2,1,0:T(8,128)S(1)} %get-tuple-element.47.refs_2_, f32[5,8,128]{2,1,0:T(8,128)S(1)} %get-tuple-element.48.refs_3_, ...), custom_call_target="tpu_custom_call" | custom-call | tf_op jit(solution)/shard_map/pallas_call | solution.py:448
  24.4 8.6 %all-gather = f32[40,16,128]{2,1,0:T(8,128)S(1)} all-gather(f32[10,16,128]{2,1,0:T(8,128)S(1)} %get-tuple-element.53), channel_id=2, replica_groups=mesh['cells'=128,'harm_0'=2,'harm_1'=2] {'harm_0','harm_1'}, dimensions={0}, use_global_device_ids=true | all-gather | bytes 409600 | tf_op jit(solution)/shard_map/all_gather | solution.py:527
  33.0 0.6 %shard_map.117 = (f32[5,16,128]{2,1,0:T(8,128)S(1)}, f32[5,16,128]{2,1,0:T(8,128)S(1)}, f32[15,8,128]{2,1,0:T(8,128)S(1)}, f32[15,8,128]{2,1,0:T(8,128)S(1)}) custom-call(f32[4,10,16,128]{3,2,1,0:T(8,128)S(1)} %bitcast.12, f32[10,16,128]{2,1,0:T(8,128)S(1)} %get-tuple-element.54.state_ref.refs_5_, s32[2,8,128]{2,1,0:T(8,128)S(1)} %get-tuple-element.55.tile_idx), custom_call_target="tpu_custom_call" | custom-call | tf_op jit(solution)/shard_map/pallas_call | solution.py:448
  33.6 3.3 %collective-permute-start.3 = (f32[15,8,128]{2,1,0:T(8,128)S(1)}, f32[15,8,128]{2,1,0:T(8,128)S(1)}, u32[]{:S(2)}, u32[]{:S(2)}) collective-permute-start(f32[15,8,128]{2,1,0:T(8,128)S(1)} %get-tuple-element.65), channel_id=1, source_target_pairs={{0,4},{4,0},{8,12},{12,8},{16,20},{20,16},{24,28},{28,24},{32,36},... | collective-permute-start | bytes 184328 | tf_op jit(solution)/shard_map/ppermute | solution.py:462
  36.9 3.7 %collective-permute-start.2 = (f32[15,8,128]{2,1,0:T(8,128)S(1)}, f32[15,8,128]{2,1,0:T(8,128)S(1)}, u32[]{:S(2)}, u32[]{:S(2)}) collective-permute-start(f32[15,8,128]{2,1,0:T(8,128)S(1)} %get-tuple-element.56), channel_id=1, source_target_pairs={{0,508},{4,8},{8,4},{12,16},{16,12},{20,24},{24,20},{28,32},{32,28... | collective-permute-start | bytes 184328 | tf_op jit(solution)/shard_map/ppermute | solution.py:461
  40.6 2.3 %shard_map.118 = (f32[5,16,128]{2,1,0:T(8,128)S(1)}, f32[10,16,128]{2,1,0:T(8,128)S(1)}) custom-call(s32[1]{0:T(128)S(6)} %copy.12.refs_1_.refs_0_, s32[12,8,128]{2,1,0:T(8,128)S(1)} %get-tuple-element.45.index_ref.refs_4_.refs_1_, f32[12,8,128]{2,1,0:T(8,128)S(1)} %get-tuple-element.46.weight_ref.refs_5_.refs_2_, f32[16,128]{1,0:T(8,128)S(1)} %get-tuple-element.57.refs_3_, ...), custom_call_target="tpu_custom_call" | custom-call | tf_op jit(solution)/shard_map/pallas_call | solution.py:448
  42.9 0.0 collective-permute-done.3.rim
  42.9 1.3 %shard_map.119.refs_7_ = f32[15,16,128]{2,1,0:T(8,128)S(1)} custom-call(f32[15,8,128]{2,1,0:T(8,128)S(1)} %collective-permute-done.3.rim, s32[12,8,128]{2,1,0:T(8,128)S(1)} %get-tuple-element.45.index_ref.refs_4_.refs_1_, f32[12,8,128]{2,1,0:T(8,128)S(1)} %get-tuple-element.46.weight_ref.refs_5_.refs_2_), custom_call_target="tpu_custom_call" | custom-call | tf_op jit(solution)/shard_map/pallas_call | solution.py:448
  44.2 1.9 %collective-permute-done.2.refs_0_ = f32[15,8,128]{2,1,0:T(8,128)S(1)} collective-permute-done((f32[15,8,128]{2,1,0:T(8,128)S(1)}, f32[15,8,128]{2,1,0:T(8,128)S(1)}, u32[]{:S(2)}, u32[]{:S(2)}) %collective-permute-start.2) | collective-permute-done | bytes 61472 | tf_op jit(solution)/shard_map/ppermute | solution.py:461
  46.1 2.0 %shard_map.120 = (f32[5,2048]{1,0:T(8,128)}, f32[5,2,2048]{2,1,0:T(2,128)}) custom-call(f32[15,8,128]{2,1,0:T(8,128)S(1)} %collective-permute-done.2.refs_0_, s32[12,8,128]{2,1,0:T(8,128)S(1)} %get-tuple-element.45.index_ref.refs_4_.refs_1_, f32[12,8,128]{2,1,0:T(8,128)S(1)} %get-tuple-element.46.weight_ref.refs_5_.refs_2_, ...), custom_call_target="tpu_custom_call" | custom-call | tf_op jit(solution)/shard_map/pallas_call | solution.py:448
Async XLA Ops:
  2.3 19.9 %collective-permute-start.1 = (f32[15,8,128]{2,1,0:T(8,128)S(1)}, f32[15,8,128]{2,1,0:T(8,128)S(1)}, u32[]{:S(2)}, u32[]{:S(2)}) collective-permute-start(f32[15,8,128]{2,1,0:T(8,128)S(1)} %get-tuple-element.36), channel_id=1, source_target_pairs={{0,508},{4,8},{8,4},{12,16},{16,12},{20,24},{24,20},{28,32},{32,28... | collective-permute-start | bytes 184328 | tf_op jit(solution)/shard_map/ppermute | solution.py:461
  17.6 5.7 %collective-permute-start = (f32[15,8,128]{2,1,0:T(8,128)S(1)}, f32[15,8,128]{2,1,0:T(8,128)S(1)}, u32[]{:S(2)}, u32[]{:S(2)}) collective-permute-start(f32[15,8,128]{2,1,0:T(8,128)S(1)} %get-tuple-element.35), channel_id=1, source_target_pairs={{0,4},{4,0},{8,12},{12,8},{16,20},{20,16},{24,28},{28,24},{32,36},... | collective-permute-start | bytes 184328 | tf_op jit(solution)/shard_map/ppermute | solution.py:462
  33.6 9.3 %collective-permute-start.3 = (f32[15,8,128]{2,1,0:T(8,128)S(1)}, f32[15,8,128]{2,1,0:T(8,128)S(1)}, u32[]{:S(2)}, u32[]{:S(2)}) collective-permute-start(f32[15,8,128]{2,1,0:T(8,128)S(1)} %get-tuple-element.65), channel_id=1, source_target_pairs={{0,4},{4,0},{8,12},{12,8},{16,20},{20,16},{24,28},{28,24},{32,36},... | collective-permute-start | bytes 184328 | tf_op jit(solution)/shard_map/ppermute | solution.py:462
  36.9 9.2 %collective-permute-start.2 = (f32[15,8,128]{2,1,0:T(8,128)S(1)}, f32[15,8,128]{2,1,0:T(8,128)S(1)}, u32[]{:S(2)}, u32[]{:S(2)}) collective-permute-start(f32[15,8,128]{2,1,0:T(8,128)S(1)} %get-tuple-element.56), channel_id=1, source_target_pairs={{0,508},{4,8},{8,4},{12,16},{16,12},{20,24},{24,20},{28,32},{32,28... | collective-permute-start | bytes 184328 | tf_op jit(solution)/shard_map/ppermute | solution.py:461

commit v11 on v9

--- a/solution.py
+++ b/solution.py
@@ -50,9 +50,18 @@
 
 
 def store_tiles(row, tile_index, pay_a, pay_b, rows):
-    for pay, index in zip((pay_a, pay_b), tile_index):
-        for r, value in enumerate(picked(row, range(ROWS), rows, index)):
-            pay[r] = value
+    def send(i, _):
+        values = picked(row, range(ROWS), rows, tile_index[i])
+        for k, pay in enumerate((pay_a, pay_b)):
+
+            @pl.when(i == k)
+            def _():
+                for r, value in enumerate(values):
+                    pay[r] = value
+
+        return 0
+
+    lax.fori_loop(0, 2, send, 0)
 
 
 def native_row(mean_ref, harm_ref):
@@ -94,7 +103,7 @@
     tile_idx[0] = first
     tile_idx[1] = second
     row = native_row(mean_ref, harm_ref)
-    store_tiles(row, (first, second), pay_a, pay_b, mean_ref.shape[1] // LANES)
+    store_tiles(row, tile_idx, pay_a, pay_b, mean_ref.shape[1] // LANES)
     for wait in waits[3:]:
         wait()
 
@@ -351,7 +360,7 @@
                 total = total + parts_ref[k, r]
             ref[v] = total
     row = fields_row(mean_ref, state_ref)
-    store_tiles(row, (tile_idx[0], tile_idx[1]), pay_a, pay_b, mean_ref.shape[1])
+    store_tiles(row, tile_idx, pay_a, pay_b, mean_ref.shape[1])
 
 
 def own_kernel(

time: 48.1 us -> 48.3 us (level)
  no operation moved by 1% of the time
where the time goes in v11:
time: 48.3 us; the launch traced here: 48 us
  starting transfers between devices  23.2 us (48%)
  Pallas kernels  11.9 us (25%)
  blocking collectives  9.4 us (19%)
  waiting for transfers between devices  2.12 us (4%)
  between operations  1.39 us (3%)
    ppermute x2, starting transfers between devices, exchange(): rim_a = lax.ppermute(pay_a, 'cells', far)  19.1 us
    pallas_call x7, Pallas kernels, launch(): pl.pallas_call(body, out_shape=out_shape, in_specs=[smem] * len(scalars)...  11.9 us
    all_gather x1, blocking collectives, shards(): parts = lax.all_gather(part, HARM)  9.4 us
    ppermute x2, starting transfers between devices, exchange(): rim_b = lax.ppermute(pay_b, 'cells', near)  4.08 us
    ppermute x2, waiting for transfers between devices, exchange(): rim_a = lax.ppermute(pay_a, 'cells', far)  1.77 us
  transfers between devices with their start and end apart: 4, of which 2 were waited for; matrix products, arithmetic and copies ran while one was open for 0% of the time, Pallas kernels for 12%

profile of v11, /device:TPU:1, one launch (start us, length us, event | category | flops | bytes accessed | tf_op | source)
XLA Modules:
  0.0 48.0 jit_solution(16313928527641085298)
XLA Ops:
  0.6 1.7 %shard_map.113 = (f32[15,8,128]{2,1,0:T(8,128)S(1)}, f32[15,8,128]{2,1,0:T(8,128)S(1)}, s32[2,8,128]{2,1,0:T(8,128)S(1)}, f32[5,2048]{1,0:T(8,128)S(1)}, f32[5,2...) custom-call(s32[1]{0:T(128)} %bitcast.place_ref.refs_0_, ...), custom_call_target="tpu_custom_call" | custom-call | tf_op jit(solution)/shard_map/pallas_call | solution.py:440
  2.4 15.3 %collective-permute-start = (f32[15,8,128]{2,1,0:T(8,128)S(1)}, f32[15,8,128]{2,1,0:T(8,128)S(1)}, u32[]{:S(2)}, u32[]{:S(2)}) collective-permute-start(f32[15,8,128]{2,1,0:T(8,128)S(1)} %get-tuple-element.33), channel_id=1, source_target_pairs={{0,508},{4,8},{8,4},{12,16},{16,12},{20,24},{24,20},{28,32},{32,28... | collective-permute-start | bytes 184328 | tf_op jit(solution)/shard_map/ppermute | solution.py:453
  17.7 1.9 %collective-permute-start.1 = (f32[15,8,128]{2,1,0:T(8,128)S(1)}, f32[15,8,128]{2,1,0:T(8,128)S(1)}, u32[]{:S(2)}, u32[]{:S(2)}) collective-permute-start(f32[15,8,128]{2,1,0:T(8,128)S(1)} %get-tuple-element.34), channel_id=1, source_target_pairs={{0,4},{4,0},{8,12},{12,8},{16,20},{20,16},{24,28},{28,24},{32,36},... | collective-permute-start | bytes 184328 | tf_op jit(solution)/shard_map/ppermute | solution.py:454
  20.3 2.0 %shard_map.114 = (f32[5,16,128]{2,1,0:T(8,128)S(1)}, f32[10,16,128]{2,1,0:T(8,128)S(1)}, s32[12,8,128]{2,1,0:T(8,128)S(1)}, f32[12,8,128]{2,1,0:T(8,128)S(1)}, f...) custom-call(s32[1]{0:T(128)} %bitcast.place_ref.refs_0_, ...), custom_call_target="tpu_custom_call" | custom-call | tf_op jit(solution)/shard_map/pallas_call | solution.py:440
  22.3 0.0 collective-permute-done.refs_1_
  22.3 0.4 collective-permute-done.1.refs_2_
  22.7 1.8 %shard_map.115 = (f32[10,16,128]{2,1,0:T(8,128)S(1)}, f32[10,16,128]{2,1,0:T(8,128)S(1)}) custom-call(s32[1]{0:T(128)} %bitcast.place_ref.refs_0_, f32[15,8,128]{2,1,0:T(8,128)S(1)} %collective-permute-done.refs_1_, f32[15,8,128]{2,1,0:T(8,128)S(1)} %collective-permute-done.1.refs_2_, s32[12,8,128]{2,1,0:T(8,128)S(1)} %get-tuple-element.43.refs_3_.refs_1_.index_ref, ...), custom_call_target="tpu_custom_call" | custom-call | tf_op jit(solution)/shard_map/pallas_call | solution.py:440
  24.5 9.4 %all-gather = f32[40,16,128]{2,1,0:T(8,128)S(1)} all-gather(f32[10,16,128]{2,1,0:T(8,128)S(1)} %get-tuple-element.49), channel_id=2, replica_groups=mesh['cells'=128,'harm_0'=2,'harm_1'=2] {'harm_0','harm_1'}, dimensions={0}, use_global_device_ids=true | all-gather | bytes 409600 | tf_op jit(solution)/shard_map/all_gather | solution.py:515
  33.9 0.7 %shard_map.116 = (f32[5,16,128]{2,1,0:T(8,128)S(1)}, f32[5,16,128]{2,1,0:T(8,128)S(1)}, f32[15,8,128]{2,1,0:T(8,128)S(1)}, f32[15,8,128]{2,1,0:T(8,128)S(1)}) custom-call(f32[4,10,16,128]{3,2,1,0:T(8,128)S(1)} %bitcast.12, f32[10,16,128]{2,1,0:T(8,128)S(1)} %get-tuple-element.50.state_ref.refs_5_, s32[2,8,128]{2,1,0:T(8,128)S(1)} %get-tuple-element.51.tile_idx), custom_call_target="tpu_custom_call" | custom-call | tf_op jit(solution)/shard_map/pallas_call | solution.py:440
  34.6 2.2 %collective-permute-start.3 = (f32[15,8,128]{2,1,0:T(8,128)S(1)}, f32[15,8,128]{2,1,0:T(8,128)S(1)}, u32[]{:S(2)}, u32[]{:S(2)}) collective-permute-start(f32[15,8,128]{2,1,0:T(8,128)S(1)} %get-tuple-element.61), channel_id=1, source_target_pairs={{0,4},{4,0},{8,12},{12,8},{16,20},{20,16},{24,28},{28,24},{32,36},... | collective-permute-start | bytes 184328 | tf_op jit(solution)/shard_map/ppermute | solution.py:454
  36.8 3.8 %collective-permute-start.2 = (f32[15,8,128]{2,1,0:T(8,128)S(1)}, f32[15,8,128]{2,1,0:T(8,128)S(1)}, u32[]{:S(2)}, u32[]{:S(2)}) collective-permute-start(f32[15,8,128]{2,1,0:T(8,128)S(1)} %get-tuple-element.52), channel_id=1, source_target_pairs={{0,508},{4,8},{8,4},{12,16},{16,12},{20,24},{24,20},{28,32},{32,28... | collective-permute-start | bytes 184328 | tf_op jit(solution)/shard_map/ppermute | solution.py:453
  40.6 2.3 %shard_map.117 = (f32[5,16,128]{2,1,0:T(8,128)S(1)}, f32[10,16,128]{2,1,0:T(8,128)S(1)}) custom-call(s32[1]{0:T(128)S(6)} %copy.12.refs_1_.refs_0_, s32[12,8,128]{2,1,0:T(8,128)S(1)} %get-tuple-element.43.refs_3_.refs_1_.index_ref, f32[12,8,128]{2,1,0:T(8,128)S(1)} %get-tuple-element.44.refs_4_.refs_2_.weight_ref, f32[16,128]{1,0:T(8,128)S(1)} %get-tuple-element.53.refs_3_, ...), custom_call_target="tpu_custom_call" | custom-call | tf_op jit(solution)/shard_map/pallas_call | solution.py:440
  42.9 0.0 collective-permute-done.3.rim
  42.9 1.3 %shard_map.118.refs_7_ = f32[15,16,128]{2,1,0:T(8,128)S(1)} custom-call(f32[15,8,128]{2,1,0:T(8,128)S(1)} %collective-permute-done.3.rim, s32[12,8,128]{2,1,0:T(8,128)S(1)} %get-tuple-element.43.refs_3_.refs_1_.index_ref, f32[12,8,128]{2,1,0:T(8,128)S(1)} %get-tuple-element.44.refs_4_.refs_2_.weight_ref), custom_call_target="tpu_custom_call" | custom-call | tf_op jit(solution)/shard_map/pallas_call | solution.py:440
  44.2 1.8 %collective-permute-done.2.refs_0_ = f32[15,8,128]{2,1,0:T(8,128)S(1)} collective-permute-done((f32[15,8,128]{2,1,0:T(8,128)S(1)}, f32[15,8,128]{2,1,0:T(8,128)S(1)}, u32[]{:S(2)}, u32[]{:S(2)}) %collective-permute-start.2) | collective-permute-done | bytes 61472 | tf_op jit(solution)/shard_map/ppermute | solution.py:453
  46.0 2.0 %shard_map.119 = (f32[5,2048]{1,0:T(8,128)}, f32[5,2,2048]{2,1,0:T(2,128)}) custom-call(f32[15,8,128]{2,1,0:T(8,128)S(1)} %collective-permute-done.2.refs_0_, s32[12,8,128]{2,1,0:T(8,128)S(1)} %get-tuple-element.43.refs_3_.refs_1_.index_ref, f32[12,8,128]{2,1,0:T(8,128)S(1)} %get-tuple-element.44.refs_4_.refs_2_.weight_ref, ...), custom_call_target="tpu_custom_call" | custom-call | tf_op jit(solution)/shard_map/pallas_call | solution.py:440
Async XLA Ops:
  2.4 19.9 %collective-permute-start = (f32[15,8,128]{2,1,0:T(8,128)S(1)}, f32[15,8,128]{2,1,0:T(8,128)S(1)}, u32[]{:S(2)}, u32[]{:S(2)}) collective-permute-start(f32[15,8,128]{2,1,0:T(8,128)S(1)} %get-tuple-element.33), channel_id=1, source_target_pairs={{0,508},{4,8},{8,4},{12,16},{16,12},{20,24},{24,20},{28,32},{32,28... | collective-permute-start | bytes 184328 | tf_op jit(solution)/shard_map/ppermute | solution.py:453
  17.7 5.0 %collective-permute-start.1 = (f32[15,8,128]{2,1,0:T(8,128)S(1)}, f32[15,8,128]{2,1,0:T(8,128)S(1)}, u32[]{:S(2)}, u32[]{:S(2)}) collective-permute-start(f32[15,8,128]{2,1,0:T(8,128)S(1)} %get-tuple-element.34), channel_id=1, source_target_pairs={{0,4},{4,0},{8,12},{12,8},{16,20},{20,16},{24,28},{28,24},{32,36},... | collective-permute-start | bytes 184328 | tf_op jit(solution)/shard_map/ppermute | solution.py:454
  34.6 8.3 %collective-permute-start.3 = (f32[15,8,128]{2,1,0:T(8,128)S(1)}, f32[15,8,128]{2,1,0:T(8,128)S(1)}, u32[]{:S(2)}, u32[]{:S(2)}) collective-permute-start(f32[15,8,128]{2,1,0:T(8,128)S(1)} %get-tuple-element.61), channel_id=1, source_target_pairs={{0,4},{4,0},{8,12},{12,8},{16,20},{20,16},{24,28},{28,24},{32,36},... | collective-permute-start | bytes 184328 | tf_op jit(solution)/shard_map/ppermute | solution.py:454
  36.8 9.2 %collective-permute-start.2 = (f32[15,8,128]{2,1,0:T(8,128)S(1)}, f32[15,8,128]{2,1,0:T(8,128)S(1)}, u32[]{:S(2)}, u32[]{:S(2)}) collective-permute-start(f32[15,8,128]{2,1,0:T(8,128)S(1)} %get-tuple-element.52), channel_id=1, source_target_pairs={{0,508},{4,8},{8,4},{12,16},{16,12},{20,24},{24,20},{28,32},{32,28... | collective-permute-start | bytes 184328 | tf_op jit(solution)/shard_map/ppermute | solution.py:453
